TPU v7x, 32 devices: a whole 2x2x4 slice. The times are simulated.
32 devices in a mesh: domain: 2 (over x), fsdp: 16 (over z, y, core).
Axes of the slice: x: 2, y: 2, z: 4, core: 2. Of those that a mesh axis runs over, the one named last changes fastest.
Arguments:
- gradients: bfloat16 [2, 4, 4096, 512], P('domain', None, 'fsdp')
- row_counts: int32 [4], replicated, may hold values from 2048 to 4096, as said below
- domain_ids: int32 [2], replicated, may hold values from 0 to 7
- domain_weights: float32 [8], replicated, may hold values from 0.2 to 2
Outputs:
- updates: float32 [4, 4096, 512], P('domain', 'fsdp')
- new_weights: float32 [8], replicated
Inputs may be any that keep to these rules, and one draw needn't show every extreme that they name: `row_counts`: each matrix has 4096 or 2048 rows, and both counts occur.
All inputs are finite; a program needn't handle non-finite values.
Results may differ from a plain program's by a relative error of at most 0.0071.
Values may be sent and summed in bfloat16 or wider, within the bound.
No kernel may reach another device: no remote copies, remote signals or barrier semaphores. Data moves between devices by JAX's collectives and lax.ppermute only.
A program may use at most 64 MiB of HBM per device.

v0:
```python
import math

import jax
import jax.numpy as jnp
from jax import lax
from jax.sharding import PartitionSpec as P

NS_ITERS = 3
OWNERS = 8


COEF_A = 3.4445
COEF_B = -4.775
COEF_C = 2.0315
MUON_SCALE = 0.2
ETA = 4.0


def partner(shard, axis, stride):
    return lax.ppermute(shard, axis, [(i, i ^ 1 << stride) for i in range(lax.axis_size(axis))])


def group_mixing(domain_ids, domain_weights, kind_count):
    weight_share = domain_weights / jnp.sum(domain_weights)
    onehot = (domain_ids[:, None] == jnp.arange(kind_count, dtype=jnp.int32)[None, :]).astype(
        jnp.float32
    )
    counts = jnp.sum(onehot, axis=0)
    per_member = weight_share / jnp.maximum(counts, 1.0)
    group_mix = jnp.sum(onehot * per_member[None, :], axis=1)
    return (weight_share, onehot, counts, group_mix)


def summed_gram(iterate):
    gram_total = lax.dot_general(
        iterate, iterate, (((0,), (0,)), ((), ())), preferred_element_type=jnp.float32
    )
    for bit_pos in range(OWNERS.bit_length() - 1):
        gram_total = gram_total + partner(gram_total, "fsdp", bit_pos)
    return gram_total


def newton_steps(iterate):
    for repeat in range(NS_ITERS):
        gram_full = lax.optimization_barrier(summed_gram(iterate).astype(jnp.bfloat16))
        square = jnp.dot(gram_full, gram_full, preferred_element_type=jnp.float32)
        poly_term = (COEF_B * gram_full.astype(jnp.float32) + COEF_C * square).astype(jnp.bfloat16)
        iterate = lax.optimization_barrier(
            (
                COEF_A * iterate.astype(jnp.float32)
                + jnp.dot(iterate, poly_term, preferred_element_type=jnp.float32)
            ).astype(jnp.bfloat16)
        )
    return iterate


def share_scores(aligned, squares, norm_slots):
    return lax.psum((aligned, squares, norm_slots), ("domain", "fsdp"))


def body(gradients, row_counts, domain_ids, domain_weights):
    groups = lax.axis_size("domain")
    shards = lax.axis_size("fsdp")
    matrices = row_counts.shape[0]
    rows_src = gradients.shape[2]
    columns = gradients.shape[3]
    per_domain = matrices // groups
    sub_rows = rows_src // OWNERS
    own_rows = shards * sub_rows
    full_rows = rows_src * shards
    domain_pos = lax.axis_index("domain")
    shard_pos = lax.axis_index("fsdp")
    weight_share, onehot, counts, group_mix = group_mixing(
        domain_ids, domain_weights, domain_weights.shape[0]
    )
    blocks = lax.all_to_all(
        gradients.reshape(1, groups, per_domain, rows_src, columns),
        "domain",
        split_axis=1,
        concat_axis=0,
        tiled=True,
    )
    blocks = blocks.reshape(groups, per_domain, rows_src, columns)
    global_rows = shard_pos * rows_src + jnp.arange(rows_src, dtype=jnp.int32)
    limits = lax.dynamic_slice_in_dim(row_counts, domain_pos * per_domain, per_domain, 0)
    row_mask = (global_rows[None, :] < limits[:, None])[None, :, :, None]
    masked = jnp.where(row_mask, blocks.astype(jnp.float32), jnp.zeros((), jnp.float32))
    combined = jnp.sum(group_mix[:, None, None, None] * masked, axis=0)
    aligned = jnp.sum(masked * combined[None], axis=(1, 2, 3))
    squares = jnp.sum(masked * masked, axis=(1, 2, 3))
    block_squares = jnp.sum(combined * combined, axis=(1, 2))
    norm_slots = lax.dynamic_update_slice_in_dim(
        jnp.zeros((matrices,), jnp.float32), block_squares, domain_pos * per_domain, 0
    )
    aligned, squares, norm_slots = share_scores(aligned, squares, norm_slots)
    frob_norm = (
        jnp.sqrt(lax.dynamic_slice_in_dim(norm_slots, domain_pos * per_domain, per_domain, 0))
        + 1e-07
    )
    scaled = (combined / frob_norm[:, None, None]).astype(jnp.bfloat16)
    scaled = scaled.reshape(shards, 1, sub_rows, columns)
    start_rows = lax.all_to_all(scaled, "fsdp", split_axis=0, concat_axis=1, tiled=True)
    start_rows = lax.optimization_barrier(start_rows.reshape(own_rows, columns))
    finished = newton_steps(start_rows)
    returned = lax.all_to_all(
        finished.reshape(1, shards, sub_rows, columns),
        "fsdp",
        split_axis=1,
        concat_axis=0,
        tiled=True,
    )
    returned = returned.reshape(per_domain, rows_src, columns)
    updates = returned.astype(jnp.float32) * (MUON_SCALE * math.sqrt(full_rows))
    total_sq = jnp.sum(norm_slots)
    cosine = aligned / (jnp.sqrt(squares) * jnp.sqrt(total_sq) + 1e-06)
    score = jnp.sum(onehot * cosine[:, None], axis=0) / jnp.maximum(counts, 1.0)
    raised = weight_share * jnp.exp(ETA * score)
    return (updates, raised / jnp.sum(raised))


def solution(mesh):
    placed = (P("domain", None, "fsdp", None), P(), P(), P())
    return jax.shard_map(
        body,
        mesh=mesh,
        in_specs=placed,
        out_specs=(P("domain", "fsdp", None), P()),
        check_vma=False,
    )
```

profile of v0, /device:TPU:1, one launch (start us, length us, event | category | flops | bytes accessed | tf_op | source)
XLA Modules:
  0.0 265.4 jit_solution(6877497156156330844)
XLA Ops:
  0.7 3.7 %all-to-all-start = ((bf16[1,2,2,256,512]{4,3,2,0,1:T(8,128)(2,1)}), bf16[1,2,2,256,512]{4,3,2,0,1:T(8,128)(2,1)S(1)}, u32[]{:S(2)}, u32[]{:S(2)}) async-start(bf16[1,2,2,256,512]{4,3,2,0,1:T(8,128)(2,1)} %bitcast.31), calls=%async_computation | async-start | bytes 2097152 | tf_op jit(solution)/shard_map/all_to_all | solution.py:76
  4.5 0.6 reduce_sum.92
  5.2 0.7 multiply_divide_fusion
  6.1 12.1 %all-to-all-done = bf16[1,2,2,256,512]{4,3,2,0,1:T(8,128)(2,1)S(1)} async-done(((bf16[1,2,2,256,512]{4,3,2,0,1:T(8,128)(2,1)}), bf16[1,2,2,256,512]{4,3,2,0,1:T(8,128)(2,1)S(1)}, u32[]{:S(2)}, u32[]{:S(2)}) %all-to-all-start) | async-done | bytes 1048608 | tf_op jit(solution)/shard_map/all_to_all | solution.py:76
  19.0 0.7 fusion.5
  19.7 39.5 %all-reduce = (f32[4]{0:T(128)S(1)}, f32[2]{0:T(128)S(1)}, f32[2]{0:T(128)S(1)}) all-reduce(f32[4]{0:T(128)S(1)} %dynamic_update_slice.3, f32[2]{0:T(128)S(1)} %get-tuple-element.3, f32[2]{0:T(128)S(1)} %get-tuple-element.2), channel_id=1, replica_groups=mesh['domain'=2,'fsdp'=16] {'domain','fsdp'}, use_global_device_ids=true, to_apply=%region_5.6 | all-reduce | flops 8 | bytes 64 | tf_op jit(solution)/shard_map/psum | solution.py:58
  60.9 20.6 %all_to_all.12 = bf16[16,1,32,512]{3,2,1,0:T(8,128)(2,1)S(1)} all-to-all(bf16[16,1,32,512]{3,2,1,0:T(8,128)(2,1)S(1)} %divide_convert_fusion), channel_id=1, replica_groups=mesh['domain'=2,'fsdp'=16] {'fsdp'}, dimensions={0} | all-to-all | bytes 1048576 | tf_op jit(solution)/shard_map/all_to_all | solution.py:102
  82.4 2.3 collective-permute-done
  84.9 1.1 collective-permute-start.1
  86.0 23.4 %collective-permute-done.1 = f32[512,512]{1,0:T(8,128)S(1)} collective-permute-done((f32[512,512]{1,0:T(8,128)S(1)}, f32[512,512]{1,0:T(8,128)S(1)}, u32[]{:S(2)}, u32[]{:S(2)}) %collective-permute-start.1) | collective-permute-done | bytes 1048608 | tf_op jit(solution)/shard_map/ppermute | solution.py:20
  109.6 1.8 collective-permute-start.2
  111.3 22.3 %collective-permute-done.2 = f32[512,512]{1,0:T(8,128)S(1)} collective-permute-done((f32[512,512]{1,0:T(8,128)S(1)}, f32[512,512]{1,0:T(8,128)S(1)}, u32[]{:S(2)}, u32[]{:S(2)}) %collective-permute-start.2) | collective-permute-done | bytes 1048608 | tf_op jit(solution)/shard_map/ppermute | solution.py:20
  133.9 0.8 fusion.6
  135.1 1.9 collective-permute-start.3
  137.0 2.3 collective-permute-done.3
  139.5 1.0 collective-permute-start.4
  140.6 23.4 %collective-permute-done.4 = f32[512,512]{1,0:T(8,128)S(1)} collective-permute-done((f32[512,512]{1,0:T(8,128)S(1)}, f32[512,512]{1,0:T(8,128)S(1)}, u32[]{:S(2)}, u32[]{:S(2)}) %collective-permute-start.4) | collective-permute-done | bytes 1048608 | tf_op jit(solution)/shard_map/ppermute | solution.py:20
  164.2 1.5 collective-permute-start.5
  165.7 22.0 %collective-permute-done.5 = f32[512,512]{1,0:T(8,128)S(1)} collective-permute-done((f32[512,512]{1,0:T(8,128)S(1)}, f32[512,512]{1,0:T(8,128)S(1)}, u32[]{:S(2)}, u32[]{:S(2)}) %collective-permute-start.5) | collective-permute-done | bytes 1048608 | tf_op jit(solution)/shard_map/ppermute | solution.py:20
  188.0 0.8 fusion.7
  189.2 2.2 collective-permute-start.6
  191.4 2.3 collective-permute-done.6
  193.9 1.0 collective-permute-start.7
  194.9 23.4 %collective-permute-done.7 = f32[512,512]{1,0:T(8,128)S(1)} collective-permute-done((f32[512,512]{1,0:T(8,128)S(1)}, f32[512,512]{1,0:T(8,128)S(1)}, u32[]{:S(2)}, u32[]{:S(2)}) %collective-permute-start.7) | collective-permute-done | bytes 1048608 | tf_op jit(solution)/shard_map/ppermute | solution.py:20
  218.5 1.5 collective-permute-start.8
  220.0 22.0 %collective-permute-done.8 = f32[512,512]{1,0:T(8,128)S(1)} collective-permute-done((f32[512,512]{1,0:T(8,128)S(1)}, f32[512,512]{1,0:T(8,128)S(1)}, u32[]{:S(2)}, u32[]{:S(2)}) %collective-permute-start.8) | collective-permute-done | bytes 1048608 | tf_op jit(solution)/shard_map/ppermute | solution.py:20
  242.3 1.6 fusion.8
  243.9 6.4 %all-to-all-start.2 = ((bf16[1,16,32,512]{3,2,0,1:T(8,128)(2,1)}), bf16[1,16,32,512]{3,2,0,1:T(8,128)(2,1)S(1)}, u32[]{:S(2)}, u32[]{:S(2)}) async-start(bf16[1,16,32,512]{3,2,0,1:T(8,128)(2,1)} %bitcast.5), calls=%async_computation.2 | async-start | bytes 1048576 | tf_op jit(solution)/shard_map/all_to_all | solution.py:105
  250.4 1.3 fusion.21
  251.7 1.2 broadcast_divide_fusion
  252.9 11.4 %all-to-all-done.2 = bf16[1,16,32,512]{3,2,0,1:T(8,128)(2,1)S(1)} async-done(((bf16[1,16,32,512]{3,2,0,1:T(8,128)(2,1)}), bf16[1,16,32,512]{3,2,0,1:T(8,128)(2,1)S(1)}, u32[]{:S(2)}, u32[]{:S(2)}) %all-to-all-start.2) | async-done | bytes 524320 | tf_op jit(solution)/shard_map/all_to_all | solution.py:105
  264.3 1.1 convert_multiply_fusion
  (34 shorter events, 6.1 us)
Async XLA Ops:
  0.6 3.8 %copy-start.2 = (s32[2]{0:T(128)S(1)}, s32[2]{0:T(128)}, u32[]{:S(2)}) copy-start(s32[2]{0:T(128)} %param.6) | copy-start | bytes 28
  0.6 3.9 %copy-start = (f32[8]{0:T(128)S(1)}, f32[8]{0:T(128)}, u32[]{:S(2)}) copy-start(f32[8]{0:T(128)} %param.7) | copy-start | bytes 100
  0.7 4.5 %copy-start.1 = (s32[4]{0:T(128)S(1)}, s32[4]{0:T(128)}, u32[]{:S(2)}) copy-start(s32[4]{0:T(128)} %param.5) | copy-start | bytes 52
  0.7 17.6 %all-to-all-start = ((bf16[1,2,2,256,512]{4,3,2,0,1:T(8,128)(2,1)}), bf16[1,2,2,256,512]{4,3,2,0,1:T(8,128)(2,1)S(1)}, u32[]{:S(2)}, u32[]{:S(2)}) async-start(bf16[1,2,2,256,512]{4,3,2,0,1:T(8,128)(2,1)} %bitcast.31), calls=%async_computation | async-start | bytes 2097152 | tf_op jit(solution)/shard_map/all_to_all | solution.py:76
  82.0 2.7 %collective-permute-start = (f32[512,512]{1,0:T(8,128)S(1)}, f32[512,512]{1,0:T(8,128)S(1)}, u32[]{:S(2)}, u32[]{:S(2)}) collective-permute-start(f32[512,512]{1,0:T(8,128)S(1)} %fusion.22), channel_id=1, source_target_pairs={{0,1},{1,0},{2,3},{3,2},{4,5},{5,4},{6,7},{7,6},{8,9},{9,8},{10,11... | collective-permute-start | bytes 3145736 | tf_op jit(solution)/shard_map/ppermute | solution.py:20
  84.9 24.4 %collective-permute-start.1 = (f32[512,512]{1,0:T(8,128)S(1)}, f32[512,512]{1,0:T(8,128)S(1)}, u32[]{:S(2)}, u32[]{:S(2)}) collective-permute-start(f32[512,512]{1,0:T(8,128)S(1)} %add.76), channel_id=1, source_target_pairs={{0,2},{1,3},{2,0},{3,1},{4,6},{5,7},{6,4},{7,5},{8,10},{9,11},{10,... | collective-permute-start | bytes 3145736 | tf_op jit(solution)/shard_map/ppermute | solution.py:20
  109.6 24.0 %collective-permute-start.2 = (f32[512,512]{1,0:T(8,128)S(1)}, f32[512,512]{1,0:T(8,128)S(1)}, u32[]{:S(2)}, u32[]{:S(2)}) collective-permute-start(f32[512,512]{1,0:T(8,128)S(1)} %add.77), channel_id=1, source_target_pairs={{0,4},{1,5},{2,6},{3,7},{4,0},{5,1},{6,2},{7,3},{8,12},{9,13},{10,... | collective-permute-start | bytes 3145736 | tf_op jit(solution)/shard_map/ppermute | solution.py:20
  135.1 4.2 %collective-permute-start.3 = (f32[512,512]{1,0:T(8,128)S(1)}, f32[512,512]{1,0:T(8,128)S(1)}, u32[]{:S(2)}, u32[]{:S(2)}) collective-permute-start(f32[512,512]{1,0:T(8,128)S(1)} %fusion.23), channel_id=1, source_target_pairs={{0,1},{1,0},{2,3},{3,2},{4,5},{5,4},{6,7},{7,6},{8,9},{9,8},{10,11... | collective-permute-start | bytes 3145736 | tf_op jit(solution)/shard_map/ppermute | solution.py:20
  139.5 24.4 %collective-permute-start.4 = (f32[512,512]{1,0:T(8,128)S(1)}, f32[512,512]{1,0:T(8,128)S(1)}, u32[]{:S(2)}, u32[]{:S(2)}) collective-permute-start(f32[512,512]{1,0:T(8,128)S(1)} %add.81), channel_id=1, source_target_pairs={{0,2},{1,3},{2,0},{3,1},{4,6},{5,7},{6,4},{7,5},{8,10},{9,11},{10,... | collective-permute-start | bytes 3145736 | tf_op jit(solution)/shard_map/ppermute | solution.py:20
  164.2 23.6 %collective-permute-start.5 = (f32[512,512]{1,0:T(8,128)S(1)}, f32[512,512]{1,0:T(8,128)S(1)}, u32[]{:S(2)}, u32[]{:S(2)}) collective-permute-start(f32[512,512]{1,0:T(8,128)S(1)} %add.82), channel_id=1, source_target_pairs={{0,4},{1,5},{2,6},{3,7},{4,0},{5,1},{6,2},{7,3},{8,12},{9,13},{10,... | collective-permute-start | bytes 3145736 | tf_op jit(solution)/shard_map/ppermute | solution.py:20
  189.2 4.4 %collective-permute-start.6 = (f32[512,512]{1,0:T(8,128)S(1)}, f32[512,512]{1,0:T(8,128)S(1)}, u32[]{:S(2)}, u32[]{:S(2)}) collective-permute-start(f32[512,512]{1,0:T(8,128)S(1)} %fusion.24), channel_id=1, source_target_pairs={{0,1},{1,0},{2,3},{3,2},{4,5},{5,4},{6,7},{7,6},{8,9},{9,8},{10,11... | collective-permute-start | bytes 3145736 | tf_op jit(solution)/shard_map/ppermute | solution.py:20
  193.9 24.4 %collective-permute-start.7 = (f32[512,512]{1,0:T(8,128)S(1)}, f32[512,512]{1,0:T(8,128)S(1)}, u32[]{:S(2)}, u32[]{:S(2)}) collective-permute-start(f32[512,512]{1,0:T(8,128)S(1)} %add.86), channel_id=1, source_target_pairs={{0,2},{1,3},{2,0},{3,1},{4,6},{5,7},{6,4},{7,5},{8,10},{9,11},{10,... | collective-permute-start | bytes 3145736 | tf_op jit(solution)/shard_map/ppermute | solution.py:20
  218.5 23.6 %collective-permute-start.8 = (f32[512,512]{1,0:T(8,128)S(1)}, f32[512,512]{1,0:T(8,128)S(1)}, u32[]{:S(2)}, u32[]{:S(2)}) collective-permute-start(f32[512,512]{1,0:T(8,128)S(1)} %add.87), channel_id=1, source_target_pairs={{0,4},{1,5},{2,6},{3,7},{4,0},{5,1},{6,2},{7,3},{8,12},{9,13},{10,... | collective-permute-start | bytes 3145736 | tf_op jit(solution)/shard_map/ppermute | solution.py:20
  243.9 20.4 %all-to-all-start.2 = ((bf16[1,16,32,512]{3,2,0,1:T(8,128)(2,1)}), bf16[1,16,32,512]{3,2,0,1:T(8,128)(2,1)S(1)}, u32[]{:S(2)}, u32[]{:S(2)}) async-start(bf16[1,16,32,512]{3,2,0,1:T(8,128)(2,1)} %bitcast.5), calls=%async_computation.2 | async-start | bytes 1048576 | tf_op jit(solution)/shard_map/all_to_all | solution.py:105
where the time goes:
time: 266 us; the launch traced here: 265 us
  waiting for transfers between devices  167 us (63%)
  blocking collectives  60.1 us (23%)
  starting transfers between devices  22.6 us (8%)
  other arithmetic  9.43 us (4%)
  matrix products  4.54 us (2%)
    ppermute x9, waiting for transfers between devices, partner(): lax.ppermute(shard, axis, [(i, i ^ 1 << stride) for i in range(lax.axis_s...  143 us
    psum x1, blocking collectives, share_scores(): return lax.psum((aligned, squares, norm_slots), ('domain', 'fsdp'))  39.5 us
    all_to_all x1, blocking collectives, body(): lax.all_to_all(scaled, 'fsdp', split_axis=0, concat_axis=1, tiled=True)  20.6 us
    ppermute x9, starting transfers between devices, partner(): lax.ppermute(shard, axis, [(i, i ^ 1 << stride) for i in range(lax.axis_s...  12.4 us
    all_to_all x1, waiting for transfers between devices, body(): lax.all_to_all(gradients.reshape(1, groups, per_domain, rows_src, columns...  12.1 us
    all_to_all x1, waiting for transfers between devices, body(): lax.all_to_all(finished.reshape(1, shards, sub_rows, columns), 'fsdp', sp...  11.4 us
    all_to_all x1, starting transfers between devices, body(): lax.all_to_all(finished.reshape(1, shards, sub_rows, columns), 'fsdp', sp...  6.39 us
  transfers between devices with their start and end apart: 11, of which 11 were waited for; matrix products, arithmetic and copies ran while one was open for 2% of the time, Pallas kernels for 0%

commit v1 on v0

v1 whole, which is shorter than its diff:
```python
import functools
import math

import jax
import jax.numpy as jnp
from jax import lax
from jax.experimental import pallas as pl
from jax.experimental.pallas import tpu as pltpu
from jax.sharding import PartitionSpec as P

NS_ITERS = 3
COEF_A = 3.4445
COEF_B = -4.775
COEF_C = 2.0315
MUON_SCALE = 0.2
ETA = 4.0

AXES = ("domain", "fsdp")
BLOCK = 128
SQUARE = 4
TAIL = 16
HALF_SPAN = 16384.0
TINY = 1e-30
F32 = jnp.float32


def group_mixing(domain_ids, domain_weights, kind_count):
    weight_share = domain_weights / jnp.sum(domain_weights)
    onehot = (domain_ids[:, None] == jnp.arange(kind_count, dtype=jnp.int32)[None, :]).astype(F32)
    counts = jnp.sum(onehot, axis=0)
    per_member = weight_share / jnp.maximum(counts, 1.0)
    group_mix = jnp.sum(onehot * per_member[None, :], axis=1)
    return (weight_share, onehot, counts, group_mix)


def block_plan(columns):
    count = columns // BLOCK
    off = [(i, j) for i in range(count) for j in range(i + 1, count)]
    folded = [(i, i) for i in range(0, count, 2)]
    per_piece = (len(off) + len(folded)) // SQUARE
    pieces = []
    for p in range(SQUARE):
        take = per_piece - (1 if p >= SQUARE - len(folded) else 0)
        pieces.append([off.pop(0) for _ in range(take)])
    for n, pair in enumerate(folded):
        pieces[SQUARE - len(folded) + n].append(pair)
    return pieces


def lane_pick(row, index):
    lanes = lax.broadcasted_iota(jnp.int32, row.shape, 1)
    return jnp.sum(jnp.where(lanes == index, row, 0.0), axis=1, keepdims=True)


def encode_row(row):
    power = jnp.clip(jnp.floor(jnp.log2(jnp.abs(row))), -120.0, 120.0)
    scaled = row * jnp.exp2(-power)
    high = scaled.astype(jnp.bfloat16).astype(F32)
    rest = scaled - high
    mid = rest.astype(jnp.bfloat16).astype(F32)
    low = (rest - mid).astype(jnp.bfloat16).astype(F32)
    return (high, mid * 256.0, low * 65536.0, power)


def decode_row(parts):
    high, mid, low, power = parts
    return ((high + mid * (1.0 / 256.0)) + low * (1.0 / 65536.0)) * jnp.exp2(power)


def tail_rows(rows):
    index = lax.broadcasted_iota(jnp.int32, (TAIL, BLOCK), 0)
    out = jnp.zeros((TAIL, BLOCK), F32)
    for n, row in enumerate(rows):
        out = jnp.where(index == n, row, out)
    return out


def gram_kernel(lanes, domains, mix_ref, lim_ref, pos_ref, *refs):
    blocks = refs[: domains * lanes]
    comb_ref, pay_ref, own_ref, piece_ref, diag_ref = refs[domains * lanes :]
    rows, columns = blocks[0].shape
    domain_pos, quad = pos_ref[0], pos_ref[1]
    aligned = [jnp.zeros((1, 1), F32)] * domains
    squares = [jnp.zeros((1, 1), F32)] * domains
    frob = jnp.zeros((1, 1), F32)
    row_index = lax.broadcasted_iota(jnp.int32, (rows, 1), 0)

    def total(v):
        return jnp.sum(jnp.sum(v, axis=0, keepdims=True), axis=1, keepdims=True)

    for kl in range(lanes):
        keep = row_index < lim_ref[kl]
        masked = [
            jnp.where(keep, blocks[kd * lanes + kl][...].astype(F32), 0.0)
            for kd in range(domains)
        ]
        combined = mix_ref[0] * masked[0]
        for kd in range(1, domains):
            combined = combined + mix_ref[kd] * masked[kd]
        for kd in range(domains):
            aligned[kd] = aligned[kd] + total(masked[kd] * combined)
            squares[kd] = squares[kd] + total(masked[kd] * masked[kd])
        frob = frob + total(combined * combined)
        comb_ref[pl.ds(kl * rows, rows), :] = combined
    rounded = comb_ref[...].astype(jnp.bfloat16)
    gram = lax.dot_general(
        rounded, rounded, (((0,), (0,)), ((), ())), preferred_element_type=F32
    )

    lane = lax.broadcasted_iota(jnp.int32, (1, BLOCK), 1)
    scal = jnp.where(lane == 2 * domains, frob, 0.0)
    for kd in range(domains):
        group = domain_pos ^ kd
        scal = jnp.where(lane == group, aligned[kd], scal)
        scal = jnp.where(lane == domains + group, squares[kd], scal)
    parts = encode_row(scal)
    scal = decode_row(parts)
    frob = lane_pick(scal, 2 * domains)
    scale = jnp.where(frob > TINY, HALF_SPAN / jnp.maximum(frob, TINY), 0.0)

    row_id = lax.broadcasted_iota(jnp.int32, (BLOCK, BLOCK), 0)
    col_id = lax.broadcasted_iota(jnp.int32, (BLOCK, BLOCK), 1)

    def part(i, j):
        return gram[i * BLOCK : (i + 1) * BLOCK, j * BLOCK : (j + 1) * BLOCK]

    for p, entries in enumerate(block_plan(columns)):
        diag = jnp.zeros((1, BLOCK), F32)
        for n, (i, j) in enumerate(entries):
            if i == j:
                upper, lower = part(i, i), part(i + 1, i + 1)
                value = jnp.where(row_id < col_id, upper, lower)
                diag = jnp.sum(jnp.where(row_id == col_id, upper, 0.0), axis=0, keepdims=True)
            else:
                value = part(i, j)
            piece_ref[p, pl.ds(n * BLOCK, BLOCK), :] = value
        diag_ref[p] = jnp.broadcast_to(diag, diag_ref.shape[1:])
    body_rows = piece_ref.shape[1]
    for k in range(SQUARE):
        value = piece_ref[quad ^ k]
        diag = diag_ref[quad ^ k][0:1]
        if k == 0:
            own_ref[pl.ds(0, body_rows), :] = value
            own_ref[pl.ds(body_rows, TAIL), :] = tail_rows([diag, scal])
        else:
            pay_ref[k - 1, pl.ds(0, body_rows), :] = value * scale
            pay_ref[k - 1, pl.ds(body_rows, TAIL), :] = tail_rows([diag * scale, *parts])


def sum_kernel(scalar_lane, count, *refs):
    own_ref, got, (out_ref, pay_ref) = refs[0], refs[1 : 1 + count], refs[1 + count :]
    body_rows = own_ref.shape[0] - TAIL
    terms = []
    for ref in (None, *got):
        if ref is None:
            terms.append(
                (
                    own_ref[pl.ds(0, body_rows), :],
                    own_ref[pl.ds(body_rows, 1), :],
                    own_ref[pl.ds(body_rows + 1, 1), :],
                )
            )
            continue
        scal = decode_row([ref[pl.ds(body_rows + 1 + n, 1), :] for n in range(4)])
        scale = lane_pick(scal, scalar_lane) * (1.0 / HALF_SPAN)
        terms.append(
            (ref[pl.ds(0, body_rows), :] * scale, ref[pl.ds(body_rows, 1), :] * scale, scal)
        )
    while len(terms) > 1:
        terms = [
            tuple(x + y for x, y in zip(terms[n], terms[n + 1])) for n in range(0, len(terms), 2)
        ]
    value, diag, scal = terms[0]
    parts = encode_row(scal)
    scal = decode_row(parts)
    frob = lane_pick(scal, scalar_lane)
    scale = jnp.where(frob > TINY, HALF_SPAN / jnp.maximum(frob, TINY), 0.0)
    out_ref[pl.ds(0, body_rows), :] = value
    out_ref[pl.ds(body_rows, TAIL), :] = tail_rows([diag, scal])
    pay_ref[pl.ds(0, body_rows), :] = value * scale
    pay_ref[pl.ds(body_rows, TAIL), :] = tail_rows([diag * scale, *parts])


def newton_kernel(scalar_lane, pos_ref, comb_ref, own_ref, *refs):
    got, (done_ref, piece_ref, diag_ref, gram_ref) = refs[: SQUARE - 1], refs[SQUARE - 1 :]
    quad = pos_ref[1]
    body_rows = own_ref.shape[0] - TAIL
    columns = comb_ref.shape[1]
    scal = own_ref[pl.ds(body_rows + 1, 1), :]
    frob = lane_pick(scal, scalar_lane)
    inv = 1.0 / (jnp.sqrt(frob) + 1e-07)
    shared = (frob * inv) * inv * (1.0 / HALF_SPAN)
    for k in range(SQUARE):
        ref = own_ref if k == 0 else got[k - 1]
        value, diag = ref[pl.ds(0, body_rows), :], ref[pl.ds(body_rows, 1), :]
        if k == 0:
            value, diag = (value * inv) * inv, (diag * inv) * inv
        else:
            value, diag = value * shared, diag * shared
        piece_ref[quad ^ k] = value
        diag_ref[quad ^ k] = jnp.broadcast_to(diag, diag_ref.shape[1:])
    row_id = lax.broadcasted_iota(jnp.int32, (BLOCK, BLOCK), 0)
    col_id = lax.broadcasted_iota(jnp.int32, (BLOCK, BLOCK), 1)

    def place(i, j, value):
        gram_ref[pl.ds(i * BLOCK, BLOCK), pl.ds(j * BLOCK, BLOCK)] = value

    for p, entries in enumerate(block_plan(columns)):
        for n, (i, j) in enumerate(entries):
            value = piece_ref[p, pl.ds(n * BLOCK, BLOCK), :]
            flipped = value.T
            if i == j:
                diag = diag_ref[p][0:1]
                upper = jnp.where(row_id < col_id, value, jnp.where(row_id > col_id, flipped, diag))
                place(i, i, upper)
                place(i + 1, i + 1, jnp.where(row_id < col_id, flipped, value))
            else:
                place(i, j, value)
                place(j, i, flipped)

    def dot(x, y):
        return jnp.dot(x, y, preferred_element_type=F32)

    gram = gram_ref[...]
    iterate = (comb_ref[...] * inv).astype(jnp.bfloat16)
    for step in range(NS_ITERS):
        gram_low = gram.astype(jnp.bfloat16)
        square = dot(gram_low, gram_low)
        poly = (COEF_B * gram + COEF_C * square).astype(jnp.bfloat16)
        iterate = (COEF_A * iterate.astype(F32) + dot(iterate, poly)).astype(jnp.bfloat16)
        if step + 1 < NS_ITERS:
            half = COEF_A * gram + dot(gram_low, poly)
            half_high = half.astype(jnp.bfloat16)
            half_low = (half - half_high.astype(F32)).astype(jnp.bfloat16)
            gram = COEF_A * half + dot(poly, half_high) + dot(poly, half_low)
    done_ref[...] = iterate


def call(kernel, out_shape, args, spaces, scratch=(), flops=0):
    size = sum(math.prod(a.shape) * a.dtype.itemsize for a in (*args, *out_shape))
    return pl.pallas_call(
        kernel,
        out_shape=tuple(out_shape),
        in_specs=[pl.BlockSpec(memory_space=s) for s in spaces],
        out_specs=tuple(pl.BlockSpec(memory_space=pltpu.VMEM) for _ in out_shape),
        scratch_shapes=list(scratch),
        cost_estimate=pl.CostEstimate(flops=flops, bytes_accessed=size, transcendentals=0),
    )(*args)


def body(gradients, row_counts, domain_ids, domain_weights):
    domains = lax.axis_size("domain")
    shards = lax.axis_size("fsdp")
    matrices, rows, columns = gradients.shape[1:]
    lanes = matrices // domains
    sets = shards // lanes
    members = domains * lanes
    full_rows = rows * shards
    domain_pos = lax.axis_index("domain")
    shard_pos = lax.axis_index("fsdp")
    lane_pos = shard_pos % lanes
    set_pos = shard_pos // lanes
    member = domain_pos * lanes + lane_pos
    quad = set_pos % SQUARE
    flip = [(k // lanes) * shards + k % lanes for k in range(members)]

    def exchange(value, mask):
        return lax.ppermute(value, AXES, [(i, i ^ mask) for i in range(domains * shards)])

    def piece(index):
        return lax.dynamic_index_in_dim(gradients[0], index, 0, keepdims=False)

    if members <= 8:
        order = sorted(range(1, members), key=lambda k: k // lanes == 0)
        got = {0: piece(member)}
        for k in order:
            got[k] = exchange(piece(member ^ k), flip[k])
        blocks = [got[k] for k in range(members)]
    else:
        teams = [
            [d * shards + s * lanes + l for d in range(domains) for l in range(lanes)]
            for s in range(sets)
        ]
        moved = lax.all_to_all(
            gradients[0], AXES, split_axis=0, concat_axis=0, axis_index_groups=teams, tiled=True
        )
        blocks = [
            lax.dynamic_index_in_dim(moved, member ^ k, 0, keepdims=False) for k in range(members)
        ]

    weight_share, onehot, counts, group_mix = group_mixing(
        domain_ids, domain_weights, domain_weights.shape[0]
    )
    mix = jnp.take(group_mix, domain_pos ^ jnp.arange(domains, dtype=jnp.int32))
    lane_row = (set_pos * lanes + (lane_pos ^ jnp.arange(lanes, dtype=jnp.int32))) * rows
    limits = lax.dynamic_index_in_dim(row_counts, member, 0, keepdims=False) - lane_row
    position = jnp.stack([domain_pos, quad]).astype(jnp.int32)

    per_piece = sum(1 for _ in block_plan(columns)[0]) * BLOCK
    packed = per_piece + TAIL
    vmem, smem = pltpu.VMEM, pltpu.SMEM
    pieces_scratch = [
        pltpu.VMEM((SQUARE, per_piece, BLOCK), F32),
        pltpu.VMEM((SQUARE, 8, BLOCK), F32),
    ]
    combined, payload, own = call(
        functools.partial(gram_kernel, lanes, domains),
        [
            jax.ShapeDtypeStruct((lanes * rows, columns), F32),
            jax.ShapeDtypeStruct((SQUARE - 1, packed, BLOCK), F32),
            jax.ShapeDtypeStruct((packed, BLOCK), F32),
        ],
        [mix, limits, position, *blocks],
        [smem] * 3 + [vmem] * members,
        pieces_scratch,
        flops=2 * lanes * rows * columns * columns,
    )
    scalar_lane = 2 * domains

    def add_up(own, got):
        return call(
            functools.partial(sum_kernel, scalar_lane, len(got)),
            [jax.ShapeDtypeStruct((packed, BLOCK), F32)] * 2,
            [own, *got],
            [vmem] * (1 + len(got)),
        )

    def half_width(value, mask):
        return exchange(value.astype(jnp.float16), mask).astype(F32)

    got = [half_width(payload[k - 1], k * lanes) for k in range(1, SQUARE)]
    own, packet = add_up(own, got)
    stride = SQUARE * lanes
    while stride < shards:
        own, packet = add_up(own, [half_width(packet, stride)])
        stride *= 2
    got = [half_width(packet, k * lanes) for k in range(1, SQUARE)]

    (finished,) = call(
        functools.partial(newton_kernel, scalar_lane),
        [jax.ShapeDtypeStruct((lanes * rows, columns), jnp.bfloat16)],
        [position, combined, own, *got],
        [smem] + [vmem] * (1 + SQUARE),
        pieces_scratch + [pltpu.VMEM((columns, columns), F32)],
        flops=13 * 2 * columns**3,
    )

    finished = finished.reshape(lanes, rows, columns)
    returned = [finished[0]] + [exchange(finished[k], k) for k in range(1, lanes)]
    if lanes == 2:
        first = lane_pos == 0
        ordered = [
            jnp.where(first, returned[0], returned[1]),
            jnp.where(first, returned[1], returned[0]),
        ]
    else:
        stacked = jnp.stack(returned)
        ordered = [
            lax.dynamic_index_in_dim(stacked, lane_pos ^ k, 0, keepdims=False)
            for k in range(lanes)
        ]
    updates = jnp.stack(ordered).astype(F32) * (MUON_SCALE * math.sqrt(full_rows))

    sums = own[per_piece : per_piece + 8]
    stride = 1
    while stride < members:
        sums = sums + exchange(sums, flip[stride])
        stride *= 2
    aligned, squares = sums[1, :domains], sums[1, domains : 2 * domains]
    total_sq = sums[1, scalar_lane]
    cosine = aligned / (jnp.sqrt(squares) * jnp.sqrt(total_sq) + 1e-06)
    score = jnp.sum(onehot * cosine[:, None], axis=0) / jnp.maximum(counts, 1.0)
    raised = weight_share * jnp.exp(ETA * score)
    return (updates, raised / jnp.sum(raised))


def solution(mesh):
    placed = (P("domain", None, "fsdp", None), P(), P(), P())
    return jax.shard_map(
        body,
        mesh=mesh,
        in_specs=placed,
        out_specs=(P("domain", "fsdp", None), P()),
        check_vma=False,
    )
```

time: 266 us -> 66.4 us (0.25)
  waiting for transfers between devices: 167 us -> 11.5 us
  blocking collectives: 60.1 us -> 0 us
  Pallas kernels: 0 us -> 13 us
  local copies, waits for them, and re-layouts: 0.45 us -> 7.53 us
  other arithmetic: 9.43 us -> 15.4 us
  starting transfers between devices: 22.6 us -> 17 us
  matrix products: 4.54 us -> 0 us
    ppermute x9 -> x13, waiting for transfers between devices: 143 us -> 11.5 us  [exchange(): lax.ppermute(value, AXES, [(i, i ^ mask) for i in range(domains * shards)])]
    psum x1 -> x0, blocking collectives: 39.5 us -> none  [share_scores(): return lax.psum((aligned, squares, norm_slots), ('domain', 'fsdp'))]
    all_to_all x2 -> x0, waiting for transfers between devices: 23.5 us -> none  [the longest x1 12.1 us: body(): lax.all_to_all(gradients.reshape(1, groups, per_domain, rows_src, columns...]
    all_to_all x1 -> x0, blocking collectives: 20.6 us -> none  [body(): lax.all_to_all(scaled, 'fsdp', split_axis=0, concat_axis=1, tiled=True)]
    pallas_call x0 -> x4, Pallas kernels: none -> 13 us  [call(): pl.pallas_call(kernel, out_shape=tuple(out_shape), in_specs=[pl.BlockSpec...]
    all_to_all x2 -> x0, starting transfers between devices: 10.1 us -> none  [the longest x1 6.39 us: body(): lax.all_to_all(finished.reshape(1, shards, sub_rows, columns), 'fsdp', sp...]
    convert_element_type x4 -> x9, other arithmetic: 0.95 us -> 6.51 us  [half_width(): return exchange(value.astype(jnp.float16), mask).astype(F32)]
    ppermute x9 -> x13, starting transfers between devices: 12.4 us -> 17 us  [exchange(): lax.ppermute(value, AXES, [(i, i ^ mask) for i in range(domains * shards)])]
  transfers between devices with their start and end apart: 11 -> 13, of which waited for: 11 -> 7; matrix products, arithmetic and copies ran while one was open for 2% -> 17% of each run, Pallas kernels for 0% -> 0%
where the time goes in v1:
time: 66.4 us; the launch traced here: 66 us
  starting transfers between devices  17 us (26%)
  other arithmetic  15.4 us (23%)
  Pallas kernels  13 us (20%)
  waiting for transfers between devices  11.5 us (17%)
  local copies, waits for them, and re-layouts  7.53 us (11%)
  between operations  1.44 us (2%)
    ppermute x13, starting transfers between devices, exchange(): lax.ppermute(value, AXES, [(i, i ^ mask) for i in range(domains * shards)])  17 us
    pallas_call x4, Pallas kernels, call(): pl.pallas_call(kernel, out_shape=tuple(out_shape), in_specs=[pl.BlockSpec...  13 us
    ppermute x13, waiting for transfers between devices, exchange(): lax.ppermute(value, AXES, [(i, i ^ mask) for i in range(domains * shards)])  11.5 us
    convert_element_type x9, other arithmetic, half_width(): return exchange(value.astype(jnp.float16), mask).astype(F32)  6.51 us
    unnamed x14, local copies, waits for them, and re-layouts  1.99 us
    squeeze x1, local copies, waits for them, and re-layouts, piece(): return lax.dynamic_index_in_dim(gradients[0], index, 0, keepdims=False)  1.96 us
  transfers between devices with their start and end apart: 13, of which 7 were waited for; matrix products, arithmetic and copies ran while one was open for 17% of the time, Pallas kernels for 0%

profile of v1, /device:TPU:1, one launch (start us, length us, event | category | flops | bytes accessed | tf_op | source)
XLA Modules:
  0.0 66.0 jit_solution(6033837758189573564)
XLA Ops:
  0.7 2.0 %dynamic-slice_bitcast_fusion = (bf16[256,512]{1,0:T(8,128)(2,1)S(1)}, bf16[256,512]{1,0:T(8,128)(2,1)S(1)}, bf16[256,512]{1,0:T(8,128)(2,1)}, bf16[256,512]{1,0:T(8,128)(2,1)S(1)}) fusion(bf16[1,4,256,512]{3,2,1,0:T(8,128)(2,1)} %param.4, s32[]{:T(128)S(6)} %select_n.72, s32[]{:T(128)S(6)} %select_n.70, s32[]{:T(128)S(6)} %select_n.69, s32[]{:T(128)S(6)} %select_n.71), kind=kLoop, calls=%fused_computation.4 | loop fusion | bytes 2097168 | tf_op jit(solution)/shard_map/jit(dynamic_index_in_dim)/squeeze | solution.py:271
  2.6 2.6 %collective-permute-start.2 = (bf16[256,512]{1,0:T(8,128)(2,1)S(1)}, bf16[256,512]{1,0:T(8,128)(2,1)S(1)}, u32[]{:S(2)}, u32[]{:S(2)}) collective-permute-start(bf16[256,512]{1,0:T(8,128)(2,1)S(1)} %get-tuple-element.18), channel_id=1, source_target_pairs={{0,17},{1,16},{2,19},{3,18},{4,21},{5,20},{6,23},{7,22},{8,25},{9,... | collective-permute-start | bytes 786440 | tf_op jit(solution)/shard_map/ppermute | solution.py:268
  8.0 0.7 %multiply_divide_fusion = f32[8]{0:T(128)S(1)} fusion(f32[8]{0:T(128)S(1)} %copy-done.4, f32[8]{0:T(128)S(1)} %convert_reduce_fusion, f32[]{:T(128)} %reduce_sum.45), kind=kLoop, calls=%fused_computation.24 | loop fusion | flops 24 | bytes 100 | tf_op jit(solution)/shard_map/div | solution.py:31
  8.9 1.2 %pad_add_fusion = (s32[2]{0:T(128)}, s32[2]{0:T(128)}) fusion(s32[1]{0:T(128)} %bitcast.1, s32[1]{0:T(128)} %bitcast, s32[]{:T(128)S(6)} %select_n.62, s32[]{:T(128)S(6)} %mul.51, s32[]{:T(128)} %bitcast.3), kind=kLoop, calls=%fused_computation.21 | loop fusion | flops 10 | bytes 36 | tf_op jit(solution)/shard_map/stack | solution.py:297
  11.3 0.8 %collective-permute-done.2.refs_3_ = bf16[256,512]{1,0:T(8,128)(2,1)S(1)} collective-permute-done((bf16[256,512]{1,0:T(8,128)(2,1)S(1)}, bf16[256,512]{1,0:T(8,128)(2,1)S(1)}, u32[]{:S(2)}, u32[]{:S(2)}) %collective-permute-start.2) | collective-permute-done | bytes 262176 | tf_op jit(solution)/shard_map/ppermute | solution.py:268
  12.1 4.9 %collective-permute-done.1.refs_2_ = bf16[256,512]{1,0:T(8,128)(2,1)S(1)} collective-permute-done((bf16[256,512]{1,0:T(8,128)(2,1)S(1)}, bf16[256,512]{1,0:T(8,128)(2,1)S(1)}, u32[]{:S(2)}, u32[]{:S(2)}) %collective-permute-start.1) | collective-permute-done | bytes 262176 | tf_op jit(solution)/shard_map/ppermute | solution.py:268
  17.0 0.7 %copy-done.3 = bf16[256,512]{1,0:T(8,128)(2,1)} copy-done((bf16[256,512]{1,0:T(8,128)(2,1)}, bf16[256,512]{1,0:T(8,128)(2,1)S(1)}, u32[]{:S(2)}) %copy-start.3) | copy-done | bytes 262168
  17.6 3.0 %shard_map.59 = (f32[512,512]{1,0:T(8,128)}, f32[3,272,128]{2,1,0:T(8,128)}, f32[272,128]{1,0:T(8,128)}) custom-call(f32[2]{0:T(128)} %and_select_fusion.mix_ref, s32[2]{0:T(128)} %get-tuple-element.28.lim_ref, s32[2]{0:T(128)} %get-tuple-element.27.pos_ref, bf16[256,512]{1,0:T(8,128)(2,1)} %get-tuple-element.20.refs_0_, bf16[256,512]{1,0:T(8,128)(2,1)} %copy-done.2, ...), custom_call_target="tpu_custom_call" | custom-call | flops 268435456 | bytes 2654232 | tf_op jit(solution)/shard_map/pallas_call | solution.py:241
  20.6 1.0 %convert.5 = f16[3,272,128]{2,1,0:T(8,128)(2,1)S(1)} convert(f32[3,272,128]{2,1,0:T(8,128)} %get-tuple-element.11) | non-fusion elementwise | flops 104448 | bytes 626688 | tf_op jit(solution)/shard_map/convert.2
  21.7 3.3 %collective-permute-start.5 = (f16[272,128]{1,0:T(8,128)(2,1)S(1)}, f16[272,128]{1,0:T(8,128)(2,1)S(1)}, u32[]{:S(2)}, u32[]{:S(2)}) collective-permute-start(f16[272,128]{1,0:T(8,128)(2,1)S(1)} %get-tuple-element.24), channel_id=1, source_target_pairs={{0,6},{1,7},{2,4},{3,5},{4,2},{5,3},{6,0},{7,1},{8,14},{9,15},{10,... | collective-permute-start | bytes 208904 | tf_op jit(solution)/shard_map/ppermute | solution.py:268
  25.4 1.8 %collective-permute-done.5 = f16[272,128]{1,0:T(8,128)(2,1)S(1)} collective-permute-done((f16[272,128]{1,0:T(8,128)(2,1)S(1)}, f16[272,128]{1,0:T(8,128)(2,1)S(1)}, u32[]{:S(2)}, u32[]{:S(2)}) %collective-permute-start.5) | collective-permute-done | bytes 69664 | tf_op jit(solution)/shard_map/ppermute | solution.py:268
  27.8 0.7 %collective-permute-done.4 = f16[272,128]{1,0:T(8,128)(2,1)S(1)} collective-permute-done((f16[272,128]{1,0:T(8,128)(2,1)S(1)}, f16[272,128]{1,0:T(8,128)(2,1)S(1)}, u32[]{:S(2)}, u32[]{:S(2)}) %collective-permute-start.4) | collective-permute-done | bytes 69664 | tf_op jit(solution)/shard_map/ppermute | solution.py:268
  29.8 1.9 %shard_map.60 = (f32[272,128]{1,0:T(8,128)}, f32[272,128]{1,0:T(8,128)}) custom-call(f32[272,128]{1,0:T(8,128)} %get-tuple-element.10.refs_0_, f32[272,128]{1,0:T(8,128)} %convert_element_type.49.refs_1_, f32[272,128]{1,0:T(8,128)} %convert_element_type.51.refs_2_, f32[272,128]{1,0:T(8,128)} %convert_element_type.53.refs_3_), custom_call_target="tpu_custom_call" | custom-call | bytes 835584 | tf_op jit(solution)/shard_map/pallas_call | solution.py:241
  31.8 0.9 %convert_element_type.54 = f16[272,128]{1,0:T(8,128)(2,1)S(1)} convert(f32[272,128]{1,0:T(8,128)} %get-tuple-element.13) | non-fusion elementwise | flops 34816 | bytes 208896 | tf_op jit(solution)/shard_map/convert_element_type | solution.py:329
  32.7 2.4 %collective-permute-start.6 = (f16[272,128]{1,0:T(8,128)(2,1)S(1)}, f16[272,128]{1,0:T(8,128)(2,1)S(1)}, u32[]{:S(2)}, u32[]{:S(2)}) collective-permute-start(f16[272,128]{1,0:T(8,128)(2,1)S(1)} %convert_element_type.54), channel_id=1, source_target_pairs={{0,8},{1,9},{2,10},{3,11},{4,12},{5,13},{6,14},{7,15},{8,0},{9,1},... | collective-permute-start | bytes 208904 | tf_op jit(solution)/shard_map/ppermute | solution.py:268
  35.1 1.7 %collective-permute-done.6 = f16[272,128]{1,0:T(8,128)(2,1)S(1)} collective-permute-done((f16[272,128]{1,0:T(8,128)(2,1)S(1)}, f16[272,128]{1,0:T(8,128)(2,1)S(1)}, u32[]{:S(2)}, u32[]{:S(2)}) %collective-permute-start.6) | collective-permute-done | bytes 69664 | tf_op jit(solution)/shard_map/ppermute | solution.py:268
  37.5 1.8 %shard_map.61 = (f32[272,128]{1,0:T(8,128)}, f32[272,128]{1,0:T(8,128)}) custom-call(f32[272,128]{1,0:T(8,128)} %get-tuple-element.12.refs_0_, f32[272,128]{1,0:T(8,128)} %convert_element_type.55.refs_1_), custom_call_target="tpu_custom_call" | custom-call | bytes 557056 | tf_op jit(solution)/shard_map/pallas_call | solution.py:241
  39.3 0.7 %slice.37 = f32[8,128]{1,0:T(8,128)S(1)} slice(f32[272,128]{1,0:T(8,128)} %get-tuple-element.14.own_ref), slice={[256:264], [0:128]} | slice | bytes 8192 | tf_op jit(solution)/shard_map/slice | solution.py:364
  40.0 2.7 %collective-permute-start.11 = (f32[8,128]{1,0:T(8,128)S(1)}, f32[8,128]{1,0:T(8,128)S(1)}, u32[]{:S(2)}, u32[]{:S(2)}) collective-permute-start(f32[8,128]{1,0:T(8,128)S(1)} %slice.37), channel_id=1, source_target_pairs={{0,1},{1,0},{2,3},{3,2},{4,5},{5,4},{6,7},{7,6},{8,9},{9,8},{10,11... | collective-permute-start | bytes 12296 | tf_op jit(solution)/shard_map/ppermute | solution.py:268
  42.7 0.8 %collective-permute-done.11 = f32[8,128]{1,0:T(8,128)S(1)} collective-permute-done((f32[8,128]{1,0:T(8,128)S(1)}, f32[8,128]{1,0:T(8,128)S(1)}, u32[]{:S(2)}, u32[]{:S(2)}) %collective-permute-start.11) | collective-permute-done | bytes 4128 | tf_op jit(solution)/shard_map/ppermute | solution.py:268
  43.5 0.7 %slice_add_fusion = f32[8,128]{1,0:T(8,128)S(1)} fusion(f32[8,128]{1,0:T(8,128)S(1)} %collective-permute-done.11, f32[272,128]{1,0:T(8,128)} %get-tuple-element.14.own_ref), kind=kLoop, calls=%fused_computation.27 | loop fusion | flops 1024 | bytes 12288 | tf_op jit(solution)/shard_map/add | solution.py:367
  44.2 1.2 %collective-permute-start.12 = (f32[8,128]{1,0:T(8,128)S(1)}, f32[8,128]{1,0:T(8,128)S(1)}, u32[]{:S(2)}, u32[]{:S(2)}) collective-permute-start(f32[8,128]{1,0:T(8,128)S(1)} %slice_add_fusion), channel_id=1, source_target_pairs={{0,16},{1,17},{2,18},{3,19},{4,20},{5,21},{6,22},{7,23},{8,24},{9,... | collective-permute-start | bytes 12296 | tf_op jit(solution)/shard_map/ppermute | solution.py:268
  45.4 0.9 %convert_element_type.56 = f16[272,128]{1,0:T(8,128)(2,1)S(1)} convert(f32[272,128]{1,0:T(8,128)} %get-tuple-element.15) | non-fusion elementwise | flops 34816 | bytes 208896 | tf_op jit(solution)/shard_map/convert_element_type | solution.py:329
  46.3 2.0 %collective-permute-start.9 = (f16[272,128]{1,0:T(8,128)(2,1)S(1)}, f16[272,128]{1,0:T(8,128)(2,1)S(1)}, u32[]{:S(2)}, u32[]{:S(2)}) collective-permute-start(f16[272,128]{1,0:T(8,128)(2,1)S(1)} %convert_element_type.56), channel_id=1, source_target_pairs={{0,6},{1,7},{2,4},{3,5},{4,2},{5,3},{6,0},{7,1},{8,14},{9,15},{10,... | collective-permute-start | bytes 208904 | tf_op jit(solution)/shard_map/ppermute | solution.py:268
  48.3 0.7 %collective-permute-start.7 = (f16[272,128]{1,0:T(8,128)(2,1)S(1)}, f16[272,128]{1,0:T(8,128)(2,1)S(1)}, u32[]{:S(2)}, u32[]{:S(2)}) collective-permute-start(f16[272,128]{1,0:T(8,128)(2,1)S(1)} %convert_element_type.56), channel_id=1, source_target_pairs={{0,2},{1,3},{2,0},{3,1},{4,6},{5,7},{6,4},{7,5},{8,10},{9,11},{10,... | collective-permute-start | bytes 208904 | tf_op jit(solution)/shard_map/ppermute | solution.py:268
  51.2 0.8 %collective-permute-done.8 = f16[272,128]{1,0:T(8,128)(2,1)S(1)} collective-permute-done((f16[272,128]{1,0:T(8,128)(2,1)S(1)}, f16[272,128]{1,0:T(8,128)(2,1)S(1)}, u32[]{:S(2)}, u32[]{:S(2)}) %collective-permute-start.8) | collective-permute-done | bytes 69664 | tf_op jit(solution)/shard_map/ppermute | solution.py:268
  53.3 6.2 %shard_map.62 = bf16[512,512]{1,0:T(8,128)(2,1)} custom-call(s32[2]{0:T(128)} %get-tuple-element.27.pos_ref, f32[512,512]{1,0:T(8,128)} %get-tuple-element.9.comb_ref, f32[272,128]{1,0:T(8,128)} %get-tuple-element.14.own_ref, f32[272,128]{1,0:T(8,128)} %convert_element_type.57.refs_0_, f32[272,128]{1,0:T(8,128)} %convert_element_type.58.refs_1_, ...), custom_call_target="tpu_custom_call" | custom-call | flops 3489660928 | bytes 2129928 | tf_op jit(solution)/shard_map/pallas_call | solution.py:241
  59.6 1.0 %slice.47 = bf16[256,512]{1,0:T(8,128)(2,1)S(1)} slice(bf16[512,512]{1,0:T(8,128)(2,1)} %shard_map.62), slice={[256:512], [0:512]} | slice | bytes 524288 | tf_op jit(solution)/shard_map/slice | solution.py:349
  60.6 1.7 %collective-permute-start.10 = (bf16[256,512]{1,0:T(8,128)(2,1)S(1)}, bf16[256,512]{1,0:T(8,128)(2,1)S(1)}, u32[]{:S(2)}, u32[]{:S(2)}) collective-permute-start(bf16[256,512]{1,0:T(8,128)(2,1)S(1)} %slice.47), channel_id=1, source_target_pairs={{0,1},{1,0},{2,3},{3,2},{4,5},{5,4},{6,7},{7,6},{8,9},{9,8},{10,11... | collective-permute-start | bytes 786440 | tf_op jit(solution)/shard_map/ppermute | solution.py:268
  62.3 1.3 %fusion.2 = (f32[]{:T(128)}, f32[8]{0:T(128)S(1)}) fusion(f32[8]{0:T(128)S(1)} %select_reduce_fusion, f32[8]{0:T(128)S(1)} %convert_reduce_fusion, f32[8]{0:T(128)S(1)} %copy-done.4, f32[]{:T(128)} %reduce_sum.45), kind=kLoop, calls=%fused_computation.28 | loop fusion | flops 47 | bytes 136 | tf_op jit(solution)/shard_map/reduce_sum | solution.py:374
  63.6 1.2 %broadcast_divide_fusion = f32[8]{0:T(128)} fusion(f32[8]{0:T(128)S(1)} %get-tuple-element.17, f32[]{:T(128)} %get-tuple-element.16), kind=kLoop, calls=%fused_computation.26 | loop fusion | flops 8 | bytes 68 | tf_op jit(solution)/shard_map/div | solution.py:374
  64.8 1.1 %convert_multiply_fusion = f32[2,256,512]{2,1,0:T(8,128)} fusion(bf16[1,256,512]{2,1,0:T(8,128)(2,1)S(1)} %get-tuple-element.23, bf16[1,256,512]{2,1,0:T(8,128)(2,1)S(1)} %get-tuple-element.22), kind=kLoop, calls=%fused_computation.1 | loop fusion | flops 786432 | bytes 1572864 | tf_op jit(solution)/shard_map/mul | solution.py:362
  (45 shorter events, 10.0 us)
Async XLA Ops:
  2.6 9.4 %collective-permute-start.2 = (bf16[256,512]{1,0:T(8,128)(2,1)S(1)}, bf16[256,512]{1,0:T(8,128)(2,1)S(1)}, u32[]{:S(2)}, u32[]{:S(2)}) collective-permute-start(bf16[256,512]{1,0:T(8,128)(2,1)S(1)} %get-tuple-element.18), channel_id=1, source_target_pairs={{0,17},{1,16},{2,19},{3,18},{4,21},{5,20},{6,23},{7,22},{8,25},{9,... | collective-permute-start | bytes 786440 | tf_op jit(solution)/shard_map/ppermute | solution.py:268
  5.2 6.9 %collective-permute-start = (bf16[256,512]{1,0:T(8,128)(2,1)S(1)}, bf16[256,512]{1,0:T(8,128)(2,1)S(1)}, u32[]{:S(2)}, u32[]{:S(2)}) collective-permute-start(bf16[256,512]{1,0:T(8,128)(2,1)S(1)} %get-tuple-element.19), channel_id=1, source_target_pairs={{0,1},{1,0},{2,3},{3,2},{4,5},{5,4},{6,7},{7,6},{8,9},{9,8},{10,11... | collective-permute-start | bytes 786440 | tf_op jit(solution)/shard_map/ppermute | solution.py:268
  5.2 11.7 %collective-permute-start.1 = (bf16[256,512]{1,0:T(8,128)(2,1)S(1)}, bf16[256,512]{1,0:T(8,128)(2,1)S(1)}, u32[]{:S(2)}, u32[]{:S(2)}) collective-permute-start(bf16[256,512]{1,0:T(8,128)(2,1)S(1)} %get-tuple-element.21), channel_id=1, source_target_pairs={{0,16},{1,17},{2,18},{3,19},{4,20},{5,21},{6,22},{7,23},{8,24},{9,... | collective-permute-start | bytes 786440 | tf_op jit(solution)/shard_map/ppermute | solution.py:268
  5.3 0.7 copy-start.5
  6.0 0.7 copy-start.6
  6.6 0.7 copy-start.4
  12.1 4.9 %copy-start.1 = (bf16[256,512]{1,0:T(8,128)(2,1)}, bf16[256,512]{1,0:T(8,128)(2,1)S(1)}, u32[]{:S(2)}) copy-start(bf16[256,512]{1,0:T(8,128)(2,1)S(1)} %collective-permute-done.2.refs_3_) | copy-start | bytes 786436
  12.1 4.9 %copy-start.2 = (bf16[256,512]{1,0:T(8,128)(2,1)}, bf16[256,512]{1,0:T(8,128)(2,1)S(1)}, u32[]{:S(2)}) copy-start(bf16[256,512]{1,0:T(8,128)(2,1)S(1)} %collective-permute-done.refs_1_) | copy-start | bytes 786436
  16.9 0.7 %copy-start.3 = (bf16[256,512]{1,0:T(8,128)(2,1)}, bf16[256,512]{1,0:T(8,128)(2,1)S(1)}, u32[]{:S(2)}) copy-start(bf16[256,512]{1,0:T(8,128)(2,1)S(1)} %collective-permute-done.1.refs_2_) | copy-start | bytes 786436
  21.7 5.4 %collective-permute-start.5 = (f16[272,128]{1,0:T(8,128)(2,1)S(1)}, f16[272,128]{1,0:T(8,128)(2,1)S(1)}, u32[]{:S(2)}, u32[]{:S(2)}) collective-permute-start(f16[272,128]{1,0:T(8,128)(2,1)S(1)} %get-tuple-element.24), channel_id=1, source_target_pairs={{0,6},{1,7},{2,4},{3,5},{4,2},{5,3},{6,0},{7,1},{8,14},{9,15},{10,... | collective-permute-start | bytes 208904 | tf_op jit(solution)/shard_map/ppermute | solution.py:268
  25.0 3.5 %collective-permute-start.4 = (f16[272,128]{1,0:T(8,128)(2,1)S(1)}, f16[272,128]{1,0:T(8,128)(2,1)S(1)}, u32[]{:S(2)}, u32[]{:S(2)}) collective-permute-start(f16[272,128]{1,0:T(8,128)(2,1)S(1)} %get-tuple-element.25), channel_id=1, source_target_pairs={{0,4},{1,5},{2,6},{3,7},{4,0},{5,1},{6,2},{7,3},{8,12},{9,13},{10,... | collective-permute-start | bytes 208904 | tf_op jit(solution)/shard_map/ppermute | solution.py:268
  25.2 4.0 %collective-permute-start.3 = (f16[272,128]{1,0:T(8,128)(2,1)S(1)}, f16[272,128]{1,0:T(8,128)(2,1)S(1)}, u32[]{:S(2)}, u32[]{:S(2)}) collective-permute-start(f16[272,128]{1,0:T(8,128)(2,1)S(1)} %get-tuple-element.26), channel_id=1, source_target_pairs={{0,2},{1,3},{2,0},{3,1},{4,6},{5,7},{6,4},{7,5},{8,10},{9,11},{10,... | collective-permute-start | bytes 208904 | tf_op jit(solution)/shard_map/ppermute | solution.py:268
  32.7 4.1 %collective-permute-start.6 = (f16[272,128]{1,0:T(8,128)(2,1)S(1)}, f16[272,128]{1,0:T(8,128)(2,1)S(1)}, u32[]{:S(2)}, u32[]{:S(2)}) collective-permute-start(f16[272,128]{1,0:T(8,128)(2,1)S(1)} %convert_element_type.54), channel_id=1, source_target_pairs={{0,8},{1,9},{2,10},{3,11},{4,12},{5,13},{6,14},{7,15},{8,0},{9,1},... | collective-permute-start | bytes 208904 | tf_op jit(solution)/shard_map/ppermute | solution.py:268
  40.0 3.5 %collective-permute-start.11 = (f32[8,128]{1,0:T(8,128)S(1)}, f32[8,128]{1,0:T(8,128)S(1)}, u32[]{:S(2)}, u32[]{:S(2)}) collective-permute-start(f32[8,128]{1,0:T(8,128)S(1)} %slice.37), channel_id=1, source_target_pairs={{0,1},{1,0},{2,3},{3,2},{4,5},{5,4},{6,7},{7,6},{8,9},{9,8},{10,11... | collective-permute-start | bytes 12296 | tf_op jit(solution)/shard_map/ppermute | solution.py:268
  44.2 4.8 %collective-permute-start.12 = (f32[8,128]{1,0:T(8,128)S(1)}, f32[8,128]{1,0:T(8,128)S(1)}, u32[]{:S(2)}, u32[]{:S(2)}) collective-permute-start(f32[8,128]{1,0:T(8,128)S(1)} %slice_add_fusion), channel_id=1, source_target_pairs={{0,16},{1,17},{2,18},{3,19},{4,20},{5,21},{6,22},{7,23},{8,24},{9,... | collective-permute-start | bytes 12296 | tf_op jit(solution)/shard_map/ppermute | solution.py:268
  46.3 4.2 %collective-permute-start.9 = (f16[272,128]{1,0:T(8,128)(2,1)S(1)}, f16[272,128]{1,0:T(8,128)(2,1)S(1)}, u32[]{:S(2)}, u32[]{:S(2)}) collective-permute-start(f16[272,128]{1,0:T(8,128)(2,1)S(1)} %convert_element_type.56), channel_id=1, source_target_pairs={{0,6},{1,7},{2,4},{3,5},{4,2},{5,3},{6,0},{7,1},{8,14},{9,15},{10,... | collective-permute-start | bytes 208904 | tf_op jit(solution)/shard_map/ppermute | solution.py:268
  48.3 3.7 %collective-permute-start.8 = (f16[272,128]{1,0:T(8,128)(2,1)S(1)}, f16[272,128]{1,0:T(8,128)(2,1)S(1)}, u32[]{:S(2)}, u32[]{:S(2)}) collective-permute-start(f16[272,128]{1,0:T(8,128)(2,1)S(1)} %convert_element_type.56), channel_id=1, source_target_pairs={{0,4},{1,5},{2,6},{3,7},{4,0},{5,1},{6,2},{7,3},{8,12},{9,13},{10,... | collective-permute-start | bytes 208904 | tf_op jit(solution)/shard_map/ppermute | solution.py:268
  48.3 4.4 %collective-permute-start.7 = (f16[272,128]{1,0:T(8,128)(2,1)S(1)}, f16[272,128]{1,0:T(8,128)(2,1)S(1)}, u32[]{:S(2)}, u32[]{:S(2)}) collective-permute-start(f16[272,128]{1,0:T(8,128)(2,1)S(1)} %convert_element_type.56), channel_id=1, source_target_pairs={{0,2},{1,3},{2,0},{3,1},{4,6},{5,7},{6,4},{7,5},{8,10},{9,11},{10,... | collective-permute-start | bytes 208904 | tf_op jit(solution)/shard_map/ppermute | solution.py:268
  59.6 5.2 %copy-start = (bf16[512,512]{1,0:T(8,128)(2,1)S(1)}, bf16[512,512]{1,0:T(8,128)(2,1)}, u32[]{:S(2)}) copy-start(bf16[512,512]{1,0:T(8,128)(2,1)} %shard_map.62) | copy-start | bytes 1572868
  60.6 4.2 %collective-permute-start.10 = (bf16[256,512]{1,0:T(8,128)(2,1)S(1)}, bf16[256,512]{1,0:T(8,128)(2,1)S(1)}, u32[]{:S(2)}, u32[]{:S(2)}) collective-permute-start(bf16[256,512]{1,0:T(8,128)(2,1)S(1)} %slice.47), channel_id=1, source_target_pairs={{0,1},{1,0},{2,3},{3,2},{4,5},{5,4},{6,7},{7,6},{8,9},{9,8},{10,11... | collective-permute-start | bytes 786440 | tf_op jit(solution)/shard_map/ppermute | solution.py:268

commit v2 on v1

--- a/solution.py
+++ b/solution.py
@@ -21,6 +21,7 @@
 TAIL = 16
 HALF_SPAN = 16384.0
 TINY = 1e-30
+VMEM_GRANT = 16 * 1024 * 1024
 F32 = jnp.float32
 
 
@@ -245,6 +246,7 @@
         out_specs=tuple(pl.BlockSpec(memory_space=pltpu.VMEM) for _ in out_shape),
         scratch_shapes=list(scratch),
         cost_estimate=pl.CostEstimate(flops=flops, bytes_accessed=size, transcendentals=0),
+        compiler_params=pltpu.CompilerParams(vmem_limit_bytes=VMEM_GRANT),
     )(*args)
 
 

time: 66.4 us -> 50.5 us (0.76)
  other arithmetic: 15.4 us -> 6.12 us
  Pallas kernels: 13 us -> 6.43 us
  local copies, waits for them, and re-layouts: 7.53 us -> 4.43 us
  waiting for transfers between devices: 11.5 us -> 14.4 us
    pallas_call x4, Pallas kernels: 13 us -> 6.43 us  [call(): pl.pallas_call(kernel, out_shape=tuple(out_shape), in_specs=[pl.BlockSpec...]
    convert_element_type x9, other arithmetic: 6.51 us -> 0.11 us  [half_width(): return exchange(value.astype(jnp.float16), mask).astype(F32)]
    ppermute x13, waiting for transfers between devices: 11.5 us -> 14.4 us  [exchange(): lax.ppermute(value, AXES, [(i, i ^ mask) for i in range(domains * shards)])]
    slice x1, local copies, waits for them, and re-layouts: 1.04 us -> 0.02 us  [body(): finished[k]]
    another operation x1, other arithmetic: 1.03 us -> 0.03 us
    unnamed x14 -> x6, local copies, waits for them, and re-layouts: 1.99 us -> 1.24 us
    squeeze x1, local copies, waits for them, and re-layouts: 1.96 us -> 1.27 us  [piece(): return lax.dynamic_index_in_dim(gradients[0], index, 0, keepdims=False)]
    add x2, other arithmetic: 0.69 us -> 0.01 us  [body(): sums = sums + exchange(sums, flip[stride])]
  transfers between devices with their start and end apart: 13 -> 13, of which waited for: 7 -> 8; matrix products, arithmetic and copies ran while one was open for 17% -> 13% of each run, Pallas kernels for 0% -> 0%
where the time goes in v2:
time: 50.5 us; the launch traced here: 50.3 us
  starting transfers between devices  17.3 us (34%)
  waiting for transfers between devices  14.4 us (29%)
  Pallas kernels  6.43 us (13%)
  other arithmetic  6.12 us (12%)
  local copies, waits for them, and re-layouts  4.43 us (9%)
  between operations  1.52 us (3%)
    ppermute x13, starting transfers between devices, exchange(): lax.ppermute(value, AXES, [(i, i ^ mask) for i in range(domains * shards)])  17.3 us
    ppermute x13, waiting for transfers between devices, exchange(): lax.ppermute(value, AXES, [(i, i ^ mask) for i in range(domains * shards)])  14.4 us
    pallas_call x4, Pallas kernels, call(): pl.pallas_call(kernel, out_shape=tuple(out_shape), in_specs=[pl.BlockSpec...  6.43 us
    squeeze x1, local copies, waits for them, and re-layouts, piece(): return lax.dynamic_index_in_dim(gradients[0], index, 0, keepdims=False)  1.27 us
    reduce_sum x1, other arithmetic, body(): return (updates, raised / jnp.sum(raised))  1.25 us
    unnamed x6, local copies, waits for them, and re-layouts  1.24 us
    div x1, other arithmetic, body(): return (updates, raised / jnp.sum(raised))  1.16 us
    mul x1, other arithmetic, body(): jnp.stack(ordered).astype(F32) * (MUON_SCALE * math.sqrt(full_rows))  1.11 us
  transfers between devices with their start and end apart: 13, of which 8 were waited for; matrix products, arithmetic and copies ran while one was open for 13% of the time, Pallas kernels for 0%

profile of v2, /device:TPU:1, one launch (start us, length us, event | category | flops | bytes accessed | tf_op | source)
XLA Modules:
  0.0 50.3 jit_solution(14797511560092653739)
XLA Ops:
  0.7 1.3 %dynamic-slice_bitcast_fusion = (bf16[256,512]{1,0:T(8,128)(2,1)S(1)}, bf16[256,512]{1,0:T(8,128)(2,1)S(1)}, bf16[256,512]{1,0:T(8,128)(2,1)S(1)}, bf16[256,512]{1,0:T(8,128)(2,1)S(1)}) fusion(bf16[1,4,256,512]{3,2,1,0:T(8,128)(2,1)} %param.4, s32[]{:T(128)S(6)} %select_n.72, s32[]{:T(128)S(6)} %select_n.70, s32[]{:T(128)S(6)} %select_n.69, s32[]{:T(128)S(6)} %select_n.71), kind=kLoop, calls=%fused_computation.4 | loop fusion | bytes 2097168 | tf_op jit(solution)/shard_map/jit(dynamic_index_in_dim)/squeeze | solution.py:273
  1.9 2.7 %collective-permute-start.2 = (bf16[256,512]{1,0:T(8,128)(2,1)S(1)}, bf16[256,512]{1,0:T(8,128)(2,1)S(1)}, u32[]{:S(2)}, u32[]{:S(2)}) collective-permute-start(bf16[256,512]{1,0:T(8,128)(2,1)S(1)} %get-tuple-element.18), channel_id=1, source_target_pairs={{0,17},{1,16},{2,19},{3,18},{4,21},{5,20},{6,23},{7,22},{8,25},{9,... | collective-permute-start | bytes 786440 | tf_op jit(solution)/shard_map/ppermute | solution.py:270
  4.8 0.6 %copy-done.1 = s32[4]{0:T(128)S(1)} copy-done((s32[4]{0:T(128)S(1)}, s32[4]{0:T(128)}, u32[]{:S(2)}) %copy-start.1) | copy-done | bytes 40
  5.4 0.6 %dynamic_slice.17 = s32[1]{0:T(128)} dynamic-slice(s32[4]{0:T(128)S(1)} %copy-done.1, s32[]{:T(128)S(6)} %select_n.69), dynamic_slice_sizes={1} | dynamic-slice | bytes 12 | tf_op jit(solution)/shard_map/jit(dynamic_index_in_dim)/dynamic_slice | solution.py:298
  6.2 0.6 %copy-done = f32[8]{0:T(128)S(1)} copy-done((f32[8]{0:T(128)S(1)}, f32[8]{0:T(128)}, u32[]{:S(2)}) %copy-start) | copy-done | bytes 56
  6.8 0.6 %reduce_sum.45 = f32[]{:T(128)} reduce(f32[8]{0:T(128)S(1)} %copy-done, f32[]{:T(128)} %constant.84.clone.1), dimensions={0}, to_apply=%region_0.1 | reduce | flops 7 | bytes 40 | tf_op jit(solution)/shard_map/reduce_sum | solution.py:29
  7.4 0.6 %multiply_divide_fusion = f32[8]{0:T(128)S(1)} fusion(f32[8]{0:T(128)S(1)} %copy-done, f32[8]{0:T(128)S(1)} %convert_reduce_fusion, f32[]{:T(128)} %reduce_sum.45), kind=kLoop, calls=%fused_computation.24 | loop fusion | flops 24 | bytes 100 | tf_op jit(solution)/shard_map/div | solution.py:32
  8.2 0.7 %pad_add_fusion = (s32[2]{0:T(128)S(1)}, s32[2]{0:T(128)S(1)}) fusion(s32[1]{0:T(128)} %bitcast.1, s32[1]{0:T(128)} %bitcast, s32[]{:T(128)S(6)} %select_n.62, s32[]{:T(128)S(6)} %mul.51, s32[]{:T(128)} %bitcast.3), kind=kLoop, calls=%fused_computation.21 | loop fusion | flops 10 | bytes 36 | tf_op jit(solution)/shard_map/stack | solution.py:299
  8.9 0.6 %gather_fusion = f32[2]{0:T(128)S(1)} fusion(f32[2]{0:T(128)S(1)} %select_reduce_fusion.1, s32[1024]{0:T(1024)S(1)} %pad_clamp_fusion), kind=kCustom, calls=%fused_computation | custom fusion | bytes 24 | tf_op jit(solution)/shard_map/jit(_take)/gather | solution.py:296
  9.6 1.9 %collective-permute-done.2.refs_3_ = bf16[256,512]{1,0:T(8,128)(2,1)S(1)} collective-permute-done((bf16[256,512]{1,0:T(8,128)(2,1)S(1)}, bf16[256,512]{1,0:T(8,128)(2,1)S(1)}, u32[]{:S(2)}, u32[]{:S(2)}) %collective-permute-start.2) | collective-permute-done | bytes 262176 | tf_op jit(solution)/shard_map/ppermute | solution.py:270
  11.5 4.9 %collective-permute-done.1.refs_2_ = bf16[256,512]{1,0:T(8,128)(2,1)S(1)} collective-permute-done((bf16[256,512]{1,0:T(8,128)(2,1)S(1)}, bf16[256,512]{1,0:T(8,128)(2,1)S(1)}, u32[]{:S(2)}, u32[]{:S(2)}) %collective-permute-start.1) | collective-permute-done | bytes 262176 | tf_op jit(solution)/shard_map/ppermute | solution.py:270
  16.3 1.6 %shard_map.59 = (f32[512,512]{1,0:T(8,128)S(1)}, f32[3,272,128]{2,1,0:T(8,128)S(1)}, f32[272,128]{1,0:T(8,128)S(1)}) custom-call(f32[2]{0:T(128)S(1)} %and_select_fusion.mix_ref, s32[2]{0:T(128)S(1)} %get-tuple-element.28.lim_ref, s32[2]{0:T(128)S(1)} %get-tuple-element.27.pos_ref, bf16[256,512]{1,0:T(8,128)(2,1)S(1)} %get-tuple-element.20.refs_0_, ...), custom_call_target="tpu_custom_call" | custom-call | flops 268435456 | bytes 2654232 | tf_op jit(solution)/shard_map/pallas_call | solution.py:242
  18.0 3.3 %collective-permute-start.5 = (f16[272,128]{1,0:T(8,128)(2,1)S(1)}, f16[272,128]{1,0:T(8,128)(2,1)S(1)}, u32[]{:S(2)}, u32[]{:S(2)}) collective-permute-start(f16[272,128]{1,0:T(8,128)(2,1)S(1)} %get-tuple-element.24), channel_id=1, source_target_pairs={{0,6},{1,7},{2,4},{3,5},{4,2},{5,3},{6,0},{7,1},{8,14},{9,15},{10,... | collective-permute-start | bytes 208904 | tf_op jit(solution)/shard_map/ppermute | solution.py:270
  21.4 0.2 collective-permute-start.3
  21.6 1.8 %collective-permute-done.5 = f16[272,128]{1,0:T(8,128)(2,1)S(1)} collective-permute-done((f16[272,128]{1,0:T(8,128)(2,1)S(1)}, f16[272,128]{1,0:T(8,128)(2,1)S(1)}, u32[]{:S(2)}, u32[]{:S(2)}) %collective-permute-start.5) | collective-permute-done | bytes 69664 | tf_op jit(solution)/shard_map/ppermute | solution.py:270
  23.4 1.4 %collective-permute-done.4 = f16[272,128]{1,0:T(8,128)(2,1)S(1)} collective-permute-done((f16[272,128]{1,0:T(8,128)(2,1)S(1)}, f16[272,128]{1,0:T(8,128)(2,1)S(1)}, u32[]{:S(2)}, u32[]{:S(2)}) %collective-permute-start.4) | collective-permute-done | bytes 69664 | tf_op jit(solution)/shard_map/ppermute | solution.py:270
  25.0 2.4 %collective-permute-start.6 = (f16[272,128]{1,0:T(8,128)(2,1)S(1)}, f16[272,128]{1,0:T(8,128)(2,1)S(1)}, u32[]{:S(2)}, u32[]{:S(2)}) collective-permute-start(f16[272,128]{1,0:T(8,128)(2,1)S(1)} %convert_element_type.54), channel_id=1, source_target_pairs={{0,8},{1,9},{2,10},{3,11},{4,12},{5,13},{6,14},{7,15},{8,0},{9,1},... | collective-permute-start | bytes 208904 | tf_op jit(solution)/shard_map/ppermute | solution.py:270
  27.4 1.7 %collective-permute-done.6 = f16[272,128]{1,0:T(8,128)(2,1)S(1)} collective-permute-done((f16[272,128]{1,0:T(8,128)(2,1)S(1)}, f16[272,128]{1,0:T(8,128)(2,1)S(1)}, u32[]{:S(2)}, u32[]{:S(2)}) %collective-permute-start.6) | collective-permute-done | bytes 69664 | tf_op jit(solution)/shard_map/ppermute | solution.py:270
  29.3 3.2 %collective-permute-start.11 = (f32[8,128]{1,0:T(8,128)S(1)}, f32[8,128]{1,0:T(8,128)S(1)}, u32[]{:S(2)}, u32[]{:S(2)}) collective-permute-start(f32[8,128]{1,0:T(8,128)S(1)} %slice.37), channel_id=1, source_target_pairs={{0,1},{1,0},{2,3},{3,2},{4,5},{5,4},{6,7},{7,6},{8,9},{9,8},{10,11... | collective-permute-start | bytes 12296 | tf_op jit(solution)/shard_map/ppermute | solution.py:270
  32.5 0.8 %collective-permute-done.11 = f32[8,128]{1,0:T(8,128)S(1)} collective-permute-done((f32[8,128]{1,0:T(8,128)S(1)}, f32[8,128]{1,0:T(8,128)S(1)}, u32[]{:S(2)}, u32[]{:S(2)}) %collective-permute-start.11) | collective-permute-done | bytes 4128 | tf_op jit(solution)/shard_map/ppermute | solution.py:270
  33.3 1.2 %collective-permute-start.12 = (f32[8,128]{1,0:T(8,128)S(1)}, f32[8,128]{1,0:T(8,128)S(1)}, u32[]{:S(2)}, u32[]{:S(2)}) collective-permute-start(f32[8,128]{1,0:T(8,128)S(1)} %slice_add_fusion), channel_id=1, source_target_pairs={{0,16},{1,17},{2,18},{3,19},{4,20},{5,21},{6,22},{7,23},{8,24},{9,... | collective-permute-start | bytes 12296 | tf_op jit(solution)/shard_map/ppermute | solution.py:270
  34.5 1.6 %collective-permute-start.9 = (f16[272,128]{1,0:T(8,128)(2,1)S(1)}, f16[272,128]{1,0:T(8,128)(2,1)S(1)}, u32[]{:S(2)}, u32[]{:S(2)}) collective-permute-start(f16[272,128]{1,0:T(8,128)(2,1)S(1)} %convert_element_type.56), channel_id=1, source_target_pairs={{0,6},{1,7},{2,4},{3,5},{4,2},{5,3},{6,0},{7,1},{8,14},{9,15},{10,... | collective-permute-start | bytes 208904 | tf_op jit(solution)/shard_map/ppermute | solution.py:270
  36.1 0.4 collective-permute-start.8
  36.5 0.7 %collective-permute-start.7 = (f16[272,128]{1,0:T(8,128)(2,1)S(1)}, f16[272,128]{1,0:T(8,128)(2,1)S(1)}, u32[]{:S(2)}, u32[]{:S(2)}) collective-permute-start(f16[272,128]{1,0:T(8,128)(2,1)S(1)} %convert_element_type.56), channel_id=1, source_target_pairs={{0,2},{1,3},{2,0},{3,1},{4,6},{5,7},{6,4},{7,5},{8,10},{9,11},{10,... | collective-permute-start | bytes 208904 | tf_op jit(solution)/shard_map/ppermute | solution.py:270
  37.2 0.6 %slice.40 = f32[1,1]{1,0:T(1,128)} slice(f32[8,128]{1,0:T(8,128)S(1)} %add.73), slice={[1:2], [4:5]} | slice | bytes 8 | tf_op jit(solution)/shard_map/slice | solution.py:372
  38.7 1.6 %collective-permute-done.8 = f16[272,128]{1,0:T(8,128)(2,1)S(1)} collective-permute-done((f16[272,128]{1,0:T(8,128)(2,1)S(1)}, f16[272,128]{1,0:T(8,128)(2,1)S(1)}, u32[]{:S(2)}, u32[]{:S(2)}) %collective-permute-start.8) | collective-permute-done | bytes 69664 | tf_op jit(solution)/shard_map/ppermute | solution.py:270
  40.3 0.4 collective-permute-done.7
  40.7 4.6 %shard_map.62 = bf16[512,512]{1,0:T(8,128)(2,1)S(1)} custom-call(s32[2]{0:T(128)S(1)} %get-tuple-element.27.pos_ref, f32[512,512]{1,0:T(8,128)S(1)} %get-tuple-element.9.comb_ref, f32[272,128]{1,0:T(8,128)S(1)} %get-tuple-element.14.own_ref, f32[272,128]{1,0:T(8,128)S(1)} %convert_element_type.57.refs_0_, f32[272,128]{1,0:T(8,128)S(1)} %convert_element_type.58.refs_1_, ...), custom_call_target="tpu_custom_call" | custom-call | flops 3489660928 | bytes 2129928 | tf_op jit(solution)/shard_map/pallas_call | solution.py:242
  45.3 1.4 %collective-permute-start.10 = (bf16[256,512]{1,0:T(8,128)(2,1)S(1)}, bf16[256,512]{1,0:T(8,128)(2,1)S(1)}, u32[]{:S(2)}, u32[]{:S(2)}) collective-permute-start(bf16[256,512]{1,0:T(8,128)(2,1)S(1)} %slice.47), channel_id=1, source_target_pairs={{0,1},{1,0},{2,3},{3,2},{4,5},{5,4},{6,7},{7,6},{8,9},{9,8},{10,11... | collective-permute-start | bytes 786440 | tf_op jit(solution)/shard_map/ppermute | solution.py:270
  46.7 1.2 %fusion.2 = (f32[]{:T(128)}, f32[8]{0:T(128)S(1)}) fusion(f32[8]{0:T(128)S(1)} %select_reduce_fusion, f32[8]{0:T(128)S(1)} %convert_reduce_fusion, f32[8]{0:T(128)S(1)} %copy-done, f32[]{:T(128)} %reduce_sum.45), kind=kLoop, calls=%fused_computation.28 | loop fusion | flops 47 | bytes 136 | tf_op jit(solution)/shard_map/reduce_sum | solution.py:376
  47.9 1.2 %broadcast_divide_fusion = f32[8]{0:T(128)} fusion(f32[8]{0:T(128)S(1)} %get-tuple-element.17, f32[]{:T(128)} %get-tuple-element.16), kind=kLoop, calls=%fused_computation.26 | loop fusion | flops 8 | bytes 68 | tf_op jit(solution)/shard_map/div | solution.py:376
  49.2 1.1 %convert_multiply_fusion = f32[2,256,512]{2,1,0:T(8,128)} fusion(bf16[1,256,512]{2,1,0:T(8,128)(2,1)S(1)} %get-tuple-element.23, bf16[1,256,512]{2,1,0:T(8,128)(2,1)S(1)} %get-tuple-element.22), kind=kLoop, calls=%fused_computation.1 | loop fusion | flops 786432 | bytes 1572864 | tf_op jit(solution)/shard_map/mul | solution.py:364
  (37 shorter events, 1.4 us)
Async XLA Ops:
  1.9 9.5 %collective-permute-start.2 = (bf16[256,512]{1,0:T(8,128)(2,1)S(1)}, bf16[256,512]{1,0:T(8,128)(2,1)S(1)}, u32[]{:S(2)}, u32[]{:S(2)}) collective-permute-start(bf16[256,512]{1,0:T(8,128)(2,1)S(1)} %get-tuple-element.18), channel_id=1, source_target_pairs={{0,17},{1,16},{2,19},{3,18},{4,21},{5,20},{6,23},{7,22},{8,25},{9,... | collective-permute-start | bytes 786440 | tf_op jit(solution)/shard_map/ppermute | solution.py:270
  4.6 6.9 %collective-permute-start = (bf16[256,512]{1,0:T(8,128)(2,1)S(1)}, bf16[256,512]{1,0:T(8,128)(2,1)S(1)}, u32[]{:S(2)}, u32[]{:S(2)}) collective-permute-start(bf16[256,512]{1,0:T(8,128)(2,1)S(1)} %get-tuple-element.19), channel_id=1, source_target_pairs={{0,1},{1,0},{2,3},{3,2},{4,5},{5,4},{6,7},{7,6},{8,9},{9,8},{10,11... | collective-permute-start | bytes 786440 | tf_op jit(solution)/shard_map/ppermute | solution.py:270
  4.6 11.7 %collective-permute-start.1 = (bf16[256,512]{1,0:T(8,128)(2,1)S(1)}, bf16[256,512]{1,0:T(8,128)(2,1)S(1)}, u32[]{:S(2)}, u32[]{:S(2)}) collective-permute-start(bf16[256,512]{1,0:T(8,128)(2,1)S(1)} %get-tuple-element.21), channel_id=1, source_target_pairs={{0,16},{1,17},{2,18},{3,19},{4,20},{5,21},{6,22},{7,23},{8,24},{9,... | collective-permute-start | bytes 786440 | tf_op jit(solution)/shard_map/ppermute | solution.py:270
  4.8 0.7 %copy-start.1 = (s32[4]{0:T(128)S(1)}, s32[4]{0:T(128)}, u32[]{:S(2)}) copy-start(s32[4]{0:T(128)} %param.5) | copy-start | bytes 52
  5.4 0.7 %copy-start.2 = (s32[2]{0:T(128)S(1)}, s32[2]{0:T(128)}, u32[]{:S(2)}) copy-start(s32[2]{0:T(128)} %param.6) | copy-start | bytes 28
  6.1 0.7 %copy-start = (f32[8]{0:T(128)S(1)}, f32[8]{0:T(128)}, u32[]{:S(2)}) copy-start(f32[8]{0:T(128)} %param.7) | copy-start | bytes 100
  18.0 5.4 %collective-permute-start.5 = (f16[272,128]{1,0:T(8,128)(2,1)S(1)}, f16[272,128]{1,0:T(8,128)(2,1)S(1)}, u32[]{:S(2)}, u32[]{:S(2)}) collective-permute-start(f16[272,128]{1,0:T(8,128)(2,1)S(1)} %get-tuple-element.24), channel_id=1, source_target_pairs={{0,6},{1,7},{2,4},{3,5},{4,2},{5,3},{6,0},{7,1},{8,14},{9,15},{10,... | collective-permute-start | bytes 208904 | tf_op jit(solution)/shard_map/ppermute | solution.py:270
  21.3 3.5 %collective-permute-start.4 = (f16[272,128]{1,0:T(8,128)(2,1)S(1)}, f16[272,128]{1,0:T(8,128)(2,1)S(1)}, u32[]{:S(2)}, u32[]{:S(2)}) collective-permute-start(f16[272,128]{1,0:T(8,128)(2,1)S(1)} %get-tuple-element.25), channel_id=1, source_target_pairs={{0,4},{1,5},{2,6},{3,7},{4,0},{5,1},{6,2},{7,3},{8,12},{9,13},{10,... | collective-permute-start | bytes 208904 | tf_op jit(solution)/shard_map/ppermute | solution.py:270
  21.4 3.4 %collective-permute-start.3 = (f16[272,128]{1,0:T(8,128)(2,1)S(1)}, f16[272,128]{1,0:T(8,128)(2,1)S(1)}, u32[]{:S(2)}, u32[]{:S(2)}) collective-permute-start(f16[272,128]{1,0:T(8,128)(2,1)S(1)} %get-tuple-element.26), channel_id=1, source_target_pairs={{0,2},{1,3},{2,0},{3,1},{4,6},{5,7},{6,4},{7,5},{8,10},{9,11},{10,... | collective-permute-start | bytes 208904 | tf_op jit(solution)/shard_map/ppermute | solution.py:270
  25.0 4.1 %collective-permute-start.6 = (f16[272,128]{1,0:T(8,128)(2,1)S(1)}, f16[272,128]{1,0:T(8,128)(2,1)S(1)}, u32[]{:S(2)}, u32[]{:S(2)}) collective-permute-start(f16[272,128]{1,0:T(8,128)(2,1)S(1)} %convert_element_type.54), channel_id=1, source_target_pairs={{0,8},{1,9},{2,10},{3,11},{4,12},{5,13},{6,14},{7,15},{8,0},{9,1},... | collective-permute-start | bytes 208904 | tf_op jit(solution)/shard_map/ppermute | solution.py:270
  29.3 4.0 %collective-permute-start.11 = (f32[8,128]{1,0:T(8,128)S(1)}, f32[8,128]{1,0:T(8,128)S(1)}, u32[]{:S(2)}, u32[]{:S(2)}) collective-permute-start(f32[8,128]{1,0:T(8,128)S(1)} %slice.37), channel_id=1, source_target_pairs={{0,1},{1,0},{2,3},{3,2},{4,5},{5,4},{6,7},{7,6},{8,9},{9,8},{10,11... | collective-permute-start | bytes 12296 | tf_op jit(solution)/shard_map/ppermute | solution.py:270
  33.3 3.9 %collective-permute-start.12 = (f32[8,128]{1,0:T(8,128)S(1)}, f32[8,128]{1,0:T(8,128)S(1)}, u32[]{:S(2)}, u32[]{:S(2)}) collective-permute-start(f32[8,128]{1,0:T(8,128)S(1)} %slice_add_fusion), channel_id=1, source_target_pairs={{0,16},{1,17},{2,18},{3,19},{4,20},{5,21},{6,22},{7,23},{8,24},{9,... | collective-permute-start | bytes 12296 | tf_op jit(solution)/shard_map/ppermute | solution.py:270
  34.5 4.2 %collective-permute-start.9 = (f16[272,128]{1,0:T(8,128)(2,1)S(1)}, f16[272,128]{1,0:T(8,128)(2,1)S(1)}, u32[]{:S(2)}, u32[]{:S(2)}) collective-permute-start(f16[272,128]{1,0:T(8,128)(2,1)S(1)} %convert_element_type.56), channel_id=1, source_target_pairs={{0,6},{1,7},{2,4},{3,5},{4,2},{5,3},{6,0},{7,1},{8,14},{9,15},{10,... | collective-permute-start | bytes 208904 | tf_op jit(solution)/shard_map/ppermute | solution.py:270
  36.1 4.2 %collective-permute-start.8 = (f16[272,128]{1,0:T(8,128)(2,1)S(1)}, f16[272,128]{1,0:T(8,128)(2,1)S(1)}, u32[]{:S(2)}, u32[]{:S(2)}) collective-permute-start(f16[272,128]{1,0:T(8,128)(2,1)S(1)} %convert_element_type.56), channel_id=1, source_target_pairs={{0,4},{1,5},{2,6},{3,7},{4,0},{5,1},{6,2},{7,3},{8,12},{9,13},{10,... | collective-permute-start | bytes 208904 | tf_op jit(solution)/shard_map/ppermute | solution.py:270
  36.5 4.2 %collective-permute-start.7 = (f16[272,128]{1,0:T(8,128)(2,1)S(1)}, f16[272,128]{1,0:T(8,128)(2,1)S(1)}, u32[]{:S(2)}, u32[]{:S(2)}) collective-permute-start(f16[272,128]{1,0:T(8,128)(2,1)S(1)} %convert_element_type.56), channel_id=1, source_target_pairs={{0,2},{1,3},{2,0},{3,1},{4,6},{5,7},{6,4},{7,5},{8,10},{9,11},{10,... | collective-permute-start | bytes 208904 | tf_op jit(solution)/shard_map/ppermute | solution.py:270
  45.3 3.8 %collective-permute-start.10 = (bf16[256,512]{1,0:T(8,128)(2,1)S(1)}, bf16[256,512]{1,0:T(8,128)(2,1)S(1)}, u32[]{:S(2)}, u32[]{:S(2)}) collective-permute-start(bf16[256,512]{1,0:T(8,128)(2,1)S(1)} %slice.47), channel_id=1, source_target_pairs={{0,1},{1,0},{2,3},{3,2},{4,5},{5,4},{6,7},{7,6},{8,9},{9,8},{10,11... | collective-permute-start | bytes 786440 | tf_op jit(solution)/shard_map/ppermute | solution.py:270

commit v3 on v2

--- a/solution.py
+++ b/solution.py
@@ -7,6 +7,7 @@
 from jax.experimental import pallas as pl
 from jax.experimental.pallas import tpu as pltpu
 from jax.sharding import PartitionSpec as P
+
 
 NS_ITERS = 3
 COEF_A = 3.4445
@@ -237,6 +238,22 @@
     done_ref[...] = iterate
 
 
+def weight_kernel(domains, count, *refs):
+    tiles, (share_ref, onehot_ref, counts_ref, out_ref) = refs[:count], refs[count:]
+    rows = [ref[1:2, :] for ref in tiles]
+    while len(rows) > 1:
+        rows = [rows[n] + rows[n + 1] for n in range(0, len(rows), 2)]
+    norm = jnp.sqrt(lane_pick(rows[0], 2 * domains))
+    score = jnp.zeros(share_ref.shape, F32)
+    for g in range(domains):
+        aligned, squares = lane_pick(rows[0], g), lane_pick(rows[0], domains + g)
+        cosine = aligned / (jnp.sqrt(squares) * norm + 1e-06)
+        score = score + onehot_ref[g : g + 1, :] * cosine
+    score = score / jnp.maximum(counts_ref[...], 1.0)
+    raised = share_ref[...] * jnp.exp(ETA * score)
+    out_ref[...] = raised / jnp.sum(raised, axis=1, keepdims=True)
+
+
 def call(kernel, out_shape, args, spaces, scratch=(), flops=0):
     size = sum(math.prod(a.shape) * a.dtype.itemsize for a in (*args, *out_shape))
     return pl.pallas_call(
@@ -269,14 +286,16 @@
     def exchange(value, mask):
         return lax.ppermute(value, AXES, [(i, i ^ mask) for i in range(domains * shards)])
 
-    def piece(index):
-        return lax.dynamic_index_in_dim(gradients[0], index, 0, keepdims=False)
+    def piece(source, index):
+        return lax.dynamic_index_in_dim(source[0], index, 0, keepdims=False)
 
     if members <= 8:
         order = sorted(range(1, members), key=lambda k: k // lanes == 0)
-        got = {0: piece(member)}
+        got, held = {}, gradients
         for k in order:
-            got[k] = exchange(piece(member ^ k), flip[k])
+            part, held = lax.optimization_barrier((piece(held, member ^ k), held))
+            got[k] = exchange(part, flip[k])
+        got[0] = piece(held, member)
         blocks = [got[k] for k in range(members)]
     else:
         teams = [
@@ -363,21 +382,26 @@
         ]
     updates = jnp.stack(ordered).astype(F32) * (MUON_SCALE * math.sqrt(full_rows))
 
-    sums = own[per_piece : per_piece + 8]
-    stride = 1
-    while stride < members:
-        sums = sums + exchange(sums, flip[stride])
-        stride *= 2
-    aligned, squares = sums[1, :domains], sums[1, domains : 2 * domains]
-    total_sq = sums[1, scalar_lane]
-    cosine = aligned / (jnp.sqrt(squares) * jnp.sqrt(total_sq) + 1e-06)
-    score = jnp.sum(onehot * cosine[:, None], axis=0) / jnp.maximum(counts, 1.0)
-    raised = weight_share * jnp.exp(ETA * score)
-    return (updates, raised / jnp.sum(raised))
+    tiles = [own[per_piece : per_piece + 8]]
+    if members <= 8:
+        tiles += [exchange(tiles[0], flip[k]) for k in range(1, members)]
+    else:
+        stride = 1
+        while stride < members:
+            tiles = [tiles[0] + exchange(tiles[0], flip[stride])]
+            stride *= 2
+    (weights,) = call(
+        functools.partial(weight_kernel, domains, len(tiles)),
+        [jax.ShapeDtypeStruct((1, weight_share.shape[0]), F32)],
+        [*tiles, weight_share[None], onehot, counts[None]],
+        [vmem] * (len(tiles) + 3),
+    )
+    return (updates, weights[0])
 
 
 def solution(mesh):
     placed = (P("domain", None, "fsdp", None), P(), P(), P())
+
     return jax.shard_map(
         body,
         mesh=mesh,

time: 50.5 us -> 52.5 us (1.040)
  waiting for transfers between devices: 14.4 us -> 17.8 us
  other arithmetic: 6.12 us -> 3.61 us
  starting transfers between devices: 17.3 us -> 18.2 us
  Pallas kernels: 6.43 us -> 7.13 us
  between operations: 1.52 us -> 0.83 us
    ppermute x13 -> x14, waiting for transfers between devices: 14.4 us -> 17.8 us  [exchange(): lax.ppermute(value, AXES, [(i, i ^ mask) for i in range(domains * shards)])]
    div x3 -> x0, other arithmetic: 1.88 us -> none  [the longest x1 1.16 us: body(): return (updates, raised / jnp.sum(raised))]
    unnamed x6 -> x8, local copies, waits for them, and re-layouts: 1.24 us -> 3.04 us
    reduce_sum x2 -> x0, other arithmetic: 1.33 us -> none  [the longest x1 1.25 us: body(): return (updates, raised / jnp.sum(raised))]
    squeeze x1 -> x4, local copies, waits for them, and re-layouts: 1.27 us -> 0.08 us  [piece(): return lax.dynamic_index_in_dim(source[0], index, 0, keepdims=False)]
    ppermute x13 -> x14, starting transfers between devices: 17.3 us -> 18.2 us  [exchange(): lax.ppermute(value, AXES, [(i, i ^ mask) for i in range(domains * shards)])]
    pallas_call x4 -> x5, Pallas kernels: 6.43 us -> 7.13 us  [call(): pl.pallas_call(kernel, out_shape=tuple(out_shape), in_specs=[pl.BlockSpec...]
    broadcast_in_dim x0 -> x1, other arithmetic: none -> 0.65 us  [body(): weight_share[None]]
  transfers between devices with their start and end apart: 13 -> 14, of which waited for: 8 -> 11; matrix products, arithmetic and copies ran while one was open for 13% -> 7% of each run, Pallas kernels for 0% -> 1%
where the time goes in v3:
time: 52.5 us; the launch traced here: 51.9 us
  starting transfers between devices  18.2 us (35%)
  waiting for transfers between devices  17.8 us (34%)
  Pallas kernels  7.13 us (14%)
  local copies, waits for them, and re-layouts  4.43 us (8%)
  other arithmetic  3.61 us (7%)
  between operations  0.83 us (2%)
    ppermute x14, starting transfers between devices, exchange(): lax.ppermute(value, AXES, [(i, i ^ mask) for i in range(domains * shards)])  18.2 us
    ppermute x14, waiting for transfers between devices, exchange(): lax.ppermute(value, AXES, [(i, i ^ mask) for i in range(domains * shards)])  17.8 us
    pallas_call x5, Pallas kernels, call(): pl.pallas_call(kernel, out_shape=tuple(out_shape), in_specs=[pl.BlockSpec...  7.13 us
    unnamed x8, local copies, waits for them, and re-layouts  3.04 us
    mul x1, other arithmetic, body(): jnp.stack(ordered).astype(F32) * (MUON_SCALE * math.sqrt(full_rows))  1.11 us
  transfers between devices with their start and end apart: 14, of which 11 were waited for; matrix products, arithmetic and copies ran while one was open for 7% of the time, Pallas kernels for 1%

profile of v3, /device:TPU:1, one launch (start us, length us, event | category | flops | bytes accessed | tf_op | source)
XLA Modules:
  0.0 51.9 jit_solution(13088261148878737283)
XLA Ops:
  0.7 1.2 %copy-done = bf16[1,4,256,512]{3,2,1,0:T(8,128)(2,1)S(1)} copy-done((bf16[1,4,256,512]{3,2,1,0:T(8,128)(2,1)S(1)}, bf16[1,4,256,512]{3,2,1,0:T(8,128)(2,1)}, u32[]{:S(2)}) %copy-start) | copy-done | bytes 1048600
  2.0 2.7 %collective-permute-start.2 = (bf16[256,512]{1,0:T(8,128)(2,1)S(1)}, bf16[256,512]{1,0:T(8,128)(2,1)S(1)}, u32[]{:S(2)}, u32[]{:S(2)}) collective-permute-start(bf16[256,512]{1,0:T(8,128)(2,1)S(1)} %dynamic-slice_bitcast_fusion.2), channel_id=1, source_target_pairs={{0,17},{1,16},{2,19},{3,18},{4,21},{5,20},{6,23},{7,22},{8,25},{9,... | collective-permute-start | bytes 786440 | tf_op jit(solution)/shard_map/ppermute | solution.py:287
  4.8 0.6 %copy-done.2 = s32[4]{0:T(128)S(1)} copy-done((s32[4]{0:T(128)S(1)}, s32[4]{0:T(128)}, u32[]{:S(2)}) %copy-start.2) | copy-done | bytes 40
  5.4 0.6 %dynamic_slice.17 = s32[1]{0:T(128)} dynamic-slice(s32[4]{0:T(128)S(1)} %copy-done.2, s32[]{:T(128)S(6)} %select_n.69), dynamic_slice_sizes={1} | dynamic-slice | bytes 12 | tf_op jit(solution)/shard_map/jit(dynamic_index_in_dim)/dynamic_slice | solution.py:317
  6.0 0.6 %copy-done.3 = s32[2]{0:T(128)S(1)} copy-done((s32[2]{0:T(128)S(1)}, s32[2]{0:T(128)}, u32[]{:S(2)}) %copy-start.3) | copy-done | bytes 32
  6.7 0.6 %copy-done.1 = f32[8]{0:T(128)S(1)} copy-done((f32[8]{0:T(128)S(1)}, f32[8]{0:T(128)}, u32[]{:S(2)}) %copy-start.1) | copy-done | bytes 56
  7.3 0.6 %reduce_sum.27 = f32[]{:T(128)} reduce(f32[8]{0:T(128)S(1)} %copy-done.1, f32[]{:T(128)} %constant.81.clone.1), dimensions={0}, to_apply=%region_0.1 | reduce | flops 7 | bytes 40 | tf_op jit(solution)/shard_map/reduce_sum | solution.py:30
  7.9 0.7 %divide_bitcast_fusion = (f32[1,8]{1,0:T(1,128)S(1)}, f32[8]{0:T(128)S(1)}) fusion(f32[8]{0:T(128)S(1)} %copy-done.1, f32[]{:T(128)} %reduce_sum.27, f32[8]{0:T(128)S(1)} %fusion.2), kind=kLoop, calls=%fused_computation.20 | loop fusion | flops 32 | bytes 132 | tf_op jit(solution)/shard_map/broadcast_in_dim | solution.py:396
  8.8 0.7 %pad_add_fusion = (s32[2]{0:T(128)S(1)}, s32[2]{0:T(128)S(1)}) fusion(s32[1]{0:T(128)} %bitcast.1, s32[1]{0:T(128)} %bitcast, s32[]{:T(128)S(6)} %select_n.62, s32[]{:T(128)S(6)} %mul.26, s32[]{:T(128)} %bitcast.3), kind=kLoop, calls=%fused_computation.19 | loop fusion | flops 10 | bytes 36 | tf_op jit(solution)/shard_map/stack | solution.py:318
  9.5 0.6 %gather_fusion = f32[2]{0:T(128)S(1)} fusion(f32[2]{0:T(128)S(1)} %select_reduce_fusion, s32[1024]{0:T(1024)S(1)} %pad_clamp_fusion), kind=kCustom, calls=%fused_computation | custom fusion | bytes 24 | tf_op jit(solution)/shard_map/jit(_take)/gather | solution.py:315
  10.1 1.4 %collective-permute-done.2.refs_3_ = bf16[256,512]{1,0:T(8,128)(2,1)S(1)} collective-permute-done((bf16[256,512]{1,0:T(8,128)(2,1)S(1)}, bf16[256,512]{1,0:T(8,128)(2,1)S(1)}, u32[]{:S(2)}, u32[]{:S(2)}) %collective-permute-start.2) | collective-permute-done | bytes 262176 | tf_op jit(solution)/shard_map/ppermute | solution.py:287
  11.6 5.4 %collective-permute-done.1.refs_2_ = bf16[256,512]{1,0:T(8,128)(2,1)S(1)} collective-permute-done((bf16[256,512]{1,0:T(8,128)(2,1)S(1)}, bf16[256,512]{1,0:T(8,128)(2,1)S(1)}, u32[]{:S(2)}, u32[]{:S(2)}) %collective-permute-start.1) | collective-permute-done | bytes 262176 | tf_op jit(solution)/shard_map/ppermute | solution.py:287
  16.9 1.6 %shard_map.59 = (f32[512,512]{1,0:T(8,128)S(1)}, f32[3,272,128]{2,1,0:T(8,128)S(1)}, f32[272,128]{1,0:T(8,128)S(1)}) custom-call(f32[2]{0:T(128)S(1)} %and_select_fusion.mix_ref, s32[2]{0:T(128)S(1)} %get-tuple-element.36.lim_ref, s32[2]{0:T(128)S(1)} %get-tuple-element.35.pos_ref, bf16[256,512]{1,0:T(8,128)(2,1)S(1)} %dynamic-slice_bitcast_fusion.refs_0_, ...), custom_call_target="tpu_custom_call" | custom-call | flops 268435456 | bytes 2654232 | tf_op jit(solution)/shard_map/pallas_call | solution.py:259
  18.6 1.2 %collective-permute-start.3 = (f16[272,128]{1,0:T(8,128)(2,1)S(1)}, f16[272,128]{1,0:T(8,128)(2,1)S(1)}, u32[]{:S(2)}, u32[]{:S(2)}) collective-permute-start(f16[272,128]{1,0:T(8,128)(2,1)S(1)} %get-tuple-element.32), channel_id=1, source_target_pairs={{0,2},{1,3},{2,0},{3,1},{4,6},{5,7},{6,4},{7,5},{8,10},{9,11},{10,... | collective-permute-start | bytes 208904 | tf_op jit(solution)/shard_map/ppermute | solution.py:287
  19.8 1.3 %collective-permute-start.4 = (f16[272,128]{1,0:T(8,128)(2,1)S(1)}, f16[272,128]{1,0:T(8,128)(2,1)S(1)}, u32[]{:S(2)}, u32[]{:S(2)}) collective-permute-start(f16[272,128]{1,0:T(8,128)(2,1)S(1)} %get-tuple-element.31), channel_id=1, source_target_pairs={{0,4},{1,5},{2,6},{3,7},{4,0},{5,1},{6,2},{7,3},{8,12},{9,13},{10,... | collective-permute-start | bytes 208904 | tf_op jit(solution)/shard_map/ppermute | solution.py:287
  21.3 0.5 collective-permute-done.3
  21.8 1.4 %collective-permute-done.4 = f16[272,128]{1,0:T(8,128)(2,1)S(1)} collective-permute-done((f16[272,128]{1,0:T(8,128)(2,1)S(1)}, f16[272,128]{1,0:T(8,128)(2,1)S(1)}, u32[]{:S(2)}, u32[]{:S(2)}) %collective-permute-start.4) | collective-permute-done | bytes 69664 | tf_op jit(solution)/shard_map/ppermute | solution.py:287
  23.2 1.9 %collective-permute-done.5 = f16[272,128]{1,0:T(8,128)(2,1)S(1)} collective-permute-done((f16[272,128]{1,0:T(8,128)(2,1)S(1)}, f16[272,128]{1,0:T(8,128)(2,1)S(1)}, u32[]{:S(2)}, u32[]{:S(2)}) %collective-permute-start.5) | collective-permute-done | bytes 69664 | tf_op jit(solution)/shard_map/ppermute | solution.py:287
  25.4 2.6 %collective-permute-start.6 = (f16[272,128]{1,0:T(8,128)(2,1)S(1)}, f16[272,128]{1,0:T(8,128)(2,1)S(1)}, u32[]{:S(2)}, u32[]{:S(2)}) collective-permute-start(f16[272,128]{1,0:T(8,128)(2,1)S(1)} %convert_element_type.54), channel_id=1, source_target_pairs={{0,8},{1,9},{2,10},{3,11},{4,12},{5,13},{6,14},{7,15},{8,0},{9,1},... | collective-permute-start | bytes 208904 | tf_op jit(solution)/shard_map/ppermute | solution.py:287
  27.9 2.3 %collective-permute-done.6 = f16[272,128]{1,0:T(8,128)(2,1)S(1)} collective-permute-done((f16[272,128]{1,0:T(8,128)(2,1)S(1)}, f16[272,128]{1,0:T(8,128)(2,1)S(1)}, u32[]{:S(2)}, u32[]{:S(2)}) %collective-permute-start.6) | collective-permute-done | bytes 69664 | tf_op jit(solution)/shard_map/ppermute | solution.py:287
  30.4 0.5 collective-permute-start.7
  30.9 2.2 %collective-permute-start.9 = (f16[272,128]{1,0:T(8,128)(2,1)S(1)}, f16[272,128]{1,0:T(8,128)(2,1)S(1)}, u32[]{:S(2)}, u32[]{:S(2)}) collective-permute-start(f16[272,128]{1,0:T(8,128)(2,1)S(1)} %convert_element_type.56), channel_id=1, source_target_pairs={{0,6},{1,7},{2,4},{3,5},{4,2},{5,3},{6,0},{7,1},{8,14},{9,15},{10,... | collective-permute-start | bytes 208904 | tf_op jit(solution)/shard_map/ppermute | solution.py:287
  33.1 0.5 collective-permute-done.7
  33.6 0.4 collective-permute-done.8
  34.1 1.5 %collective-permute-done.9 = f16[272,128]{1,0:T(8,128)(2,1)S(1)} collective-permute-done((f16[272,128]{1,0:T(8,128)(2,1)S(1)}, f16[272,128]{1,0:T(8,128)(2,1)S(1)}, u32[]{:S(2)}, u32[]{:S(2)}) %collective-permute-start.9) | collective-permute-done | bytes 69664 | tf_op jit(solution)/shard_map/ppermute | solution.py:287
  35.6 4.6 %shard_map.62 = bf16[512,512]{1,0:T(8,128)(2,1)S(1)} custom-call(s32[2]{0:T(128)S(1)} %get-tuple-element.35.pos_ref, f32[512,512]{1,0:T(8,128)S(1)} %get-tuple-element.21.comb_ref, f32[272,128]{1,0:T(8,128)S(1)} %get-tuple-element.26.own_ref, f32[272,128]{1,0:T(8,128)S(1)} %convert_element_type.57.refs_0_, f32[272,128]{1,0:T(8,128)S(1)} %convert_element_type.58.refs_1_, ...), custom_call_target="tpu_custom_call" | custom-call | flops 3489660928 | bytes 2129928 | tf_op jit(solution)/shard_map/pallas_call | solution.py:259
  40.2 5.2 %collective-permute-start.10 = (bf16[256,512]{1,0:T(8,128)(2,1)S(1)}, bf16[256,512]{1,0:T(8,128)(2,1)S(1)}, u32[]{:S(2)}, u32[]{:S(2)}) collective-permute-start(bf16[256,512]{1,0:T(8,128)(2,1)S(1)} %slice.35), channel_id=1, source_target_pairs={{0,1},{1,0},{2,3},{3,2},{4,5},{5,4},{6,7},{7,6},{8,9},{9,8},{10,11... | collective-permute-start | bytes 786440 | tf_op jit(solution)/shard_map/ppermute | solution.py:287
  45.5 1.2 %collective-permute-start.12 = (f32[8,128]{1,0:T(8,128)S(1)}, f32[8,128]{1,0:T(8,128)S(1)}, u32[]{:S(2)}, u32[]{:S(2)}) collective-permute-start(f32[8,128]{1,0:T(8,128)S(1)} %slice.28.refs_0_), channel_id=1, source_target_pairs={{0,16},{1,17},{2,18},{3,19},{4,20},{5,21},{6,22},{7,23},{8,24},{9,... | collective-permute-start | bytes 12296 | tf_op jit(solution)/shard_map/ppermute | solution.py:287
  46.7 0.8 %collective-permute-start.13 = (f32[8,128]{1,0:T(8,128)S(1)}, f32[8,128]{1,0:T(8,128)S(1)}, u32[]{:S(2)}, u32[]{:S(2)}) collective-permute-start(f32[8,128]{1,0:T(8,128)S(1)} %slice.28.refs_0_), channel_id=1, source_target_pairs={{0,17},{1,16},{2,19},{3,18},{4,21},{5,20},{6,23},{7,22},{8,25},{9,... | collective-permute-start | bytes 12296 | tf_op jit(solution)/shard_map/ppermute | solution.py:287
  48.0 2.1 %collective-permute-done.13.refs_3_ = f32[8,128]{1,0:T(8,128)S(1)} collective-permute-done((f32[8,128]{1,0:T(8,128)S(1)}, f32[8,128]{1,0:T(8,128)S(1)}, u32[]{:S(2)}, u32[]{:S(2)}) %collective-permute-start.13) | collective-permute-done | bytes 4128 | tf_op jit(solution)/shard_map/ppermute | solution.py:287
  50.1 0.7 %shard_map.63 = f32[1,8]{1,0:T(1,128)} custom-call(f32[8,128]{1,0:T(8,128)S(1)} %slice.28.refs_0_, f32[8,128]{1,0:T(8,128)S(1)} %collective-permute-done.11.refs_1_, f32[8,128]{1,0:T(8,128)S(1)} %collective-permute-done.12.refs_2_, f32[8,128]{1,0:T(8,128)S(1)} %collective-permute-done.13.refs_3_, f32[1,8]{1,0:T(1,128)S(1)} %get-tuple-element.33.refs_4_, ...), custom_call_target="tpu_custom_call" | custom-call | bytes 16544 | tf_op jit(solution)/shard_map/pallas_call | solution.py:259
  50.8 1.1 %convert_multiply_fusion = f32[2,256,512]{2,1,0:T(8,128)} fusion(bf16[1,256,512]{2,1,0:T(8,128)(2,1)S(1)} %get-tuple-element.29, bf16[1,256,512]{2,1,0:T(8,128)(2,1)S(1)} %get-tuple-element.28), kind=kLoop, calls=%fused_computation.1 | loop fusion | flops 786432 | bytes 1572864 | tf_op jit(solution)/shard_map/mul | solution.py:383
  (39 shorter events, 1.8 us)
Async XLA Ops:
  0.6 1.2 %copy-start = (bf16[1,4,256,512]{3,2,1,0:T(8,128)(2,1)S(1)}, bf16[1,4,256,512]{3,2,1,0:T(8,128)(2,1)}, u32[]{:S(2)}) copy-start(bf16[1,4,256,512]{3,2,1,0:T(8,128)(2,1)} %param.4) | copy-start | bytes 3145732
  2.0 8.2 %collective-permute-start = (bf16[256,512]{1,0:T(8,128)(2,1)S(1)}, bf16[256,512]{1,0:T(8,128)(2,1)S(1)}, u32[]{:S(2)}, u32[]{:S(2)}) collective-permute-start(bf16[256,512]{1,0:T(8,128)(2,1)S(1)} %dynamic-slice_bitcast_fusion.1), channel_id=1, source_target_pairs={{0,1},{1,0},{2,3},{3,2},{4,5},{5,4},{6,7},{7,6},{8,9},{9,8},{10,11... | collective-permute-start | bytes 786440 | tf_op jit(solution)/shard_map/ppermute | solution.py:287
  2.0 9.5 %collective-permute-start.2 = (bf16[256,512]{1,0:T(8,128)(2,1)S(1)}, bf16[256,512]{1,0:T(8,128)(2,1)S(1)}, u32[]{:S(2)}, u32[]{:S(2)}) collective-permute-start(bf16[256,512]{1,0:T(8,128)(2,1)S(1)} %dynamic-slice_bitcast_fusion.2), channel_id=1, source_target_pairs={{0,17},{1,16},{2,19},{3,18},{4,21},{5,20},{6,23},{7,22},{8,25},{9,... | collective-permute-start | bytes 786440 | tf_op jit(solution)/shard_map/ppermute | solution.py:287
  4.7 12.3 %collective-permute-start.1 = (bf16[256,512]{1,0:T(8,128)(2,1)S(1)}, bf16[256,512]{1,0:T(8,128)(2,1)S(1)}, u32[]{:S(2)}, u32[]{:S(2)}) collective-permute-start(bf16[256,512]{1,0:T(8,128)(2,1)S(1)} %dynamic-slice_bitcast_fusion.3), channel_id=1, source_target_pairs={{0,16},{1,17},{2,18},{3,19},{4,20},{5,21},{6,22},{7,23},{8,24},{9,... | collective-permute-start | bytes 786440 | tf_op jit(solution)/shard_map/ppermute | solution.py:287
  4.7 0.7 %copy-start.2 = (s32[4]{0:T(128)S(1)}, s32[4]{0:T(128)}, u32[]{:S(2)}) copy-start(s32[4]{0:T(128)} %param.5) | copy-start | bytes 52
  6.0 0.7 %copy-start.3 = (s32[2]{0:T(128)S(1)}, s32[2]{0:T(128)}, u32[]{:S(2)}) copy-start(s32[2]{0:T(128)} %param.6) | copy-start | bytes 28
  6.7 0.7 %copy-start.1 = (f32[8]{0:T(128)S(1)}, f32[8]{0:T(128)}, u32[]{:S(2)}) copy-start(f32[8]{0:T(128)} %param.7) | copy-start | bytes 100
  18.6 3.2 %collective-permute-start.3 = (f16[272,128]{1,0:T(8,128)(2,1)S(1)}, f16[272,128]{1,0:T(8,128)(2,1)S(1)}, u32[]{:S(2)}, u32[]{:S(2)}) collective-permute-start(f16[272,128]{1,0:T(8,128)(2,1)S(1)} %get-tuple-element.32), channel_id=1, source_target_pairs={{0,2},{1,3},{2,0},{3,1},{4,6},{5,7},{6,4},{7,5},{8,10},{9,11},{10,... | collective-permute-start | bytes 208904 | tf_op jit(solution)/shard_map/ppermute | solution.py:287
  19.8 3.5 %collective-permute-start.4 = (f16[272,128]{1,0:T(8,128)(2,1)S(1)}, f16[272,128]{1,0:T(8,128)(2,1)S(1)}, u32[]{:S(2)}, u32[]{:S(2)}) collective-permute-start(f16[272,128]{1,0:T(8,128)(2,1)S(1)} %get-tuple-element.31), channel_id=1, source_target_pairs={{0,4},{1,5},{2,6},{3,7},{4,0},{5,1},{6,2},{7,3},{8,12},{9,13},{10,... | collective-permute-start | bytes 208904 | tf_op jit(solution)/shard_map/ppermute | solution.py:287
  21.1 4.1 %collective-permute-start.5 = (f16[272,128]{1,0:T(8,128)(2,1)S(1)}, f16[272,128]{1,0:T(8,128)(2,1)S(1)}, u32[]{:S(2)}, u32[]{:S(2)}) collective-permute-start(f16[272,128]{1,0:T(8,128)(2,1)S(1)} %get-tuple-element.30), channel_id=1, source_target_pairs={{0,6},{1,7},{2,4},{3,5},{4,2},{5,3},{6,0},{7,1},{8,14},{9,15},{10,... | collective-permute-start | bytes 208904 | tf_op jit(solution)/shard_map/ppermute | solution.py:287
  25.4 4.9 %collective-permute-start.6 = (f16[272,128]{1,0:T(8,128)(2,1)S(1)}, f16[272,128]{1,0:T(8,128)(2,1)S(1)}, u32[]{:S(2)}, u32[]{:S(2)}) collective-permute-start(f16[272,128]{1,0:T(8,128)(2,1)S(1)} %convert_element_type.54), channel_id=1, source_target_pairs={{0,8},{1,9},{2,10},{3,11},{4,12},{5,13},{6,14},{7,15},{8,0},{9,1},... | collective-permute-start | bytes 208904 | tf_op jit(solution)/shard_map/ppermute | solution.py:287
  30.4 3.2 %collective-permute-start.7 = (f16[272,128]{1,0:T(8,128)(2,1)S(1)}, f16[272,128]{1,0:T(8,128)(2,1)S(1)}, u32[]{:S(2)}, u32[]{:S(2)}) collective-permute-start(f16[272,128]{1,0:T(8,128)(2,1)S(1)} %convert_element_type.56), channel_id=1, source_target_pairs={{0,2},{1,3},{2,0},{3,1},{4,6},{5,7},{6,4},{7,5},{8,10},{9,11},{10,... | collective-permute-start | bytes 208904 | tf_op jit(solution)/shard_map/ppermute | solution.py:287
  30.9 3.2 %collective-permute-start.8 = (f16[272,128]{1,0:T(8,128)(2,1)S(1)}, f16[272,128]{1,0:T(8,128)(2,1)S(1)}, u32[]{:S(2)}, u32[]{:S(2)}) collective-permute-start(f16[272,128]{1,0:T(8,128)(2,1)S(1)} %convert_element_type.56), channel_id=1, source_target_pairs={{0,4},{1,5},{2,6},{3,7},{4,0},{5,1},{6,2},{7,3},{8,12},{9,13},{10,... | collective-permute-start | bytes 208904 | tf_op jit(solution)/shard_map/ppermute | solution.py:287
  30.9 4.6 %collective-permute-start.9 = (f16[272,128]{1,0:T(8,128)(2,1)S(1)}, f16[272,128]{1,0:T(8,128)(2,1)S(1)}, u32[]{:S(2)}, u32[]{:S(2)}) collective-permute-start(f16[272,128]{1,0:T(8,128)(2,1)S(1)} %convert_element_type.56), channel_id=1, source_target_pairs={{0,6},{1,7},{2,4},{3,5},{4,2},{5,3},{6,0},{7,1},{8,14},{9,15},{10,... | collective-permute-start | bytes 208904 | tf_op jit(solution)/shard_map/ppermute | solution.py:287
  40.2 10.6 %collective-permute-start.10 = (bf16[256,512]{1,0:T(8,128)(2,1)S(1)}, bf16[256,512]{1,0:T(8,128)(2,1)S(1)}, u32[]{:S(2)}, u32[]{:S(2)}) collective-permute-start(bf16[256,512]{1,0:T(8,128)(2,1)S(1)} %slice.35), channel_id=1, source_target_pairs={{0,1},{1,0},{2,3},{3,2},{4,5},{5,4},{6,7},{7,6},{8,9},{9,8},{10,11... | collective-permute-start | bytes 786440 | tf_op jit(solution)/shard_map/ppermute | solution.py:287
  45.4 2.2 %collective-permute-start.11 = (f32[8,128]{1,0:T(8,128)S(1)}, f32[8,128]{1,0:T(8,128)S(1)}, u32[]{:S(2)}, u32[]{:S(2)}) collective-permute-start(f32[8,128]{1,0:T(8,128)S(1)} %slice.28.refs_0_), channel_id=1, source_target_pairs={{0,1},{1,0},{2,3},{3,2},{4,5},{5,4},{6,7},{7,6},{8,9},{9,8},{10,11... | collective-permute-start | bytes 12296 | tf_op jit(solution)/shard_map/ppermute | solution.py:287
  45.5 2.5 %collective-permute-start.12 = (f32[8,128]{1,0:T(8,128)S(1)}, f32[8,128]{1,0:T(8,128)S(1)}, u32[]{:S(2)}, u32[]{:S(2)}) collective-permute-start(f32[8,128]{1,0:T(8,128)S(1)} %slice.28.refs_0_), channel_id=1, source_target_pairs={{0,16},{1,17},{2,18},{3,19},{4,20},{5,21},{6,22},{7,23},{8,24},{9,... | collective-permute-start | bytes 12296 | tf_op jit(solution)/shard_map/ppermute | solution.py:287
  46.7 3.4 %collective-permute-start.13 = (f32[8,128]{1,0:T(8,128)S(1)}, f32[8,128]{1,0:T(8,128)S(1)}, u32[]{:S(2)}, u32[]{:S(2)}) collective-permute-start(f32[8,128]{1,0:T(8,128)S(1)} %slice.28.refs_0_), channel_id=1, source_target_pairs={{0,17},{1,16},{2,19},{3,18},{4,21},{5,20},{6,23},{7,22},{8,25},{9,... | collective-permute-start | bytes 12296 | tf_op jit(solution)/shard_map/ppermute | solution.py:287

commit v4 on v2

v4 whole, which is shorter than its diff:
```python
import functools
import math

import jax
import jax.numpy as jnp
from jax import lax
from jax.experimental import pallas as pl
from jax.experimental.pallas import tpu as pltpu
from jax.sharding import PartitionSpec as P


NS_ITERS = 3
COEF_A = 3.4445
COEF_B = -4.775
COEF_C = 2.0315
MUON_SCALE = 0.2
ETA = 4.0

AXES = ("domain", "fsdp")
BLOCK = 128
SQUARE = 4
TAIL = 16
HALF_SPAN = 16384.0
TINY = 1e-30
VMEM_GRANT = 16 * 1024 * 1024
F32 = jnp.float32


def group_mixing(domain_ids, domain_weights, kind_count):
    weight_share = domain_weights / jnp.sum(domain_weights)
    onehot = (domain_ids[:, None] == jnp.arange(kind_count, dtype=jnp.int32)[None, :]).astype(F32)
    counts = jnp.sum(onehot, axis=0)
    per_member = weight_share / jnp.maximum(counts, 1.0)
    group_mix = jnp.sum(onehot * per_member[None, :], axis=1)
    return (weight_share, onehot, counts, group_mix)


def block_plan(columns):
    count = columns // BLOCK
    off = [(i, j) for i in range(count) for j in range(i + 1, count)]
    folded = [(i, i) for i in range(0, count, 2)]
    per_piece = (len(off) + len(folded)) // SQUARE
    pieces = []
    for p in range(SQUARE):
        take = per_piece - (1 if p >= SQUARE - len(folded) else 0)
        pieces.append([off.pop(0) for _ in range(take)])
    for n, pair in enumerate(folded):
        pieces[SQUARE - len(folded) + n].append(pair)
    return pieces


def lane_pick(row, index):
    lanes = lax.broadcasted_iota(jnp.int32, row.shape, 1)
    return jnp.sum(jnp.where(lanes == index, row, 0.0), axis=1, keepdims=True)


def encode_row(row):
    power = jnp.clip(jnp.floor(jnp.log2(jnp.abs(row))), -120.0, 120.0)
    scaled = row * jnp.exp2(-power)
    high = scaled.astype(jnp.bfloat16).astype(F32)
    rest = scaled - high
    mid = rest.astype(jnp.bfloat16).astype(F32)
    low = (rest - mid).astype(jnp.bfloat16).astype(F32)
    return (high, mid * 256.0, low * 65536.0, power)


def decode_row(parts):
    high, mid, low, power = parts
    return ((high + mid * (1.0 / 256.0)) + low * (1.0 / 65536.0)) * jnp.exp2(power)


def tail_rows(rows):
    index = lax.broadcasted_iota(jnp.int32, (TAIL, BLOCK), 0)
    out = jnp.zeros((TAIL, BLOCK), F32)
    for n, row in enumerate(rows):
        out = jnp.where(index == n, row, out)
    return out


def fetch_kernel(count, index_ref, source_ref, *refs):
    outs, sems = refs[:count], refs[count]
    copies = [
        pltpu.make_async_copy(source_ref.at[index_ref[n]], outs[n], sems.at[n])
        for n in range(count)
    ]
    for copy in copies:
        copy.start()
    for copy in copies:
        copy.wait()


def gram_kernel(domains, stage, last, mix_ref, lim_ref, pos_ref, *refs):
    blocks, refs = refs[:domains], refs[domains:]
    if stage:
        sofar_ref, scal_ref, refs = refs[0], refs[1], refs[2:]
    comb_ref, refs = refs[0], refs[1:]
    rows, columns = blocks[0].shape
    domain_pos, quad = pos_ref[0], pos_ref[1]

    def total(v):
        return jnp.sum(jnp.sum(v, axis=0, keepdims=True), axis=1, keepdims=True)

    keep = lax.broadcasted_iota(jnp.int32, (rows, 1), 0) < lim_ref[stage]
    masked = [jnp.where(keep, ref[...].astype(F32), 0.0) for ref in blocks]
    combined = mix_ref[0] * masked[0]
    for kd in range(1, domains):
        combined = combined + mix_ref[kd] * masked[kd]
    comb_ref[...] = combined
    rounded = combined.astype(jnp.bfloat16)
    gram = lax.dot_general(
        rounded, rounded, (((0,), (0,)), ((), ())), preferred_element_type=F32
    )
    lane = lax.broadcasted_iota(jnp.int32, (1, BLOCK), 1)
    scal = jnp.where(lane == 2 * domains, total(combined * combined), 0.0)
    for kd in range(domains):
        group = domain_pos ^ kd
        scal = jnp.where(lane == group, total(masked[kd] * combined), scal)
        scal = jnp.where(lane == domains + group, total(masked[kd] * masked[kd]), scal)
    if stage:
        scal = scal + scal_ref[0:1, :]
    if not last:
        gram_ref, sums_ref = refs
        gram_ref[...] = gram + sofar_ref[...] if stage else gram
        sums_ref[...] = jnp.broadcast_to(scal, sums_ref.shape)
        return

    pay_ref, own_ref, piece_ref, diag_ref = refs
    parts = encode_row(scal)
    scal = decode_row(parts)
    frob = lane_pick(scal, 2 * domains)
    scale = jnp.where(frob > TINY, HALF_SPAN / jnp.maximum(frob, TINY), 0.0)
    row_id = lax.broadcasted_iota(jnp.int32, (BLOCK, BLOCK), 0)
    col_id = lax.broadcasted_iota(jnp.int32, (BLOCK, BLOCK), 1)

    def part(i, j):
        value = gram[i * BLOCK : (i + 1) * BLOCK, j * BLOCK : (j + 1) * BLOCK]
        if stage:
            value = value + sofar_ref[pl.ds(i * BLOCK, BLOCK), pl.ds(j * BLOCK, BLOCK)]
        return value

    for p, entries in enumerate(block_plan(columns)):
        diag = jnp.zeros((1, BLOCK), F32)
        for n, (i, j) in enumerate(entries):
            if i == j:
                upper, lower = part(i, i), part(i + 1, i + 1)
                value = jnp.where(row_id < col_id, upper, lower)
                diag = jnp.sum(jnp.where(row_id == col_id, upper, 0.0), axis=0, keepdims=True)
            else:
                value = part(i, j)
            piece_ref[p, pl.ds(n * BLOCK, BLOCK), :] = value
        diag_ref[p] = jnp.broadcast_to(diag, diag_ref.shape[1:])
    body_rows = piece_ref.shape[1]
    for k in range(SQUARE):
        value = piece_ref[quad ^ k]
        diag = diag_ref[quad ^ k][0:1]
        if k == 0:
            own_ref[pl.ds(0, body_rows), :] = value
            own_ref[pl.ds(body_rows, TAIL), :] = tail_rows([diag, scal])
        else:
            pay_ref[k - 1, pl.ds(0, body_rows), :] = value * scale
            pay_ref[k - 1, pl.ds(body_rows, TAIL), :] = tail_rows([diag * scale, *parts])


def tree_sum(terms):
    while len(terms) > 1:
        terms = [terms[n] + terms[n + 1] for n in range(0, len(terms), 2)]
    return terms[0]


def sum_kernel(scalar_lane, count, tile_count, *refs):
    own_ref, got, refs = refs[0], refs[1 : 1 + count], refs[1 + count :]
    tiles, (out_ref, pay_ref) = refs[:tile_count], refs[tile_count:]
    body_rows = own_ref.shape[0] - TAIL

    def row(ref, n):
        return ref[pl.ds(body_rows + n, 1), :]

    scals = [row(own_ref, 1)] + [decode_row([row(ref, 1 + n) for n in range(4)]) for ref in got]
    scales = [1.0] + [lane_pick(scal, scalar_lane) * (1.0 / HALF_SPAN) for scal in scals[1:]]
    refs = (own_ref, *got)
    value = tree_sum([ref[pl.ds(0, body_rows), :] * x for ref, x in zip(refs, scales)])
    diag = tree_sum([row(ref, 0) * x for ref, x in zip(refs, scales)])
    scal = tree_sum(scals)
    if tile_count:
        every = tree_sum([ref[1:2, :] for ref in tiles])
    else:
        every = tree_sum(
            [row(own_ref, 2)] + [decode_row([row(ref, 5 + n) for n in range(4)]) for ref in got]
        )
    parts, every_parts = encode_row(scal), encode_row(every)
    scal, every = decode_row(parts), decode_row(every_parts)
    frob = lane_pick(scal, scalar_lane)
    scale = jnp.where(frob > TINY, HALF_SPAN / jnp.maximum(frob, TINY), 0.0)
    out_ref[pl.ds(0, body_rows), :] = value
    out_ref[pl.ds(body_rows, TAIL), :] = tail_rows([diag, scal, every])
    pay_ref[pl.ds(0, body_rows), :] = value * scale
    pay_ref[pl.ds(body_rows, TAIL), :] = tail_rows([diag * scale, *parts, *every_parts])


def newton_kernel(scalar_lane, lanes, pos_ref, own_ref, *refs):
    got, refs = refs[: SQUARE - 1], refs[SQUARE - 1 :]
    combs, (away_ref, stay_ref, poly_ref, piece_ref, diag_ref, gram_ref, start_ref) = (
        refs[:lanes],
        refs[lanes:],
    )
    quad = pos_ref[1]
    body_rows = own_ref.shape[0] - TAIL
    rows, columns = combs[0].shape
    scal = own_ref[pl.ds(body_rows + 1, 1), :]
    frob = lane_pick(scal, scalar_lane)
    inv = 1.0 / (jnp.sqrt(frob) + 1e-07)
    shared = (frob * inv) * inv * (1.0 / HALF_SPAN)
    for k in range(SQUARE):
        ref = own_ref if k == 0 else got[k - 1]
        value, diag = ref[pl.ds(0, body_rows), :], ref[pl.ds(body_rows, 1), :]
        if k == 0:
            value, diag = (value * inv) * inv, (diag * inv) * inv
        else:
            value, diag = value * shared, diag * shared
        piece_ref[quad ^ k] = value
        diag_ref[quad ^ k] = jnp.broadcast_to(diag, diag_ref.shape[1:])
    row_id = lax.broadcasted_iota(jnp.int32, (BLOCK, BLOCK), 0)
    col_id = lax.broadcasted_iota(jnp.int32, (BLOCK, BLOCK), 1)

    def place(i, j, value):
        gram_ref[pl.ds(i * BLOCK, BLOCK), pl.ds(j * BLOCK, BLOCK)] = value

    for p, entries in enumerate(block_plan(columns)):
        for n, (i, j) in enumerate(entries):
            value = piece_ref[p, pl.ds(n * BLOCK, BLOCK), :]
            flipped = value.T
            if i == j:
                diag = diag_ref[p][0:1]
                upper = jnp.where(row_id < col_id, value, jnp.where(row_id > col_id, flipped, diag))
                place(i, i, upper)
                place(i + 1, i + 1, jnp.where(row_id < col_id, flipped, value))
            else:
                place(i, j, value)
                place(j, i, flipped)

    def dot(x, y):
        return jnp.dot(x, y, preferred_element_type=F32)

    for kl in range(lanes):
        start_ref[pl.ds(kl * rows, rows), :] = (combs[kl][...] * inv).astype(jnp.bfloat16)
    gram = gram_ref[...]
    iterate = start_ref[...]
    for step in range(NS_ITERS):
        gram_low = gram.astype(jnp.bfloat16)
        square = dot(gram_low, gram_low)
        poly = (COEF_B * gram + COEF_C * square).astype(jnp.bfloat16)
        if step + 1 == NS_ITERS:
            away_ref[...] = newton_rows(iterate[rows:], poly)
            stay_ref[...] = iterate[:rows]
            poly_ref[...] = poly
            return
        iterate = newton_rows(iterate, poly)
        half = COEF_A * gram + dot(gram_low, poly)
        half_high = half.astype(jnp.bfloat16)
        half_low = (half - half_high.astype(F32)).astype(jnp.bfloat16)
        gram = COEF_A * half + dot(poly, half_high) + dot(poly, half_low)


def newton_rows(iterate, poly):
    moved = jnp.dot(iterate, poly, preferred_element_type=F32)
    return (COEF_A * iterate.astype(F32) + moved).astype(jnp.bfloat16)


def own_rows_kernel(stay_ref, poly_ref, out_ref):
    out_ref[...] = newton_rows(stay_ref[...], poly_ref[...])


def weight_kernel(domains, own_ref, *refs):
    got, (share_ref, onehot_ref, counts_ref, out_ref) = refs[:-4], refs[-4:]
    body_rows = own_ref.shape[0] - TAIL
    sums = tree_sum(
        [own_ref[pl.ds(body_rows + 2, 1), :]]
        + [decode_row([ref[pl.ds(body_rows + 5 + n, 1), :] for n in range(4)]) for ref in got]
    )
    norm = jnp.sqrt(lane_pick(sums, 2 * domains))
    score = jnp.zeros(share_ref.shape, F32)
    for g in range(domains):
        aligned, squares = lane_pick(sums, g), lane_pick(sums, domains + g)
        cosine = aligned / (jnp.sqrt(squares) * norm + 1e-06)
        score = score + onehot_ref[g : g + 1, :] * cosine
    score = score / jnp.maximum(counts_ref[...], 1.0)
    raised = share_ref[...] * jnp.exp(ETA * score)
    out_ref[...] = raised / jnp.sum(raised, axis=1, keepdims=True)


def call(kernel, out_shape, args, spaces, scratch=(), flops=0, grant=VMEM_GRANT):
    size = sum(math.prod(a.shape) * a.dtype.itemsize for a in (*args, *out_shape))
    return pl.pallas_call(
        kernel,
        out_shape=tuple(out_shape),
        in_specs=[pl.BlockSpec(memory_space=s) for s in spaces],
        out_specs=tuple(pl.BlockSpec(memory_space=pltpu.VMEM) for _ in out_shape),
        scratch_shapes=list(scratch),
        cost_estimate=pl.CostEstimate(flops=flops, bytes_accessed=size, transcendentals=0),
        compiler_params=pltpu.CompilerParams(vmem_limit_bytes=grant),
    )(*args)


def spread_order(members, lanes):
    return sorted(range(1, members), key=lambda k: k // lanes == 0)


def body(gradients, row_counts, domain_ids, domain_weights):
    domains = lax.axis_size("domain")
    shards = lax.axis_size("fsdp")
    matrices, rows, columns = gradients.shape[1:]
    lanes = matrices // domains
    sets = shards // lanes
    members = domains * lanes
    full_rows = rows * shards
    domain_pos = lax.axis_index("domain")
    shard_pos = lax.axis_index("fsdp")
    lane_pos = shard_pos % lanes
    set_pos = shard_pos // lanes
    member = domain_pos * lanes + lane_pos
    quad = set_pos % SQUARE
    flip = [(k // lanes) * shards + k % lanes for k in range(members)]

    def exchange(value, mask):
        return lax.ppermute(value, AXES, [(i, i ^ mask) for i in range(domains * shards)])

    vmem, smem, hbm = pltpu.VMEM, pltpu.SMEM, pltpu.HBM
    tile = jax.ShapeDtypeStruct((rows, columns), gradients.dtype)

    def fetch(wanted):
        index = jnp.stack([member ^ k for k in wanted]).astype(jnp.int32)
        return call(
            functools.partial(fetch_kernel, len(wanted)),
            [tile] * len(wanted),
            [index, gradients[0]],
            [smem, hbm],
            [pltpu.SemaphoreType.DMA((len(wanted),))],
        )

    if members <= 8:
        order = spread_order(members, lanes)
        ahead = lax.dynamic_index_in_dim(gradients[0], member ^ order[0], 0, keepdims=False)
        fetched = (ahead, *fetch(order[1:] + [0]))
        pieces = dict(zip(order + [0], fetched))
        got = {k: exchange(pieces[k], flip[k]) for k in order}
        got[0] = pieces[0]
        blocks = [got[k] for k in range(members)]
    else:
        teams = [
            [d * shards + s * lanes + l for d in range(domains) for l in range(lanes)]
            for s in range(sets)
        ]
        moved = lax.all_to_all(
            gradients[0], AXES, split_axis=0, concat_axis=0, axis_index_groups=teams, tiled=True
        )
        blocks = [
            lax.dynamic_index_in_dim(moved, member ^ k, 0, keepdims=False) for k in range(members)
        ]

    weight_share, onehot, counts, group_mix = group_mixing(
        domain_ids, domain_weights, domain_weights.shape[0]
    )
    mix = jnp.take(group_mix, domain_pos ^ jnp.arange(domains, dtype=jnp.int32))
    lane_row = (set_pos * lanes + (lane_pos ^ jnp.arange(lanes, dtype=jnp.int32))) * rows
    limits = lax.dynamic_index_in_dim(row_counts, member, 0, keepdims=False) - lane_row
    position = jnp.stack([domain_pos, quad, lane_pos]).astype(jnp.int32)

    per_piece = len(block_plan(columns)[0]) * BLOCK
    packed = per_piece + TAIL
    pieces_scratch = [
        pltpu.VMEM((SQUARE, per_piece, BLOCK), F32),
        pltpu.VMEM((SQUARE, 8, BLOCK), F32),
    ]
    square = jax.ShapeDtypeStruct((columns, columns), F32)
    combs, carried = [], []
    for kl in range(lanes):
        last = kl == lanes - 1
        results = [jax.ShapeDtypeStruct((rows, columns), F32)]
        if last:
            results += [
                jax.ShapeDtypeStruct((SQUARE - 1, packed, BLOCK), F32),
                jax.ShapeDtypeStruct((packed, BLOCK), F32),
            ]
        else:
            results += [square, jax.ShapeDtypeStruct((8, BLOCK), F32)]
        comb, *carried = call(
            functools.partial(gram_kernel, domains, kl, last),
            results,
            [mix, limits, position, *blocks[kl::lanes], *carried],
            [smem] * 3 + [vmem] * (domains + len(carried)),
            pieces_scratch if last else (),
            flops=2 * rows * columns * columns,
        )
        combs.append(comb)
    payload, own = carried
    scalar_lane = 2 * domains

    def add_up(own, got, tiles=()):
        return call(
            functools.partial(sum_kernel, scalar_lane, len(got), len(tiles)),
            [jax.ShapeDtypeStruct((packed, BLOCK), F32)] * 2,
            [own, *got, *tiles],
            [vmem] * (1 + len(got) + len(tiles)),
        )

    def half_width(value, mask):
        return exchange(value.astype(jnp.float16), mask).astype(F32)

    got = [half_width(payload[k - 1], k * lanes) for k in range(1, SQUARE)]
    tiles = [own[per_piece : per_piece + 8]]
    if members <= 8:
        tiles += [exchange(tiles[0], flip[k]) for k in range(1, members)]
    else:
        stride = 1
        while stride < members:
            tiles = [tiles[0] + exchange(tiles[0], flip[stride])]
            stride *= 2
    own, packet = add_up(own, got, tiles)
    stride = SQUARE * lanes
    while stride < shards:
        own, packet = add_up(own, [half_width(packet, stride)])
        stride *= 2
    got = [half_width(packet, k * lanes) for k in range(1, SQUARE)]

    away, stay, poly = call(
        functools.partial(newton_kernel, scalar_lane, lanes),
        [
            jax.ShapeDtypeStruct(((lanes - 1) * rows, columns), jnp.bfloat16),
            jax.ShapeDtypeStruct((rows, columns), jnp.bfloat16),
            jax.ShapeDtypeStruct((columns, columns), jnp.bfloat16),
        ],
        [position, own, *got, *combs],
        [smem] + [vmem] * (SQUARE + lanes),
        pieces_scratch
        + [pltpu.VMEM((columns, columns), F32), pltpu.VMEM((lanes * rows, columns), jnp.bfloat16)],
        flops=12 * 2 * columns**3,
    )
    away = away.reshape(lanes - 1, rows, columns)
    returned = [exchange(away[k - 1], k) for k in range(1, lanes)]
    (kept,) = call(
        own_rows_kernel,
        [jax.ShapeDtypeStruct((rows, columns), jnp.bfloat16)],
        [stay, poly],
        [vmem, vmem],
        flops=2 * rows * columns * columns,
    )
    (weights,) = call(
        functools.partial(weight_kernel, domains),
        [jax.ShapeDtypeStruct((1, weight_share.shape[0]), F32)],
        [own, *got, weight_share[None], onehot, counts[None]],
        [vmem] * (SQUARE + 3),
    )
    returned = [kept, *returned]
    if lanes == 2:
        first = lane_pos == 0
        ordered = [
            jnp.where(first, returned[0], returned[1]),
            jnp.where(first, returned[1], returned[0]),
        ]
    else:
        stacked = jnp.stack(returned)
        ordered = [
            lax.dynamic_index_in_dim(stacked, lane_pos ^ k, 0, keepdims=False)
            for k in range(lanes)
        ]
    updates = jnp.stack(ordered).astype(F32) * (MUON_SCALE * math.sqrt(full_rows))
    return (updates, weights[0])


def solution(mesh):
    placed = (P("domain", None, "fsdp", None), P(), P(), P())

    return jax.shard_map(
        body,
        mesh=mesh,
        in_specs=placed,
        out_specs=(P("domain", "fsdp", None), P()),
        check_vma=False,
    )
```

time: 50.5 us -> 47.1 us (0.933)
  waiting for transfers between devices: 14.4 us -> 11 us
  other arithmetic: 6.12 us -> 3.7 us
  Pallas kernels: 6.43 us -> 8.6 us
  local copies, waits for them, and re-layouts: 4.43 us -> 5.32 us
  between operations: 1.52 us -> 0.86 us
    ppermute x13 -> x14, waiting for transfers between devices: 14.4 us -> 11 us  [exchange(): lax.ppermute(value, AXES, [(i, i ^ mask) for i in range(domains * shards)])]
    pallas_call x4 -> x8, Pallas kernels: 6.43 us -> 8.6 us  [call(): pl.pallas_call(kernel, out_shape=tuple(out_shape), in_specs=[pl.BlockSpec...]
    div x3 -> x0, other arithmetic: 1.88 us -> none  [the longest x1 1.16 us: body(): return (updates, raised / jnp.sum(raised))]
    unnamed x6 -> x8, local copies, waits for them, and re-layouts: 1.24 us -> 3.08 us
    reduce_sum x2 -> x0, other arithmetic: 1.33 us -> none  [the longest x1 1.25 us: body(): return (updates, raised / jnp.sum(raised))]
    broadcast_in_dim x0 -> x1, other arithmetic: none -> 0.65 us  [body(): weight_share[None]]
    sub x0 -> x1, other arithmetic: none -> 0.65 us  [body(): lax.dynamic_index_in_dim(row_counts, member, 0, keepdims=False) - lane_row]
    slice x3 -> x1, local copies, waits for them, and re-layouts: 0.61 us -> 0.01 us  [body(): tiles = [own[per_piece:per_piece + 8]]]
  transfers between devices with their start and end apart: 13 -> 14, of which waited for: 8 -> 7; matrix products, arithmetic and copies ran while one was open for 13% -> 8% of each run, Pallas kernels for 0% -> 6%
where the time goes in v4:
time: 47.1 us; the launch traced here: 46.5 us
  starting transfers between devices  17 us (36%)
  waiting for transfers between devices  11 us (23%)
  Pallas kernels  8.6 us (18%)
  local copies, waits for them, and re-layouts  5.32 us (11%)
  other arithmetic  3.7 us (8%)
  between operations  0.86 us (2%)
    ppermute x14, starting transfers between devices, exchange(): lax.ppermute(value, AXES, [(i, i ^ mask) for i in range(domains * shards)])  17 us
    ppermute x14, waiting for transfers between devices, exchange(): lax.ppermute(value, AXES, [(i, i ^ mask) for i in range(domains * shards)])  11 us
    pallas_call x8, Pallas kernels, call(): pl.pallas_call(kernel, out_shape=tuple(out_shape), in_specs=[pl.BlockSpec...  8.6 us
    unnamed x8, local copies, waits for them, and re-layouts  3.08 us
    mul x1, other arithmetic, body(): jnp.stack(ordered).astype(F32) * (MUON_SCALE * math.sqrt(full_rows))  1.11 us
    squeeze x1, local copies, waits for them, and re-layouts, body(): lax.dynamic_index_in_dim(gradients[0], member ^ order[0], 0, keepdims=False)  0.97 us
  transfers between devices with their start and end apart: 14, of which 7 were waited for; matrix products, arithmetic and copies ran while one was open for 8% of the time, Pallas kernels for 6%

profile of v4, /device:TPU:1, one launch (start us, length us, event | category | flops | bytes accessed | tf_op | source)
XLA Modules:
  0.0 46.5 jit_solution(3667409036449639668)
XLA Ops:
  0.7 1.0 %dynamic-slice_bitcast_fusion = bf16[256,512]{1,0:T(8,128)(2,1)S(1)} fusion(bf16[1,4,256,512]{3,2,1,0:T(8,128)(2,1)} %param.4, s32[]{:T(128)S(6)} %select_n.63), kind=kLoop, calls=%fused_computation.4 | loop fusion | bytes 524292 | tf_op jit(solution)/shard_map/jit(dynamic_index_in_dim)/squeeze | solution.py:342
  1.6 2.1 %collective-permute-start.2 = (bf16[256,512]{1,0:T(8,128)(2,1)S(1)}, bf16[256,512]{1,0:T(8,128)(2,1)S(1)}, u32[]{:S(2)}, u32[]{:S(2)}) collective-permute-start(bf16[256,512]{1,0:T(8,128)(2,1)S(1)} %dynamic-slice_bitcast_fusion), channel_id=1, source_target_pairs={{0,16},{1,17},{2,18},{3,19},{4,20},{5,21},{6,22},{7,23},{8,24},{9,... | collective-permute-start | bytes 786440 | tf_op jit(solution)/shard_map/ppermute | solution.py:325
  3.8 1.2 %copy-done = bf16[1,4,256,512]{3,2,1,0:T(8,128)(2,1)S(1)} copy-done((bf16[1,4,256,512]{3,2,1,0:T(8,128)(2,1)S(1)}, bf16[1,4,256,512]{3,2,1,0:T(8,128)(2,1)}, u32[]{:S(2)}) %copy-start) | copy-done | bytes 1048600
  5.0 0.6 %shard_map.59 = (bf16[256,512]{1,0:T(8,128)(2,1)S(1)}, bf16[256,512]{1,0:T(8,128)(2,1)S(1)}, bf16[256,512]{1,0:T(8,128)(2,1)S(1)}) custom-call(s32[3]{0:T(128)S(1)} %pad_add_fusion.1.index_ref, bf16[4,256,512]{2,1,0:T(8,128)(2,1)S(1)} %bitcast.26), custom_call_target="tpu_custom_call" | custom-call | bytes 1835020 | tf_op jit(solution)/shard_map/pallas_call | solution.py:293
  5.7 1.0 %collective-permute-start = (bf16[256,512]{1,0:T(8,128)(2,1)S(1)}, bf16[256,512]{1,0:T(8,128)(2,1)S(1)}, u32[]{:S(2)}, u32[]{:S(2)}) collective-permute-start(bf16[256,512]{1,0:T(8,128)(2,1)S(1)} %get-tuple-element.18), channel_id=1, source_target_pairs={{0,1},{1,0},{2,3},{3,2},{4,5},{5,4},{6,7},{7,6},{8,9},{9,8},{10,11... | collective-permute-start | bytes 786440 | tf_op jit(solution)/shard_map/ppermute | solution.py:325
  6.7 0.6 %copy-done.3 = s32[2]{0:T(128)S(1)} copy-done((s32[2]{0:T(128)S(1)}, s32[2]{0:T(128)}, u32[]{:S(2)}) %copy-start.3) | copy-done | bytes 32
  8.0 0.6 %reduce_sum.27 = f32[]{:T(128)} reduce(f32[8]{0:T(128)S(1)} %copy-done.1, f32[]{:T(128)} %constant.72.clone.1), dimensions={0}, to_apply=%region_0.1 | reduce | flops 7 | bytes 40 | tf_op jit(solution)/shard_map/reduce_sum | solution.py:30
  8.6 0.7 %divide_bitcast_fusion = (f32[1,8]{1,0:T(1,128)S(1)}, f32[8]{0:T(128)S(1)}) fusion(f32[8]{0:T(128)S(1)} %copy-done.1, f32[]{:T(128)} %reduce_sum.27, f32[8]{0:T(128)S(1)} %fusion.2), kind=kLoop, calls=%fused_computation.18 | loop fusion | flops 32 | bytes 132 | tf_op jit(solution)/shard_map/broadcast_in_dim | solution.py:450
  9.5 0.6 %copy-done.2 = s32[4]{0:T(128)S(1)} copy-done((s32[4]{0:T(128)S(1)}, s32[4]{0:T(128)}, u32[]{:S(2)}) %copy-start.2) | copy-done | bytes 40
  10.1 0.6 %dynamic_slice.8 = s32[1]{0:T(128)} dynamic-slice(s32[4]{0:T(128)S(1)} %copy-done.2, s32[]{:T(128)S(6)} %select_n.62), dynamic_slice_sizes={1} | dynamic-slice | bytes 12 | tf_op jit(solution)/shard_map/jit(dynamic_index_in_dim)/dynamic_slice | solution.py:365
  10.7 0.7 %multiply_subtract_fusion.lim_ref = s32[2]{0:T(128)S(1)} fusion(s32[]{:T(128)} %select_n.55, s32[]{:T(128)S(6)} %mul.26, s32[]{:T(128)} %bitcast.4), kind=kLoop, calls=%fused_computation.19 | loop fusion | flops 8 | bytes 20 | tf_op jit(solution)/shard_map/sub | solution.py:365
  11.4 0.6 %gather_fusion = f32[2]{0:T(128)S(1)} fusion(f32[2]{0:T(128)S(1)} %select_reduce_fusion, s32[1024]{0:T(1024)S(1)} %pad_clamp_fusion), kind=kCustom, calls=%fused_computation | custom fusion | bytes 24 | tf_op jit(solution)/shard_map/jit(_take)/gather | solution.py:363
  12.1 1.1 %shard_map.60 = (f32[256,512]{1,0:T(8,128)S(1)}, f32[512,512]{1,0:T(8,128)S(1)}, f32[8,128]{1,0:T(8,128)S(1)}) custom-call(f32[2]{0:T(128)S(1)} %and_select_fusion.mix_ref, s32[2]{0:T(128)S(1)} %multiply_subtract_fusion.lim_ref, s32[3]{0:T(128)S(1)} %pad_add_fusion.pos_ref, bf16[256,512]{1,0:T(8,128)(2,1)S(1)} %get-tuple-element.20.refs_0_, ...), custom_call_target="tpu_custom_call" | custom-call | flops 134217728 | bytes 2101276 | tf_op jit(solution)/shard_map/pallas_call | solution.py:293
  13.2 2.7 %collective-permute-done.1.refs_1_ = bf16[256,512]{1,0:T(8,128)(2,1)S(1)} collective-permute-done((bf16[256,512]{1,0:T(8,128)(2,1)S(1)}, bf16[256,512]{1,0:T(8,128)(2,1)S(1)}, u32[]{:S(2)}, u32[]{:S(2)}) %collective-permute-start.1) | collective-permute-done | bytes 262176 | tf_op jit(solution)/shard_map/ppermute | solution.py:325
  15.9 1.1 %shard_map.61 = (f32[256,512]{1,0:T(8,128)S(1)}, f32[3,272,128]{2,1,0:T(8,128)S(1)}, f32[272,128]{1,0:T(8,128)S(1)}) custom-call(f32[2]{0:T(128)S(1)} %and_select_fusion.mix_ref, s32[2]{0:T(128)S(1)} %multiply_subtract_fusion.lim_ref, s32[3]{0:T(128)S(1)} %pad_add_fusion.pos_ref, bf16[256,512]{1,0:T(8,128)(2,1)S(1)} %collective-permute-done.refs_0_, ...), custom_call_target="tpu_custom_call" | custom-call | flops 134217728 | bytes 2658332 | tf_op jit(solution)/shard_map/pallas_call | solution.py:293
  17.2 1.6 %collective-permute-start.3 = (f16[272,128]{1,0:T(8,128)(2,1)S(1)}, f16[272,128]{1,0:T(8,128)(2,1)S(1)}, u32[]{:S(2)}, u32[]{:S(2)}) collective-permute-start(f16[272,128]{1,0:T(8,128)(2,1)S(1)} %get-tuple-element.38), channel_id=1, source_target_pairs={{0,2},{1,3},{2,0},{3,1},{4,6},{5,7},{6,4},{7,5},{8,10},{9,11},{10,... | collective-permute-start | bytes 208904 | tf_op jit(solution)/shard_map/ppermute | solution.py:325
  18.7 1.3 %collective-permute-start.4 = (f16[272,128]{1,0:T(8,128)(2,1)S(1)}, f16[272,128]{1,0:T(8,128)(2,1)S(1)}, u32[]{:S(2)}, u32[]{:S(2)}) collective-permute-start(f16[272,128]{1,0:T(8,128)(2,1)S(1)} %get-tuple-element.37), channel_id=1, source_target_pairs={{0,4},{1,5},{2,6},{3,7},{4,0},{5,1},{6,2},{7,3},{8,12},{9,13},{10,... | collective-permute-start | bytes 208904 | tf_op jit(solution)/shard_map/ppermute | solution.py:325
  20.0 0.6 %collective-permute-start.6 = (f32[8,128]{1,0:T(8,128)S(1)}, f32[8,128]{1,0:T(8,128)S(1)}, u32[]{:S(2)}, u32[]{:S(2)}) collective-permute-start(f32[8,128]{1,0:T(8,128)S(1)} %slice.18.refs_4_), channel_id=1, source_target_pairs={{0,1},{1,0},{2,3},{3,2},{4,5},{5,4},{6,7},{7,6},{8,9},{9,8},{10,11... | collective-permute-start | bytes 12296 | tf_op jit(solution)/shard_map/ppermute | solution.py:325
  20.7 1.1 %collective-permute-start.7 = (f32[8,128]{1,0:T(8,128)S(1)}, f32[8,128]{1,0:T(8,128)S(1)}, u32[]{:S(2)}, u32[]{:S(2)}) collective-permute-start(f32[8,128]{1,0:T(8,128)S(1)} %slice.18.refs_4_), channel_id=1, source_target_pairs={{0,16},{1,17},{2,18},{3,19},{4,20},{5,21},{6,22},{7,23},{8,24},{9,... | collective-permute-start | bytes 12296 | tf_op jit(solution)/shard_map/ppermute | solution.py:325
  21.7 1.4 %collective-permute-start.8 = (f32[8,128]{1,0:T(8,128)S(1)}, f32[8,128]{1,0:T(8,128)S(1)}, u32[]{:S(2)}, u32[]{:S(2)}) collective-permute-start(f32[8,128]{1,0:T(8,128)S(1)} %slice.18.refs_4_), channel_id=1, source_target_pairs={{0,17},{1,16},{2,19},{3,18},{4,21},{5,20},{6,23},{7,22},{8,25},{9,... | collective-permute-start | bytes 12296 | tf_op jit(solution)/shard_map/ppermute | solution.py:325
  23.2 1.2 %collective-permute-done.5 = f16[272,128]{1,0:T(8,128)(2,1)S(1)} collective-permute-done((f16[272,128]{1,0:T(8,128)(2,1)S(1)}, f16[272,128]{1,0:T(8,128)(2,1)S(1)}, u32[]{:S(2)}, u32[]{:S(2)}) %collective-permute-start.5) | collective-permute-done | bytes 69664 | tf_op jit(solution)/shard_map/ppermute | solution.py:325
  24.4 0.6 %collective-permute-done.8.refs_7_ = f32[8,128]{1,0:T(8,128)S(1)} collective-permute-done((f32[8,128]{1,0:T(8,128)S(1)}, f32[8,128]{1,0:T(8,128)S(1)}, u32[]{:S(2)}, u32[]{:S(2)}) %collective-permute-start.8) | collective-permute-done | bytes 4128 | tf_op jit(solution)/shard_map/ppermute | solution.py:325
  25.2 2.4 %collective-permute-start.9 = (f16[272,128]{1,0:T(8,128)(2,1)S(1)}, f16[272,128]{1,0:T(8,128)(2,1)S(1)}, u32[]{:S(2)}, u32[]{:S(2)}) collective-permute-start(f16[272,128]{1,0:T(8,128)(2,1)S(1)} %convert_element_type.54), channel_id=1, source_target_pairs={{0,8},{1,9},{2,10},{3,11},{4,12},{5,13},{6,14},{7,15},{8,0},{9,1},... | collective-permute-start | bytes 208904 | tf_op jit(solution)/shard_map/ppermute | solution.py:325
  27.6 1.8 %collective-permute-done.9 = f16[272,128]{1,0:T(8,128)(2,1)S(1)} collective-permute-done((f16[272,128]{1,0:T(8,128)(2,1)S(1)}, f16[272,128]{1,0:T(8,128)(2,1)S(1)}, u32[]{:S(2)}, u32[]{:S(2)}) %collective-permute-start.9) | collective-permute-done | bytes 69664 | tf_op jit(solution)/shard_map/ppermute | solution.py:325
  29.5 1.0 %collective-permute-start.10 = (f16[272,128]{1,0:T(8,128)(2,1)S(1)}, f16[272,128]{1,0:T(8,128)(2,1)S(1)}, u32[]{:S(2)}, u32[]{:S(2)}) collective-permute-start(f16[272,128]{1,0:T(8,128)(2,1)S(1)} %convert_element_type.56), channel_id=1, source_target_pairs={{0,2},{1,3},{2,0},{3,1},{4,6},{5,7},{6,4},{7,5},{8,10},{9,11},{10,... | collective-permute-start | bytes 208904 | tf_op jit(solution)/shard_map/ppermute | solution.py:325
  30.5 2.8 %collective-permute-start.11 = (f16[272,128]{1,0:T(8,128)(2,1)S(1)}, f16[272,128]{1,0:T(8,128)(2,1)S(1)}, u32[]{:S(2)}, u32[]{:S(2)}) collective-permute-start(f16[272,128]{1,0:T(8,128)(2,1)S(1)} %convert_element_type.56), channel_id=1, source_target_pairs={{0,4},{1,5},{2,6},{3,7},{4,0},{5,1},{6,2},{7,3},{8,12},{9,13},{10,... | collective-permute-start | bytes 208904 | tf_op jit(solution)/shard_map/ppermute | solution.py:325
  33.4 1.7 %collective-permute-done.11 = f16[272,128]{1,0:T(8,128)(2,1)S(1)} collective-permute-done((f16[272,128]{1,0:T(8,128)(2,1)S(1)}, f16[272,128]{1,0:T(8,128)(2,1)S(1)}, u32[]{:S(2)}, u32[]{:S(2)}) %collective-permute-start.11) | collective-permute-done | bytes 69664 | tf_op jit(solution)/shard_map/ppermute | solution.py:325
  35.1 2.9 %collective-permute-done.12 = f16[272,128]{1,0:T(8,128)(2,1)S(1)} collective-permute-done((f16[272,128]{1,0:T(8,128)(2,1)S(1)}, f16[272,128]{1,0:T(8,128)(2,1)S(1)}, u32[]{:S(2)}, u32[]{:S(2)}) %collective-permute-start.12) | collective-permute-done | bytes 69664 | tf_op jit(solution)/shard_map/ppermute | solution.py:325
  38.0 4.4 %shard_map.64 = (bf16[256,512]{1,0:T(8,128)(2,1)S(1)}, bf16[256,512]{1,0:T(8,128)(2,1)S(1)}, bf16[512,512]{1,0:T(8,128)(2,1)S(1)}) custom-call(s32[3]{0:T(128)S(1)} %pad_add_fusion.pos_ref, f32[272,128]{1,0:T(8,128)S(1)} %get-tuple-element.27.own_ref, f32[272,128]{1,0:T(8,128)S(1)} %convert_element_type.57.refs_0_, ...), custom_call_target="tpu_custom_call" | custom-call | flops 3221225472 | bytes 2654220 | tf_op jit(solution)/shard_map/pallas_call | solution.py:293
  42.5 1.7 %collective-permute-start.13 = (bf16[256,512]{1,0:T(8,128)(2,1)S(1)}, bf16[256,512]{1,0:T(8,128)(2,1)S(1)}, u32[]{:S(2)}, u32[]{:S(2)}) collective-permute-start(bf16[256,512]{1,0:T(8,128)(2,1)S(1)} %get-tuple-element.33), channel_id=1, source_target_pairs={{0,1},{1,0},{2,3},{3,2},{4,5},{5,4},{6,7},{7,6},{8,9},{9,8},{10,11... | collective-permute-start | bytes 786440 | tf_op jit(solution)/shard_map/ppermute | solution.py:325
  44.2 0.7 %shard_map.66 = f32[1,8]{1,0:T(1,128)} custom-call(f32[272,128]{1,0:T(8,128)S(1)} %get-tuple-element.27.own_ref, f32[272,128]{1,0:T(8,128)S(1)} %convert_element_type.57.refs_0_, f32[272,128]{1,0:T(8,128)S(1)} %convert_element_type.58.refs_1_, f32[272,128]{1,0:T(8,128)S(1)} %convert_element_type.59.refs_2_, f32[1,8]{1,0:T(1,128)S(1)} %get-tuple-element.39.refs_3_, ...), custom_call_target="tpu_custom_call" | custom-call | bytes 557216 | tf_op jit(solution)/shard_map/pallas_call | solution.py:293
  45.4 1.1 %convert_multiply_fusion = f32[2,256,512]{2,1,0:T(8,128)} fusion(bf16[1,256,512]{2,1,0:T(8,128)(2,1)S(1)} %get-tuple-element.35, bf16[1,256,512]{2,1,0:T(8,128)(2,1)S(1)} %get-tuple-element.34), kind=kLoop, calls=%fused_computation.1 | loop fusion | flops 786432 | bytes 1572864 | tf_op jit(solution)/shard_map/mul | solution.py:466
  (40 shorter events, 2.0 us)
Async XLA Ops:
  1.6 10.5 %collective-permute-start.2 = (bf16[256,512]{1,0:T(8,128)(2,1)S(1)}, bf16[256,512]{1,0:T(8,128)(2,1)S(1)}, u32[]{:S(2)}, u32[]{:S(2)}) collective-permute-start(bf16[256,512]{1,0:T(8,128)(2,1)S(1)} %dynamic-slice_bitcast_fusion), channel_id=1, source_target_pairs={{0,16},{1,17},{2,18},{3,19},{4,20},{5,21},{6,22},{7,23},{8,24},{9,... | collective-permute-start | bytes 786440 | tf_op jit(solution)/shard_map/ppermute | solution.py:325
  3.8 1.2 %copy-start = (bf16[1,4,256,512]{3,2,1,0:T(8,128)(2,1)S(1)}, bf16[1,4,256,512]{3,2,1,0:T(8,128)(2,1)}, u32[]{:S(2)}) copy-start(bf16[1,4,256,512]{3,2,1,0:T(8,128)(2,1)} %param.4) | copy-start | bytes 3145732
  5.7 7.5 %collective-permute-start = (bf16[256,512]{1,0:T(8,128)(2,1)S(1)}, bf16[256,512]{1,0:T(8,128)(2,1)S(1)}, u32[]{:S(2)}, u32[]{:S(2)}) collective-permute-start(bf16[256,512]{1,0:T(8,128)(2,1)S(1)} %get-tuple-element.18), channel_id=1, source_target_pairs={{0,1},{1,0},{2,3},{3,2},{4,5},{5,4},{6,7},{7,6},{8,9},{9,8},{10,11... | collective-permute-start | bytes 786440 | tf_op jit(solution)/shard_map/ppermute | solution.py:325
  6.7 9.2 %collective-permute-start.1 = (bf16[256,512]{1,0:T(8,128)(2,1)S(1)}, bf16[256,512]{1,0:T(8,128)(2,1)S(1)}, u32[]{:S(2)}, u32[]{:S(2)}) collective-permute-start(bf16[256,512]{1,0:T(8,128)(2,1)S(1)} %get-tuple-element.19), channel_id=1, source_target_pairs={{0,17},{1,16},{2,19},{3,18},{4,21},{5,20},{6,23},{7,22},{8,25},{9,... | collective-permute-start | bytes 786440 | tf_op jit(solution)/shard_map/ppermute | solution.py:325
  6.7 0.7 %copy-start.3 = (s32[2]{0:T(128)S(1)}, s32[2]{0:T(128)}, u32[]{:S(2)}) copy-start(s32[2]{0:T(128)} %param.6) | copy-start | bytes 28
  7.3 0.7 %copy-start.1 = (f32[8]{0:T(128)S(1)}, f32[8]{0:T(128)}, u32[]{:S(2)}) copy-start(f32[8]{0:T(128)} %param.7) | copy-start | bytes 100
  9.4 0.7 %copy-start.2 = (s32[4]{0:T(128)S(1)}, s32[4]{0:T(128)}, u32[]{:S(2)}) copy-start(s32[4]{0:T(128)} %param.5) | copy-start | bytes 52
  17.2 4.6 %collective-permute-start.3 = (f16[272,128]{1,0:T(8,128)(2,1)S(1)}, f16[272,128]{1,0:T(8,128)(2,1)S(1)}, u32[]{:S(2)}, u32[]{:S(2)}) collective-permute-start(f16[272,128]{1,0:T(8,128)(2,1)S(1)} %get-tuple-element.38), channel_id=1, source_target_pairs={{0,2},{1,3},{2,0},{3,1},{4,6},{5,7},{6,4},{7,5},{8,10},{9,11},{10,... | collective-permute-start | bytes 208904 | tf_op jit(solution)/shard_map/ppermute | solution.py:325
  18.7 4.5 %collective-permute-start.4 = (f16[272,128]{1,0:T(8,128)(2,1)S(1)}, f16[272,128]{1,0:T(8,128)(2,1)S(1)}, u32[]{:S(2)}, u32[]{:S(2)}) collective-permute-start(f16[272,128]{1,0:T(8,128)(2,1)S(1)} %get-tuple-element.37), channel_id=1, source_target_pairs={{0,4},{1,5},{2,6},{3,7},{4,0},{5,1},{6,2},{7,3},{8,12},{9,13},{10,... | collective-permute-start | bytes 208904 | tf_op jit(solution)/shard_map/ppermute | solution.py:325
  20.0 4.4 %collective-permute-start.5 = (f16[272,128]{1,0:T(8,128)(2,1)S(1)}, f16[272,128]{1,0:T(8,128)(2,1)S(1)}, u32[]{:S(2)}, u32[]{:S(2)}) collective-permute-start(f16[272,128]{1,0:T(8,128)(2,1)S(1)} %get-tuple-element.36), channel_id=1, source_target_pairs={{0,6},{1,7},{2,4},{3,5},{4,2},{5,3},{6,0},{7,1},{8,14},{9,15},{10,... | collective-permute-start | bytes 208904 | tf_op jit(solution)/shard_map/ppermute | solution.py:325
  20.0 4.4 %collective-permute-start.6 = (f32[8,128]{1,0:T(8,128)S(1)}, f32[8,128]{1,0:T(8,128)S(1)}, u32[]{:S(2)}, u32[]{:S(2)}) collective-permute-start(f32[8,128]{1,0:T(8,128)S(1)} %slice.18.refs_4_), channel_id=1, source_target_pairs={{0,1},{1,0},{2,3},{3,2},{4,5},{5,4},{6,7},{7,6},{8,9},{9,8},{10,11... | collective-permute-start | bytes 12296 | tf_op jit(solution)/shard_map/ppermute | solution.py:325
  20.7 3.8 %collective-permute-start.7 = (f32[8,128]{1,0:T(8,128)S(1)}, f32[8,128]{1,0:T(8,128)S(1)}, u32[]{:S(2)}, u32[]{:S(2)}) collective-permute-start(f32[8,128]{1,0:T(8,128)S(1)} %slice.18.refs_4_), channel_id=1, source_target_pairs={{0,16},{1,17},{2,18},{3,19},{4,20},{5,21},{6,22},{7,23},{8,24},{9,... | collective-permute-start | bytes 12296 | tf_op jit(solution)/shard_map/ppermute | solution.py:325
  21.7 3.3 %collective-permute-start.8 = (f32[8,128]{1,0:T(8,128)S(1)}, f32[8,128]{1,0:T(8,128)S(1)}, u32[]{:S(2)}, u32[]{:S(2)}) collective-permute-start(f32[8,128]{1,0:T(8,128)S(1)} %slice.18.refs_4_), channel_id=1, source_target_pairs={{0,17},{1,16},{2,19},{3,18},{4,21},{5,20},{6,23},{7,22},{8,25},{9,... | collective-permute-start | bytes 12296 | tf_op jit(solution)/shard_map/ppermute | solution.py:325
  25.2 4.1 %collective-permute-start.9 = (f16[272,128]{1,0:T(8,128)(2,1)S(1)}, f16[272,128]{1,0:T(8,128)(2,1)S(1)}, u32[]{:S(2)}, u32[]{:S(2)}) collective-permute-start(f16[272,128]{1,0:T(8,128)(2,1)S(1)} %convert_element_type.54), channel_id=1, source_target_pairs={{0,8},{1,9},{2,10},{3,11},{4,12},{5,13},{6,14},{7,15},{8,0},{9,1},... | collective-permute-start | bytes 208904 | tf_op jit(solution)/shard_map/ppermute | solution.py:325
  29.5 3.8 %collective-permute-start.10 = (f16[272,128]{1,0:T(8,128)(2,1)S(1)}, f16[272,128]{1,0:T(8,128)(2,1)S(1)}, u32[]{:S(2)}, u32[]{:S(2)}) collective-permute-start(f16[272,128]{1,0:T(8,128)(2,1)S(1)} %convert_element_type.56), channel_id=1, source_target_pairs={{0,2},{1,3},{2,0},{3,1},{4,6},{5,7},{6,4},{7,5},{8,10},{9,11},{10,... | collective-permute-start | bytes 208904 | tf_op jit(solution)/shard_map/ppermute | solution.py:325
  30.5 4.5 %collective-permute-start.11 = (f16[272,128]{1,0:T(8,128)(2,1)S(1)}, f16[272,128]{1,0:T(8,128)(2,1)S(1)}, u32[]{:S(2)}, u32[]{:S(2)}) collective-permute-start(f16[272,128]{1,0:T(8,128)(2,1)S(1)} %convert_element_type.56), channel_id=1, source_target_pairs={{0,4},{1,5},{2,6},{3,7},{4,0},{5,1},{6,2},{7,3},{8,12},{9,13},{10,... | collective-permute-start | bytes 208904 | tf_op jit(solution)/shard_map/ppermute | solution.py:325
  33.4 4.6 %collective-permute-start.12 = (f16[272,128]{1,0:T(8,128)(2,1)S(1)}, f16[272,128]{1,0:T(8,128)(2,1)S(1)}, u32[]{:S(2)}, u32[]{:S(2)}) collective-permute-start(f16[272,128]{1,0:T(8,128)(2,1)S(1)} %convert_element_type.56), channel_id=1, source_target_pairs={{0,6},{1,7},{2,4},{3,5},{4,2},{5,3},{6,0},{7,1},{8,14},{9,15},{10,... | collective-permute-start | bytes 208904 | tf_op jit(solution)/shard_map/ppermute | solution.py:325
  42.5 2.9 %collective-permute-start.13 = (bf16[256,512]{1,0:T(8,128)(2,1)S(1)}, bf16[256,512]{1,0:T(8,128)(2,1)S(1)}, u32[]{:S(2)}, u32[]{:S(2)}) collective-permute-start(bf16[256,512]{1,0:T(8,128)(2,1)S(1)} %get-tuple-element.33), channel_id=1, source_target_pairs={{0,1},{1,0},{2,3},{3,2},{4,5},{5,4},{6,7},{7,6},{8,9},{9,8},{10,11... | collective-permute-start | bytes 786440 | tf_op jit(solution)/shard_map/ppermute | solution.py:325

commit v5 on v4

--- a/solution.py
+++ b/solution.py
@@ -270,13 +270,19 @@
     out_ref[...] = newton_rows(stay_ref[...], poly_ref[...])
 
 
-def weight_kernel(domains, own_ref, *refs):
-    got, (share_ref, onehot_ref, counts_ref, out_ref) = refs[:-4], refs[-4:]
+def every_kernel(own_ref, *refs):
+    got, out_ref = refs[:-1], refs[-1]
     body_rows = own_ref.shape[0] - TAIL
     sums = tree_sum(
         [own_ref[pl.ds(body_rows + 2, 1), :]]
         + [decode_row([ref[pl.ds(body_rows + 5 + n, 1), :] for n in range(4)]) for ref in got]
     )
+    out_ref[...] = jnp.broadcast_to(sums, out_ref.shape)
+
+
+def weight_kernel(domains, *refs):
+    tiles, (share_ref, onehot_ref, counts_ref, out_ref) = refs[:-4], refs[-4:]
+    sums = tree_sum([ref[0:1, :] for ref in tiles])
     norm = jnp.sqrt(lane_pick(sums, 2 * domains))
     score = jnp.zeros(share_ref.shape, F32)
     for g in range(domains):
@@ -408,12 +414,12 @@
 
     got = [half_width(payload[k - 1], k * lanes) for k in range(1, SQUARE)]
     tiles = [own[per_piece : per_piece + 8]]
-    if members <= 8:
-        tiles += [exchange(tiles[0], flip[k]) for k in range(1, members)]
+    if domains <= 4:
+        tiles += [exchange(tiles[0], kd * shards) for kd in range(1, domains)]
     else:
         stride = 1
-        while stride < members:
-            tiles = [tiles[0] + exchange(tiles[0], flip[stride])]
+        while stride < domains:
+            tiles = [tiles[0] + exchange(tiles[0], stride * shards)]
             stride *= 2
     own, packet = add_up(own, got, tiles)
     stride = SQUARE * lanes
@@ -421,6 +427,15 @@
         own, packet = add_up(own, [half_width(packet, stride)])
         stride *= 2
     got = [half_width(packet, k * lanes) for k in range(1, SQUARE)]
+
+    (every,) = call(
+        every_kernel, [jax.ShapeDtypeStruct((8, BLOCK), F32)], [own, *got], [vmem] * SQUARE
+    )
+    tiles, stride = [every], 1
+    while stride < lanes:
+        every = tree_sum(tiles)
+        tiles = [every, exchange(every, stride)]
+        stride *= 2
 
     away, stay, poly = call(
         functools.partial(newton_kernel, scalar_lane, lanes),
@@ -447,8 +462,8 @@
     (weights,) = call(
         functools.partial(weight_kernel, domains),
         [jax.ShapeDtypeStruct((1, weight_share.shape[0]), F32)],
-        [own, *got, weight_share[None], onehot, counts[None]],
-        [vmem] * (SQUARE + 3),
+        [*tiles, weight_share[None], onehot, counts[None]],
+        [vmem] * (len(tiles) + 3),
     )
     returned = [kept, *returned]
     if lanes == 2:

time: 47.1 us -> 47 us (level)
  waiting for transfers between devices: 11 us -> 12 us
  starting transfers between devices: 17 us -> 16.2 us
    ppermute x14 -> x13, waiting for transfers between devices: 11 us -> 12 us  [exchange(): lax.ppermute(value, AXES, [(i, i ^ mask) for i in range(domains * shards)])]
    ppermute x14 -> x13, starting transfers between devices: 17 us -> 16.2 us  [exchange(): lax.ppermute(value, AXES, [(i, i ^ mask) for i in range(domains * shards)])]
    pallas_call x8 -> x9, Pallas kernels: 8.6 us -> 8.6 us  [call(): pl.pallas_call(kernel, out_shape=tuple(out_shape), in_specs=[pl.BlockSpec...]
  transfers between devices with their start and end apart: 14 -> 13, of which waited for: 7 -> 8; matrix products, arithmetic and copies ran while one was open for 8% -> 8% of each run, Pallas kernels for 6% -> 6%
where the time goes in v5:
time: 47 us; the launch traced here: 46.6 us
  starting transfers between devices  16.2 us (34%)
  waiting for transfers between devices  12 us (26%)
  Pallas kernels  8.6 us (18%)
  local copies, waits for them, and re-layouts  5.32 us (11%)
  other arithmetic  3.7 us (8%)
  between operations  0.85 us (2%)
    ppermute x13, starting transfers between devices, exchange(): lax.ppermute(value, AXES, [(i, i ^ mask) for i in range(domains * shards)])  16.2 us
    ppermute x13, waiting for transfers between devices, exchange(): lax.ppermute(value, AXES, [(i, i ^ mask) for i in range(domains * shards)])  12 us
    pallas_call x9, Pallas kernels, call(): pl.pallas_call(kernel, out_shape=tuple(out_shape), in_specs=[pl.BlockSpec...  8.6 us
    unnamed x8, local copies, waits for them, and re-layouts  3.08 us
    mul x1, other arithmetic, body(): jnp.stack(ordered).astype(F32) * (MUON_SCALE * math.sqrt(full_rows))  1.11 us
    squeeze x1, local copies, waits for them, and re-layouts, body(): lax.dynamic_index_in_dim(gradients[0], member ^ order[0], 0, keepdims=False)  0.97 us
  transfers between devices with their start and end apart: 13, of which 8 were waited for; matrix products, arithmetic and copies ran while one was open for 8% of the time, Pallas kernels for 6%

profile of v5, /device:TPU:1, one launch (start us, length us, event | category | flops | bytes accessed | tf_op | source)
XLA Modules:
  0.0 46.6 jit_solution(17249798377401392639)
XLA Ops:
  0.7 1.0 %dynamic-slice_bitcast_fusion = bf16[256,512]{1,0:T(8,128)(2,1)S(1)} fusion(bf16[1,4,256,512]{3,2,1,0:T(8,128)(2,1)} %param.4, s32[]{:T(128)S(6)} %select_n.63), kind=kLoop, calls=%fused_computation.4 | loop fusion | bytes 524292 | tf_op jit(solution)/shard_map/jit(dynamic_index_in_dim)/squeeze | solution.py:348
  1.6 2.1 %collective-permute-start.2 = (bf16[256,512]{1,0:T(8,128)(2,1)S(1)}, bf16[256,512]{1,0:T(8,128)(2,1)S(1)}, u32[]{:S(2)}, u32[]{:S(2)}) collective-permute-start(bf16[256,512]{1,0:T(8,128)(2,1)S(1)} %dynamic-slice_bitcast_fusion), channel_id=1, source_target_pairs={{0,16},{1,17},{2,18},{3,19},{4,20},{5,21},{6,22},{7,23},{8,24},{9,... | collective-permute-start | bytes 786440 | tf_op jit(solution)/shard_map/ppermute | solution.py:331
  3.8 1.2 %copy-done = bf16[1,4,256,512]{3,2,1,0:T(8,128)(2,1)S(1)} copy-done((bf16[1,4,256,512]{3,2,1,0:T(8,128)(2,1)S(1)}, bf16[1,4,256,512]{3,2,1,0:T(8,128)(2,1)}, u32[]{:S(2)}) %copy-start) | copy-done | bytes 1048600
  5.0 0.6 %shard_map.59 = (bf16[256,512]{1,0:T(8,128)(2,1)S(1)}, bf16[256,512]{1,0:T(8,128)(2,1)S(1)}, bf16[256,512]{1,0:T(8,128)(2,1)S(1)}) custom-call(s32[3]{0:T(128)S(1)} %pad_add_fusion.1.index_ref, bf16[4,256,512]{2,1,0:T(8,128)(2,1)S(1)} %bitcast.26), custom_call_target="tpu_custom_call" | custom-call | bytes 1835020 | tf_op jit(solution)/shard_map/pallas_call | solution.py:299
  5.7 1.0 %collective-permute-start = (bf16[256,512]{1,0:T(8,128)(2,1)S(1)}, bf16[256,512]{1,0:T(8,128)(2,1)S(1)}, u32[]{:S(2)}, u32[]{:S(2)}) collective-permute-start(bf16[256,512]{1,0:T(8,128)(2,1)S(1)} %get-tuple-element.18), channel_id=1, source_target_pairs={{0,1},{1,0},{2,3},{3,2},{4,5},{5,4},{6,7},{7,6},{8,9},{9,8},{10,11... | collective-permute-start | bytes 786440 | tf_op jit(solution)/shard_map/ppermute | solution.py:331
  6.7 0.6 %copy-done.3 = s32[2]{0:T(128)S(1)} copy-done((s32[2]{0:T(128)S(1)}, s32[2]{0:T(128)}, u32[]{:S(2)}) %copy-start.3) | copy-done | bytes 32
  7.4 0.6 %copy-done.1 = f32[8]{0:T(128)S(1)} copy-done((f32[8]{0:T(128)S(1)}, f32[8]{0:T(128)}, u32[]{:S(2)}) %copy-start.1) | copy-done | bytes 56
  8.0 0.6 %reduce_sum.27 = f32[]{:T(128)} reduce(f32[8]{0:T(128)S(1)} %copy-done.1, f32[]{:T(128)} %constant.72.clone.1), dimensions={0}, to_apply=%region_0.1 | reduce | flops 7 | bytes 40 | tf_op jit(solution)/shard_map/reduce_sum | solution.py:30
  8.6 0.7 %divide_bitcast_fusion = (f32[1,8]{1,0:T(1,128)S(1)}, f32[8]{0:T(128)S(1)}) fusion(f32[8]{0:T(128)S(1)} %copy-done.1, f32[]{:T(128)} %reduce_sum.27, f32[8]{0:T(128)S(1)} %fusion.2), kind=kLoop, calls=%fused_computation.18 | loop fusion | flops 32 | bytes 132 | tf_op jit(solution)/shard_map/broadcast_in_dim | solution.py:465
  9.5 0.6 %copy-done.2 = s32[4]{0:T(128)S(1)} copy-done((s32[4]{0:T(128)S(1)}, s32[4]{0:T(128)}, u32[]{:S(2)}) %copy-start.2) | copy-done | bytes 40
  10.1 0.6 %dynamic_slice.8 = s32[1]{0:T(128)} dynamic-slice(s32[4]{0:T(128)S(1)} %copy-done.2, s32[]{:T(128)S(6)} %select_n.62), dynamic_slice_sizes={1} | dynamic-slice | bytes 12 | tf_op jit(solution)/shard_map/jit(dynamic_index_in_dim)/dynamic_slice | solution.py:371
  10.7 0.7 %multiply_subtract_fusion.lim_ref = s32[2]{0:T(128)S(1)} fusion(s32[]{:T(128)} %select_n.55, s32[]{:T(128)S(6)} %mul.26, s32[]{:T(128)} %bitcast.4), kind=kLoop, calls=%fused_computation.19 | loop fusion | flops 8 | bytes 20 | tf_op jit(solution)/shard_map/sub | solution.py:371
  11.4 0.6 %gather_fusion = f32[2]{0:T(128)S(1)} fusion(f32[2]{0:T(128)S(1)} %select_reduce_fusion, s32[1024]{0:T(1024)S(1)} %pad_clamp_fusion), kind=kCustom, calls=%fused_computation | custom fusion | bytes 24 | tf_op jit(solution)/shard_map/jit(_take)/gather | solution.py:369
  12.1 1.1 %shard_map.60 = (f32[256,512]{1,0:T(8,128)S(1)}, f32[512,512]{1,0:T(8,128)S(1)}, f32[8,128]{1,0:T(8,128)S(1)}) custom-call(f32[2]{0:T(128)S(1)} %and_select_fusion.mix_ref, s32[2]{0:T(128)S(1)} %multiply_subtract_fusion.lim_ref, s32[3]{0:T(128)S(1)} %pad_add_fusion.pos_ref, bf16[256,512]{1,0:T(8,128)(2,1)S(1)} %get-tuple-element.20.refs_0_, ...), custom_call_target="tpu_custom_call" | custom-call | flops 134217728 | bytes 2101276 | tf_op jit(solution)/shard_map/pallas_call | solution.py:299
  13.2 2.7 %collective-permute-done.1.refs_1_ = bf16[256,512]{1,0:T(8,128)(2,1)S(1)} collective-permute-done((bf16[256,512]{1,0:T(8,128)(2,1)S(1)}, bf16[256,512]{1,0:T(8,128)(2,1)S(1)}, u32[]{:S(2)}, u32[]{:S(2)}) %collective-permute-start.1) | collective-permute-done | bytes 262176 | tf_op jit(solution)/shard_map/ppermute | solution.py:331
  15.9 1.1 %shard_map.61 = (f32[256,512]{1,0:T(8,128)S(1)}, f32[3,272,128]{2,1,0:T(8,128)S(1)}, f32[272,128]{1,0:T(8,128)S(1)}) custom-call(f32[2]{0:T(128)S(1)} %and_select_fusion.mix_ref, s32[2]{0:T(128)S(1)} %multiply_subtract_fusion.lim_ref, s32[3]{0:T(128)S(1)} %pad_add_fusion.pos_ref, bf16[256,512]{1,0:T(8,128)(2,1)S(1)} %collective-permute-done.refs_0_, ...), custom_call_target="tpu_custom_call" | custom-call | flops 134217728 | bytes 2658332 | tf_op jit(solution)/shard_map/pallas_call | solution.py:299
  17.2 1.6 %collective-permute-start.3 = (f16[272,128]{1,0:T(8,128)(2,1)S(1)}, f16[272,128]{1,0:T(8,128)(2,1)S(1)}, u32[]{:S(2)}, u32[]{:S(2)}) collective-permute-start(f16[272,128]{1,0:T(8,128)(2,1)S(1)} %get-tuple-element.38), channel_id=1, source_target_pairs={{0,2},{1,3},{2,0},{3,1},{4,6},{5,7},{6,4},{7,5},{8,10},{9,11},{10,... | collective-permute-start | bytes 208904 | tf_op jit(solution)/shard_map/ppermute | solution.py:331
  18.7 1.3 %collective-permute-start.4 = (f16[272,128]{1,0:T(8,128)(2,1)S(1)}, f16[272,128]{1,0:T(8,128)(2,1)S(1)}, u32[]{:S(2)}, u32[]{:S(2)}) collective-permute-start(f16[272,128]{1,0:T(8,128)(2,1)S(1)} %get-tuple-element.37), channel_id=1, source_target_pairs={{0,4},{1,5},{2,6},{3,7},{4,0},{5,1},{6,2},{7,3},{8,12},{9,13},{10,... | collective-permute-start | bytes 208904 | tf_op jit(solution)/shard_map/ppermute | solution.py:331
  20.0 1.3 %collective-permute-start.6 = (f32[8,128]{1,0:T(8,128)S(1)}, f32[8,128]{1,0:T(8,128)S(1)}, u32[]{:S(2)}, u32[]{:S(2)}) collective-permute-start(f32[8,128]{1,0:T(8,128)S(1)} %slice.18.refs_4_), channel_id=1, source_target_pairs={{0,16},{1,17},{2,18},{3,19},{4,20},{5,21},{6,22},{7,23},{8,24},{9,... | collective-permute-start | bytes 12296 | tf_op jit(solution)/shard_map/ppermute | solution.py:331
  21.3 1.1 %collective-permute-done.4 = f16[272,128]{1,0:T(8,128)(2,1)S(1)} collective-permute-done((f16[272,128]{1,0:T(8,128)(2,1)S(1)}, f16[272,128]{1,0:T(8,128)(2,1)S(1)}, u32[]{:S(2)}, u32[]{:S(2)}) %collective-permute-start.4) | collective-permute-done | bytes 69664 | tf_op jit(solution)/shard_map/ppermute | solution.py:331
  22.5 1.9 %collective-permute-done.5 = f16[272,128]{1,0:T(8,128)(2,1)S(1)} collective-permute-done((f16[272,128]{1,0:T(8,128)(2,1)S(1)}, f16[272,128]{1,0:T(8,128)(2,1)S(1)}, u32[]{:S(2)}, u32[]{:S(2)}) %collective-permute-start.5) | collective-permute-done | bytes 69664 | tf_op jit(solution)/shard_map/ppermute | solution.py:331
  24.6 2.4 %collective-permute-start.7 = (f16[272,128]{1,0:T(8,128)(2,1)S(1)}, f16[272,128]{1,0:T(8,128)(2,1)S(1)}, u32[]{:S(2)}, u32[]{:S(2)}) collective-permute-start(f16[272,128]{1,0:T(8,128)(2,1)S(1)} %convert_element_type.54), channel_id=1, source_target_pairs={{0,8},{1,9},{2,10},{3,11},{4,12},{5,13},{6,14},{7,15},{8,0},{9,1},... | collective-permute-start | bytes 208904 | tf_op jit(solution)/shard_map/ppermute | solution.py:331
  27.0 2.5 %collective-permute-done.7 = f16[272,128]{1,0:T(8,128)(2,1)S(1)} collective-permute-done((f16[272,128]{1,0:T(8,128)(2,1)S(1)}, f16[272,128]{1,0:T(8,128)(2,1)S(1)}, u32[]{:S(2)}, u32[]{:S(2)}) %collective-permute-start.7) | collective-permute-done | bytes 69664 | tf_op jit(solution)/shard_map/ppermute | solution.py:331
  29.7 1.4 %collective-permute-start.9 = (f16[272,128]{1,0:T(8,128)(2,1)S(1)}, f16[272,128]{1,0:T(8,128)(2,1)S(1)}, u32[]{:S(2)}, u32[]{:S(2)}) collective-permute-start(f16[272,128]{1,0:T(8,128)(2,1)S(1)} %convert_element_type.56), channel_id=1, source_target_pairs={{0,4},{1,5},{2,6},{3,7},{4,0},{5,1},{6,2},{7,3},{8,12},{9,13},{10,... | collective-permute-start | bytes 208904 | tf_op jit(solution)/shard_map/ppermute | solution.py:331
  31.1 1.2 %collective-permute-start.10 = (f16[272,128]{1,0:T(8,128)(2,1)S(1)}, f16[272,128]{1,0:T(8,128)(2,1)S(1)}, u32[]{:S(2)}, u32[]{:S(2)}) collective-permute-start(f16[272,128]{1,0:T(8,128)(2,1)S(1)} %convert_element_type.56), channel_id=1, source_target_pairs={{0,6},{1,7},{2,4},{3,5},{4,2},{5,3},{6,0},{7,1},{8,14},{9,15},{10,... | collective-permute-start | bytes 208904 | tf_op jit(solution)/shard_map/ppermute | solution.py:331
  32.4 0.5 %collective-permute-done.8 = f16[272,128]{1,0:T(8,128)(2,1)S(1)} collective-permute-done((f16[272,128]{1,0:T(8,128)(2,1)S(1)}, f16[272,128]{1,0:T(8,128)(2,1)S(1)}, u32[]{:S(2)}, u32[]{:S(2)}) %collective-permute-start.8) | collective-permute-done | bytes 69664 | tf_op jit(solution)/shard_map/ppermute | solution.py:331
  33.0 2.2 %collective-permute-done.10 = f16[272,128]{1,0:T(8,128)(2,1)S(1)} collective-permute-done((f16[272,128]{1,0:T(8,128)(2,1)S(1)}, f16[272,128]{1,0:T(8,128)(2,1)S(1)}, u32[]{:S(2)}, u32[]{:S(2)}) %collective-permute-start.10) | collective-permute-done | bytes 69664 | tf_op jit(solution)/shard_map/ppermute | solution.py:331
  35.2 4.4 %shard_map.64 = (bf16[256,512]{1,0:T(8,128)(2,1)S(1)}, bf16[256,512]{1,0:T(8,128)(2,1)S(1)}, bf16[512,512]{1,0:T(8,128)(2,1)S(1)}) custom-call(s32[3]{0:T(128)S(1)} %pad_add_fusion.pos_ref, f32[272,128]{1,0:T(8,128)S(1)} %get-tuple-element.27.own_ref, f32[272,128]{1,0:T(8,128)S(1)} %convert_element_type.57.refs_0_, ...), custom_call_target="tpu_custom_call" | custom-call | flops 3221225472 | bytes 2654220 | tf_op jit(solution)/shard_map/pallas_call | solution.py:299
  39.7 3.7 %collective-permute-start.11 = (bf16[256,512]{1,0:T(8,128)(2,1)S(1)}, bf16[256,512]{1,0:T(8,128)(2,1)S(1)}, u32[]{:S(2)}, u32[]{:S(2)}) collective-permute-start(bf16[256,512]{1,0:T(8,128)(2,1)S(1)} %get-tuple-element.33), channel_id=1, source_target_pairs={{0,1},{1,0},{2,3},{3,2},{4,5},{5,4},{6,7},{7,6},{8,9},{9,8},{10,11... | collective-permute-start | bytes 786440 | tf_op jit(solution)/shard_map/ppermute | solution.py:331
  43.9 0.8 %collective-permute-done.12.refs_1_ = f32[8,128]{1,0:T(8,128)S(1)} collective-permute-done((f32[8,128]{1,0:T(8,128)S(1)}, f32[8,128]{1,0:T(8,128)S(1)}, u32[]{:S(2)}, u32[]{:S(2)}) %collective-permute-start.12) | collective-permute-done | bytes 4128 | tf_op jit(solution)/shard_map/ppermute | solution.py:331
  44.7 0.7 %shard_map.67 = f32[1,8]{1,0:T(1,128)} custom-call(f32[8,128]{1,0:T(8,128)S(1)} %shard_map.66.refs_0_, f32[8,128]{1,0:T(8,128)S(1)} %collective-permute-done.12.refs_1_, f32[1,8]{1,0:T(1,128)S(1)} %get-tuple-element.39.refs_2_, f32[2,8]{1,0:T(2,128)S(1)} %fusion.refs_3_, f32[1,8]{1,0:T(1,128)S(1)} %bitcast.27), custom_call_target="tpu_custom_call" | custom-call | bytes 8352 | tf_op jit(solution)/shard_map/pallas_call | solution.py:299
  45.5 1.1 %convert_multiply_fusion = f32[2,256,512]{2,1,0:T(8,128)} fusion(bf16[1,256,512]{2,1,0:T(8,128)(2,1)S(1)} %get-tuple-element.35, bf16[1,256,512]{2,1,0:T(8,128)(2,1)S(1)} %get-tuple-element.34), kind=kLoop, calls=%fused_computation.1 | loop fusion | flops 786432 | bytes 1572864 | tf_op jit(solution)/shard_map/mul | solution.py:481
  (39 shorter events, 1.6 us)
Async XLA Ops:
  1.6 10.5 %collective-permute-start.2 = (bf16[256,512]{1,0:T(8,128)(2,1)S(1)}, bf16[256,512]{1,0:T(8,128)(2,1)S(1)}, u32[]{:S(2)}, u32[]{:S(2)}) collective-permute-start(bf16[256,512]{1,0:T(8,128)(2,1)S(1)} %dynamic-slice_bitcast_fusion), channel_id=1, source_target_pairs={{0,16},{1,17},{2,18},{3,19},{4,20},{5,21},{6,22},{7,23},{8,24},{9,... | collective-permute-start | bytes 786440 | tf_op jit(solution)/shard_map/ppermute | solution.py:331
  3.8 1.2 %copy-start = (bf16[1,4,256,512]{3,2,1,0:T(8,128)(2,1)S(1)}, bf16[1,4,256,512]{3,2,1,0:T(8,128)(2,1)}, u32[]{:S(2)}) copy-start(bf16[1,4,256,512]{3,2,1,0:T(8,128)(2,1)} %param.4) | copy-start | bytes 3145732
  5.7 7.5 %collective-permute-start = (bf16[256,512]{1,0:T(8,128)(2,1)S(1)}, bf16[256,512]{1,0:T(8,128)(2,1)S(1)}, u32[]{:S(2)}, u32[]{:S(2)}) collective-permute-start(bf16[256,512]{1,0:T(8,128)(2,1)S(1)} %get-tuple-element.18), channel_id=1, source_target_pairs={{0,1},{1,0},{2,3},{3,2},{4,5},{5,4},{6,7},{7,6},{8,9},{9,8},{10,11... | collective-permute-start | bytes 786440 | tf_op jit(solution)/shard_map/ppermute | solution.py:331
  6.7 9.2 %collective-permute-start.1 = (bf16[256,512]{1,0:T(8,128)(2,1)S(1)}, bf16[256,512]{1,0:T(8,128)(2,1)S(1)}, u32[]{:S(2)}, u32[]{:S(2)}) collective-permute-start(bf16[256,512]{1,0:T(8,128)(2,1)S(1)} %get-tuple-element.19), channel_id=1, source_target_pairs={{0,17},{1,16},{2,19},{3,18},{4,21},{5,20},{6,23},{7,22},{8,25},{9,... | collective-permute-start | bytes 786440 | tf_op jit(solution)/shard_map/ppermute | solution.py:331
  6.7 0.7 %copy-start.3 = (s32[2]{0:T(128)S(1)}, s32[2]{0:T(128)}, u32[]{:S(2)}) copy-start(s32[2]{0:T(128)} %param.6) | copy-start | bytes 28
  7.3 0.7 %copy-start.1 = (f32[8]{0:T(128)S(1)}, f32[8]{0:T(128)}, u32[]{:S(2)}) copy-start(f32[8]{0:T(128)} %param.7) | copy-start | bytes 100
  9.4 0.7 %copy-start.2 = (s32[4]{0:T(128)S(1)}, s32[4]{0:T(128)}, u32[]{:S(2)}) copy-start(s32[4]{0:T(128)} %param.5) | copy-start | bytes 52
  17.2 4.2 %collective-permute-start.3 = (f16[272,128]{1,0:T(8,128)(2,1)S(1)}, f16[272,128]{1,0:T(8,128)(2,1)S(1)}, u32[]{:S(2)}, u32[]{:S(2)}) collective-permute-start(f16[272,128]{1,0:T(8,128)(2,1)S(1)} %get-tuple-element.38), channel_id=1, source_target_pairs={{0,2},{1,3},{2,0},{3,1},{4,6},{5,7},{6,4},{7,5},{8,10},{9,11},{10,... | collective-permute-start | bytes 208904 | tf_op jit(solution)/shard_map/ppermute | solution.py:331
  18.7 3.8 %collective-permute-start.4 = (f16[272,128]{1,0:T(8,128)(2,1)S(1)}, f16[272,128]{1,0:T(8,128)(2,1)S(1)}, u32[]{:S(2)}, u32[]{:S(2)}) collective-permute-start(f16[272,128]{1,0:T(8,128)(2,1)S(1)} %get-tuple-element.37), channel_id=1, source_target_pairs={{0,4},{1,5},{2,6},{3,7},{4,0},{5,1},{6,2},{7,3},{8,12},{9,13},{10,... | collective-permute-start | bytes 208904 | tf_op jit(solution)/shard_map/ppermute | solution.py:331
  20.0 4.4 %collective-permute-start.5 = (f16[272,128]{1,0:T(8,128)(2,1)S(1)}, f16[272,128]{1,0:T(8,128)(2,1)S(1)}, u32[]{:S(2)}, u32[]{:S(2)}) collective-permute-start(f16[272,128]{1,0:T(8,128)(2,1)S(1)} %get-tuple-element.36), channel_id=1, source_target_pairs={{0,6},{1,7},{2,4},{3,5},{4,2},{5,3},{6,0},{7,1},{8,14},{9,15},{10,... | collective-permute-start | bytes 208904 | tf_op jit(solution)/shard_map/ppermute | solution.py:331
  20.0 4.4 %collective-permute-start.6 = (f32[8,128]{1,0:T(8,128)S(1)}, f32[8,128]{1,0:T(8,128)S(1)}, u32[]{:S(2)}, u32[]{:S(2)}) collective-permute-start(f32[8,128]{1,0:T(8,128)S(1)} %slice.18.refs_4_), channel_id=1, source_target_pairs={{0,16},{1,17},{2,18},{3,19},{4,20},{5,21},{6,22},{7,23},{8,24},{9,... | collective-permute-start | bytes 12296 | tf_op jit(solution)/shard_map/ppermute | solution.py:331
  24.6 4.9 %collective-permute-start.7 = (f16[272,128]{1,0:T(8,128)(2,1)S(1)}, f16[272,128]{1,0:T(8,128)(2,1)S(1)}, u32[]{:S(2)}, u32[]{:S(2)}) collective-permute-start(f16[272,128]{1,0:T(8,128)(2,1)S(1)} %convert_element_type.54), channel_id=1, source_target_pairs={{0,8},{1,9},{2,10},{3,11},{4,12},{5,13},{6,14},{7,15},{8,0},{9,1},... | collective-permute-start | bytes 208904 | tf_op jit(solution)/shard_map/ppermute | solution.py:331
  29.7 3.2 %collective-permute-start.8 = (f16[272,128]{1,0:T(8,128)(2,1)S(1)}, f16[272,128]{1,0:T(8,128)(2,1)S(1)}, u32[]{:S(2)}, u32[]{:S(2)}) collective-permute-start(f16[272,128]{1,0:T(8,128)(2,1)S(1)} %convert_element_type.56), channel_id=1, source_target_pairs={{0,2},{1,3},{2,0},{3,1},{4,6},{5,7},{6,4},{7,5},{8,10},{9,11},{10,... | collective-permute-start | bytes 208904 | tf_op jit(solution)/shard_map/ppermute | solution.py:331
  29.7 3.2 %collective-permute-start.9 = (f16[272,128]{1,0:T(8,128)(2,1)S(1)}, f16[272,128]{1,0:T(8,128)(2,1)S(1)}, u32[]{:S(2)}, u32[]{:S(2)}) collective-permute-start(f16[272,128]{1,0:T(8,128)(2,1)S(1)} %convert_element_type.56), channel_id=1, source_target_pairs={{0,4},{1,5},{2,6},{3,7},{4,0},{5,1},{6,2},{7,3},{8,12},{9,13},{10,... | collective-permute-start | bytes 208904 | tf_op jit(solution)/shard_map/ppermute | solution.py:331
  31.1 4.1 %collective-permute-start.10 = (f16[272,128]{1,0:T(8,128)(2,1)S(1)}, f16[272,128]{1,0:T(8,128)(2,1)S(1)}, u32[]{:S(2)}, u32[]{:S(2)}) collective-permute-start(f16[272,128]{1,0:T(8,128)(2,1)S(1)} %convert_element_type.56), channel_id=1, source_target_pairs={{0,6},{1,7},{2,4},{3,5},{4,2},{5,3},{6,0},{7,1},{8,14},{9,15},{10,... | collective-permute-start | bytes 208904 | tf_op jit(solution)/shard_map/ppermute | solution.py:331
  39.7 5.7 %collective-permute-start.11 = (bf16[256,512]{1,0:T(8,128)(2,1)S(1)}, bf16[256,512]{1,0:T(8,128)(2,1)S(1)}, u32[]{:S(2)}, u32[]{:S(2)}) collective-permute-start(bf16[256,512]{1,0:T(8,128)(2,1)S(1)} %get-tuple-element.33), channel_id=1, source_target_pairs={{0,1},{1,0},{2,3},{3,2},{4,5},{5,4},{6,7},{7,6},{8,9},{9,8},{10,11... | collective-permute-start | bytes 786440 | tf_op jit(solution)/shard_map/ppermute | solution.py:331
  43.5 1.2 %collective-permute-start.12 = (f32[8,128]{1,0:T(8,128)S(1)}, f32[8,128]{1,0:T(8,128)S(1)}, u32[]{:S(2)}, u32[]{:S(2)}) collective-permute-start(f32[8,128]{1,0:T(8,128)S(1)} %shard_map.66.refs_0_), channel_id=1, source_target_pairs={{0,1},{1,0},{2,3},{3,2},{4,5},{5,4},{6,7},{7,6},{8,9},{9,8},{10,11... | collective-permute-start | bytes 12296 | tf_op jit(solution)/shard_map/ppermute | solution.py:331

commit v6 on v5

--- a/solution.py
+++ b/solution.py
@@ -94,17 +94,18 @@
     if stage:
         sofar_ref, scal_ref, refs = refs[0], refs[1], refs[2:]
     comb_ref, refs = refs[0], refs[1:]
-    rows, columns = blocks[0].shape
+    _, columns = blocks[0].shape
     domain_pos, quad = pos_ref[0], pos_ref[1]
 
     def total(v):
         return jnp.sum(jnp.sum(v, axis=0, keepdims=True), axis=1, keepdims=True)
 
-    keep = lax.broadcasted_iota(jnp.int32, (rows, 1), 0) < lim_ref[stage]
-    masked = [jnp.where(keep, ref[...].astype(F32), 0.0) for ref in blocks]
-    combined = mix_ref[0] * masked[0]
+    keep = lim_ref[stage] > 0
+    values = [ref[...].astype(F32) for ref in blocks]
+    weights = [jnp.where(keep, mix_ref[kd], 0.0) for kd in range(domains)]
+    combined = weights[0] * values[0]
     for kd in range(1, domains):
-        combined = combined + mix_ref[kd] * masked[kd]
+        combined = combined + weights[kd] * values[kd]
     comb_ref[...] = combined
     rounded = combined.astype(jnp.bfloat16)
     gram = lax.dot_general(
@@ -114,8 +115,9 @@
     scal = jnp.where(lane == 2 * domains, total(combined * combined), 0.0)
     for kd in range(domains):
         group = domain_pos ^ kd
-        scal = jnp.where(lane == group, total(masked[kd] * combined), scal)
-        scal = jnp.where(lane == domains + group, total(masked[kd] * masked[kd]), scal)
+        square = jnp.where(keep, total(values[kd] * values[kd]), 0.0)
+        scal = jnp.where(lane == group, total(values[kd] * combined), scal)
+        scal = jnp.where(lane == domains + group, square, scal)
     if stage:
         scal = scal + scal_ref[0:1, :]
     if not last:
@@ -124,7 +126,8 @@
         sums_ref[...] = jnp.broadcast_to(scal, sums_ref.shape)
         return
 
-    pay_ref, own_ref, piece_ref, diag_ref = refs
+    (pay_ref,) = refs
+    body_rows = pay_ref.shape[1] - TAIL
     parts = encode_row(scal)
     scal = decode_row(parts)
     frob = lane_pick(scal, 2 * domains)
@@ -139,6 +142,8 @@
         return value
 
     for p, entries in enumerate(block_plan(columns)):
+        slot = quad ^ p
+        factor = jnp.where(slot == 0, 1.0, scale)
         diag = jnp.zeros((1, BLOCK), F32)
         for n, (i, j) in enumerate(entries):
             if i == j:
@@ -147,18 +152,10 @@
                 diag = jnp.sum(jnp.where(row_id == col_id, upper, 0.0), axis=0, keepdims=True)
             else:
                 value = part(i, j)
-            piece_ref[p, pl.ds(n * BLOCK, BLOCK), :] = value
-        diag_ref[p] = jnp.broadcast_to(diag, diag_ref.shape[1:])
-    body_rows = piece_ref.shape[1]
-    for k in range(SQUARE):
-        value = piece_ref[quad ^ k]
-        diag = diag_ref[quad ^ k][0:1]
-        if k == 0:
-            own_ref[pl.ds(0, body_rows), :] = value
-            own_ref[pl.ds(body_rows, TAIL), :] = tail_rows([diag, scal])
-        else:
-            pay_ref[k - 1, pl.ds(0, body_rows), :] = value * scale
-            pay_ref[k - 1, pl.ds(body_rows, TAIL), :] = tail_rows([diag * scale, *parts])
+            pay_ref[slot, pl.ds(n * BLOCK, BLOCK), :] = value * factor
+        own_tail = tail_rows([diag, scal])
+        sent_tail = tail_rows([diag * scale, *parts])
+        pay_ref[slot, pl.ds(body_rows, TAIL), :] = jnp.where(slot == 0, own_tail, sent_tail)
 
 
 def tree_sum(terms):
@@ -199,10 +196,8 @@
 
 def newton_kernel(scalar_lane, lanes, pos_ref, own_ref, *refs):
     got, refs = refs[: SQUARE - 1], refs[SQUARE - 1 :]
-    combs, (away_ref, stay_ref, poly_ref, piece_ref, diag_ref, gram_ref, start_ref) = (
-        refs[:lanes],
-        refs[lanes:],
-    )
+    combs, refs = refs[: lanes - 1], refs[lanes - 1 :]
+    away_ref, poly_ref, inv_ref, piece_ref, diag_ref, gram_ref, start_ref = refs
     quad = pos_ref[1]
     body_rows = own_ref.shape[0] - TAIL
     rows, columns = combs[0].shape
@@ -241,20 +236,20 @@
     def dot(x, y):
         return jnp.dot(x, y, preferred_element_type=F32)
 
-    for kl in range(lanes):
-        start_ref[pl.ds(kl * rows, rows), :] = (combs[kl][...] * inv).astype(jnp.bfloat16)
+    inv_ref[...] = jnp.broadcast_to(inv, inv_ref.shape)
+    for n, ref in enumerate(combs):
+        start_ref[pl.ds(n * rows, rows), :] = (ref[...] * inv).astype(jnp.bfloat16)
     gram = gram_ref[...]
     iterate = start_ref[...]
     for step in range(NS_ITERS):
         gram_low = gram.astype(jnp.bfloat16)
         square = dot(gram_low, gram_low)
         poly = (COEF_B * gram + COEF_C * square).astype(jnp.bfloat16)
+        poly_ref[step] = poly
+        iterate = newton_rows(iterate, poly)
         if step + 1 == NS_ITERS:
-            away_ref[...] = newton_rows(iterate[rows:], poly)
-            stay_ref[...] = iterate[:rows]
-            poly_ref[...] = poly
+            away_ref[...] = iterate
             return
-        iterate = newton_rows(iterate, poly)
         half = COEF_A * gram + dot(gram_low, poly)
         half_high = half.astype(jnp.bfloat16)
         half_low = (half - half_high.astype(F32)).astype(jnp.bfloat16)
@@ -264,10 +259,6 @@
 def newton_rows(iterate, poly):
     moved = jnp.dot(iterate, poly, preferred_element_type=F32)
     return (COEF_A * iterate.astype(F32) + moved).astype(jnp.bfloat16)
-
-
-def own_rows_kernel(stay_ref, poly_ref, out_ref):
-    out_ref[...] = newton_rows(stay_ref[...], poly_ref[...])
 
 
 def every_kernel(own_ref, *refs):
@@ -280,8 +271,9 @@
     out_ref[...] = jnp.broadcast_to(sums, out_ref.shape)
 
 
-def weight_kernel(domains, *refs):
-    tiles, (share_ref, onehot_ref, counts_ref, out_ref) = refs[:-4], refs[-4:]
+def finish_kernel(domains, count, comb_ref, inv_ref, poly_ref, *refs):
+    tiles, refs = refs[:count], refs[count:]
+    share_ref, onehot_ref, counts_ref, rows_ref, out_ref, held_ref, sem = refs
     sums = tree_sum([ref[0:1, :] for ref in tiles])
     norm = jnp.sqrt(lane_pick(sums, 2 * domains))
     score = jnp.zeros(share_ref.shape, F32)
@@ -291,19 +283,27 @@
         score = score + onehot_ref[g : g + 1, :] * cosine
     score = score / jnp.maximum(counts_ref[...], 1.0)
     raised = share_ref[...] * jnp.exp(ETA * score)
-    out_ref[...] = raised / jnp.sum(raised, axis=1, keepdims=True)
-
-
-def call(kernel, out_shape, args, spaces, scratch=(), flops=0, grant=VMEM_GRANT):
+    held_ref[...] = raised / jnp.sum(raised, axis=1, keepdims=True)
+    copy = pltpu.make_async_copy(held_ref, out_ref, sem)
+    copy.start()
+    iterate = (comb_ref[...] * inv_ref[0:1, 0:1]).astype(jnp.bfloat16)
+    for step in range(NS_ITERS):
+        iterate = newton_rows(iterate, poly_ref[step])
+    rows_ref[...] = iterate
+    copy.wait()
+
+
+def call(kernel, out_shape, args, spaces, scratch=(), flops=0, outs=None):
     size = sum(math.prod(a.shape) * a.dtype.itemsize for a in (*args, *out_shape))
+    outs = outs or [pltpu.VMEM] * len(out_shape)
     return pl.pallas_call(
         kernel,
         out_shape=tuple(out_shape),
         in_specs=[pl.BlockSpec(memory_space=s) for s in spaces],
-        out_specs=tuple(pl.BlockSpec(memory_space=pltpu.VMEM) for _ in out_shape),
+        out_specs=tuple(pl.BlockSpec(memory_space=s) for s in outs),
         scratch_shapes=list(scratch),
         cost_estimate=pl.CostEstimate(flops=flops, bytes_accessed=size, transcendentals=0),
-        compiler_params=pltpu.CompilerParams(vmem_limit_bytes=grant),
+        compiler_params=pltpu.CompilerParams(vmem_limit_bytes=VMEM_GRANT),
     )(*args)
 
 
@@ -383,10 +383,7 @@
         last = kl == lanes - 1
         results = [jax.ShapeDtypeStruct((rows, columns), F32)]
         if last:
-            results += [
-                jax.ShapeDtypeStruct((SQUARE - 1, packed, BLOCK), F32),
-                jax.ShapeDtypeStruct((packed, BLOCK), F32),
-            ]
+            results += [jax.ShapeDtypeStruct((SQUARE, packed, BLOCK), F32)]
         else:
             results += [square, jax.ShapeDtypeStruct((8, BLOCK), F32)]
         comb, *carried = call(
@@ -394,11 +391,11 @@
             results,
             [mix, limits, position, *blocks[kl::lanes], *carried],
             [smem] * 3 + [vmem] * (domains + len(carried)),
-            pieces_scratch if last else (),
             flops=2 * rows * columns * columns,
         )
         combs.append(comb)
-    payload, own = carried
+    (payload,) = carried
+    own = payload[0]
     scalar_lane = 2 * domains
 
     def add_up(own, got, tiles=()):
@@ -412,7 +409,7 @@
     def half_width(value, mask):
         return exchange(value.astype(jnp.float16), mask).astype(F32)
 
-    got = [half_width(payload[k - 1], k * lanes) for k in range(1, SQUARE)]
+    got = [half_width(payload[k], k * lanes) for k in range(1, SQUARE)]
     tiles = [own[per_piece : per_piece + 8]]
     if domains <= 4:
         tiles += [exchange(tiles[0], kd * shards) for kd in range(1, domains)]
@@ -437,33 +434,33 @@
         tiles = [every, exchange(every, stride)]
         stride *= 2
 
-    away, stay, poly = call(
+    away, poly, inv = call(
         functools.partial(newton_kernel, scalar_lane, lanes),
         [
             jax.ShapeDtypeStruct(((lanes - 1) * rows, columns), jnp.bfloat16),
-            jax.ShapeDtypeStruct((rows, columns), jnp.bfloat16),
-            jax.ShapeDtypeStruct((columns, columns), jnp.bfloat16),
+            jax.ShapeDtypeStruct((NS_ITERS, columns, columns), jnp.bfloat16),
+            jax.ShapeDtypeStruct((8, BLOCK), F32),
         ],
-        [position, own, *got, *combs],
-        [smem] + [vmem] * (SQUARE + lanes),
+        [position, own, *got, *combs[1:]],
+        [smem] + [vmem] * (SQUARE + lanes - 1),
         pieces_scratch
-        + [pltpu.VMEM((columns, columns), F32), pltpu.VMEM((lanes * rows, columns), jnp.bfloat16)],
-        flops=12 * 2 * columns**3,
+        + [
+            pltpu.VMEM((columns, columns), F32),
+            pltpu.VMEM(((lanes - 1) * rows, columns), jnp.bfloat16),
+        ],
+        flops=10 * 2 * columns**3,
     )
     away = away.reshape(lanes - 1, rows, columns)
     returned = [exchange(away[k - 1], k) for k in range(1, lanes)]
-    (kept,) = call(
-        own_rows_kernel,
-        [jax.ShapeDtypeStruct((rows, columns), jnp.bfloat16)],
-        [stay, poly],
-        [vmem, vmem],
-        flops=2 * rows * columns * columns,
-    )
-    (weights,) = call(
-        functools.partial(weight_kernel, domains),
-        [jax.ShapeDtypeStruct((1, weight_share.shape[0]), F32)],
-        [*tiles, weight_share[None], onehot, counts[None]],
-        [vmem] * (len(tiles) + 3),
+    kinds = jax.ShapeDtypeStruct((1, weight_share.shape[0]), F32)
+    kept, weights = call(
+        functools.partial(finish_kernel, domains, len(tiles)),
+        [jax.ShapeDtypeStruct((rows, columns), jnp.bfloat16), kinds],
+        [combs[0], inv, poly, *tiles, weight_share[None], onehot, counts[None]],
+        [vmem] * (6 + len(tiles)),
+        [pltpu.VMEM(kinds.shape, F32), pltpu.SemaphoreType.DMA],
+        flops=NS_ITERS * 2 * rows * columns * columns,
+        outs=[vmem, hbm],
     )
     returned = [kept, *returned]
     if lanes == 2:

time: 47 us -> 46.8 us (level)
  local copies, waits for them, and re-layouts: 5.32 us -> 3.49 us
  waiting for transfers between devices: 12 us -> 13.7 us
    unnamed x8, local copies, waits for them, and re-layouts: 3.08 us -> 1.24 us
    ppermute x13, waiting for transfers between devices: 12 us -> 13.7 us  [exchange(): lax.ppermute(value, AXES, [(i, i ^ mask) for i in range(domains * shards)])]
    pallas_call x9 -> x8, Pallas kernels: 8.6 us -> 8.35 us  [call(): pl.pallas_call(kernel, out_shape=tuple(out_shape), in_specs=[pl.BlockSpec...]
where the time goes in v6:
time: 46.8 us; the launch traced here: 46.3 us
  starting transfers between devices  16.1 us (34%)
  waiting for transfers between devices  13.7 us (29%)
  Pallas kernels  8.35 us (18%)
  other arithmetic  3.71 us (8%)
  local copies, waits for them, and re-layouts  3.49 us (7%)
  between operations  0.91 us (2%)
    ppermute x13, starting transfers between devices, exchange(): lax.ppermute(value, AXES, [(i, i ^ mask) for i in range(domains * shards)])  16.1 us
    ppermute x13, waiting for transfers between devices, exchange(): lax.ppermute(value, AXES, [(i, i ^ mask) for i in range(domains * shards)])  13.7 us
    pallas_call x8, Pallas kernels, call(): pl.pallas_call(kernel, out_shape=tuple(out_shape), in_specs=[pl.BlockSpec...  8.35 us
    unnamed x8, local copies, waits for them, and re-layouts  1.24 us
    mul x1, other arithmetic, body(): jnp.stack(ordered).astype(F32) * (MUON_SCALE * math.sqrt(full_rows))  1.11 us
    squeeze x1, local copies, waits for them, and re-layouts, body(): lax.dynamic_index_in_dim(gradients[0], member ^ order[0], 0, keepdims=False)  0.97 us
  transfers between devices with their start and end apart: 13, of which 8 were waited for; matrix products, arithmetic and copies ran while one was open for 8% of the time, Pallas kernels for 6%

profile of v6, /device:TPU:1, one launch (start us, length us, event | category | flops | bytes accessed | tf_op | source)
XLA Modules:
  0.0 46.3 jit_solution(4228785573487644123)
XLA Ops:
  0.7 1.0 %dynamic-slice_bitcast_fusion = bf16[256,512]{1,0:T(8,128)(2,1)S(1)} fusion(bf16[1,4,256,512]{3,2,1,0:T(8,128)(2,1)} %param.4, s32[]{:T(128)S(6)} %select_n.63), kind=kLoop, calls=%fused_computation.4 | loop fusion | bytes 524292 | tf_op jit(solution)/shard_map/jit(dynamic_index_in_dim)/squeeze | solution.py:348
  1.7 2.1 %collective-permute-start = (bf16[256,512]{1,0:T(8,128)(2,1)S(1)}, bf16[256,512]{1,0:T(8,128)(2,1)S(1)}, u32[]{:S(2)}, u32[]{:S(2)}) collective-permute-start(bf16[256,512]{1,0:T(8,128)(2,1)S(1)} %dynamic-slice_bitcast_fusion), channel_id=1, source_target_pairs={{0,16},{1,17},{2,18},{3,19},{4,20},{5,21},{6,22},{7,23},{8,24},{9,... | collective-permute-start | bytes 786440 | tf_op jit(solution)/shard_map/ppermute | solution.py:331
  3.8 1.2 %copy-done = bf16[1,4,256,512]{3,2,1,0:T(8,128)(2,1)S(1)} copy-done((bf16[1,4,256,512]{3,2,1,0:T(8,128)(2,1)S(1)}, bf16[1,4,256,512]{3,2,1,0:T(8,128)(2,1)}, u32[]{:S(2)}) %copy-start) | copy-done | bytes 1048600
  5.1 0.6 %shard_map.59 = (bf16[256,512]{1,0:T(8,128)(2,1)S(1)}, bf16[256,512]{1,0:T(8,128)(2,1)S(1)}, bf16[256,512]{1,0:T(8,128)(2,1)S(1)}) custom-call(s32[3]{0:T(128)S(1)} %pad_add_fusion.1.index_ref, bf16[4,256,512]{2,1,0:T(8,128)(2,1)S(1)} %bitcast.30), custom_call_target="tpu_custom_call" | custom-call | bytes 1835020 | tf_op jit(solution)/shard_map/pallas_call | solution.py:299
  5.7 1.0 %collective-permute-start.1 = (bf16[256,512]{1,0:T(8,128)(2,1)S(1)}, bf16[256,512]{1,0:T(8,128)(2,1)S(1)}, u32[]{:S(2)}, u32[]{:S(2)}) collective-permute-start(bf16[256,512]{1,0:T(8,128)(2,1)S(1)} %get-tuple-element.21), channel_id=1, source_target_pairs={{0,1},{1,0},{2,3},{3,2},{4,5},{5,4},{6,7},{7,6},{8,9},{9,8},{10,11... | collective-permute-start | bytes 786440 | tf_op jit(solution)/shard_map/ppermute | solution.py:331
  6.8 0.6 %reduce_sum.27 = f32[]{:T(128)} reduce(f32[8]{0:T(128)S(1)} %copy-done.1, f32[]{:T(128)} %constant.69.clone.1), dimensions={0}, to_apply=%region_0.1 | reduce | flops 7 | bytes 40 | tf_op jit(solution)/shard_map/reduce_sum | solution.py:30
  7.4 0.7 %divide_bitcast_fusion = (f32[1,8]{1,0:T(1,128)S(1)}, f32[8]{0:T(128)S(1)}) fusion(f32[8]{0:T(128)S(1)} %copy-done.1, f32[]{:T(128)} %reduce_sum.27, f32[8]{0:T(128)S(1)} %fusion.2), kind=kLoop, calls=%fused_computation.20 | loop fusion | flops 32 | bytes 132 | tf_op jit(solution)/shard_map/broadcast_in_dim | solution.py:459
  8.1 0.2 select_reduce_fusion
  8.3 0.6 %dynamic_slice.8 = s32[1]{0:T(128)} dynamic-slice(s32[4]{0:T(128)S(1)} %copy-done.2, s32[]{:T(128)S(6)} %select_n.60), dynamic_slice_sizes={1} | dynamic-slice | bytes 12 | tf_op jit(solution)/shard_map/jit(dynamic_index_in_dim)/dynamic_slice | solution.py:371
  8.9 0.7 %multiply_subtract_fusion.lim_ref = s32[2]{0:T(128)S(1)} fusion(s32[]{:T(128)} %select_n.55, s32[]{:T(128)S(6)} %mul.26, s32[]{:T(128)} %bitcast.1), kind=kLoop, calls=%fused_computation.21 | loop fusion | flops 8 | bytes 20 | tf_op jit(solution)/shard_map/sub | solution.py:371
  9.6 0.6 %gather_fusion = f32[2]{0:T(128)S(1)} fusion(f32[2]{0:T(128)S(1)} %select_reduce_fusion, s32[1024]{0:T(1024)S(1)} %pad_clamp_fusion), kind=kCustom, calls=%fused_computation | custom fusion | bytes 24 | tf_op jit(solution)/shard_map/jit(_take)/gather | solution.py:369
  10.3 1.0 %shard_map.60 = (f32[256,512]{1,0:T(8,128)S(1)}, f32[512,512]{1,0:T(8,128)S(1)}, f32[8,128]{1,0:T(8,128)S(1)}) custom-call(f32[2]{0:T(128)S(1)} %and_select_fusion.mix_ref, s32[2]{0:T(128)S(1)} %multiply_subtract_fusion.lim_ref, s32[3]{0:T(128)S(1)} %pad_add_fusion.pos_ref, bf16[256,512]{1,0:T(8,128)(2,1)S(1)} %get-tuple-element.19.refs_0_, ...), custom_call_target="tpu_custom_call" | custom-call | flops 134217728 | bytes 2101276 | tf_op jit(solution)/shard_map/pallas_call | solution.py:299
  11.3 4.7 %collective-permute-done.2.refs_1_ = bf16[256,512]{1,0:T(8,128)(2,1)S(1)} collective-permute-done((bf16[256,512]{1,0:T(8,128)(2,1)S(1)}, bf16[256,512]{1,0:T(8,128)(2,1)S(1)}, u32[]{:S(2)}, u32[]{:S(2)}) %collective-permute-start.2) | collective-permute-done | bytes 262176 | tf_op jit(solution)/shard_map/ppermute | solution.py:331
  15.9 1.1 %shard_map.61 = (f32[256,512]{1,0:T(8,128)S(1)}, f32[4,272,128]{2,1,0:T(8,128)S(1)}) custom-call(f32[2]{0:T(128)S(1)} %and_select_fusion.mix_ref, s32[2]{0:T(128)S(1)} %multiply_subtract_fusion.lim_ref, s32[3]{0:T(128)S(1)} %pad_add_fusion.pos_ref, bf16[256,512]{1,0:T(8,128)(2,1)S(1)} %collective-permute-done.1.refs_0_, ...), custom_call_target="tpu_custom_call" | custom-call | flops 134217728 | bytes 2658332 | tf_op jit(solution)/shard_map/pallas_call | solution.py:299
  17.2 1.6 %collective-permute-start.3 = (f16[272,128]{1,0:T(8,128)(2,1)S(1)}, f16[272,128]{1,0:T(8,128)(2,1)S(1)}, u32[]{:S(2)}, u32[]{:S(2)}) collective-permute-start(f16[272,128]{1,0:T(8,128)(2,1)S(1)} %get-tuple-element.40), channel_id=1, source_target_pairs={{0,2},{1,3},{2,0},{3,1},{4,6},{5,7},{6,4},{7,5},{8,10},{9,11},{10,... | collective-permute-start | bytes 208904 | tf_op jit(solution)/shard_map/ppermute | solution.py:331
  18.7 1.3 %collective-permute-start.4 = (f16[272,128]{1,0:T(8,128)(2,1)S(1)}, f16[272,128]{1,0:T(8,128)(2,1)S(1)}, u32[]{:S(2)}, u32[]{:S(2)}) collective-permute-start(f16[272,128]{1,0:T(8,128)(2,1)S(1)} %get-tuple-element.39), channel_id=1, source_target_pairs={{0,4},{1,5},{2,6},{3,7},{4,0},{5,1},{6,2},{7,3},{8,12},{9,13},{10,... | collective-permute-start | bytes 208904 | tf_op jit(solution)/shard_map/ppermute | solution.py:331
  20.0 1.3 %collective-permute-start.6 = (f32[8,128]{1,0:T(8,128)S(1)}, f32[8,128]{1,0:T(8,128)S(1)}, u32[]{:S(2)}, u32[]{:S(2)}) collective-permute-start(f32[8,128]{1,0:T(8,128)S(1)} %slice_bitcast_fusion.4.refs_4_), channel_id=1, source_target_pairs={{0,16},{1,17},{2,18},{3,19},{4,20},{5,21},{6,22},{7,23},{8,24},{9,... | collective-permute-start | bytes 12296 | tf_op jit(solution)/shard_map/ppermute | solution.py:331
  21.4 1.1 %collective-permute-done.4 = f16[272,128]{1,0:T(8,128)(2,1)S(1)} collective-permute-done((f16[272,128]{1,0:T(8,128)(2,1)S(1)}, f16[272,128]{1,0:T(8,128)(2,1)S(1)}, u32[]{:S(2)}, u32[]{:S(2)}) %collective-permute-start.4) | collective-permute-done | bytes 69664 | tf_op jit(solution)/shard_map/ppermute | solution.py:331
  22.5 1.9 %collective-permute-done.5 = f16[272,128]{1,0:T(8,128)(2,1)S(1)} collective-permute-done((f16[272,128]{1,0:T(8,128)(2,1)S(1)}, f16[272,128]{1,0:T(8,128)(2,1)S(1)}, u32[]{:S(2)}, u32[]{:S(2)}) %collective-permute-start.5) | collective-permute-done | bytes 69664 | tf_op jit(solution)/shard_map/ppermute | solution.py:331
  24.4 0.1 shard_map.62
  24.6 2.3 %collective-permute-start.7 = (f16[272,128]{1,0:T(8,128)(2,1)S(1)}, f16[272,128]{1,0:T(8,128)(2,1)S(1)}, u32[]{:S(2)}, u32[]{:S(2)}) collective-permute-start(f16[272,128]{1,0:T(8,128)(2,1)S(1)} %convert_element_type.54), channel_id=1, source_target_pairs={{0,8},{1,9},{2,10},{3,11},{4,12},{5,13},{6,14},{7,15},{8,0},{9,1},... | collective-permute-start | bytes 208904 | tf_op jit(solution)/shard_map/ppermute | solution.py:331
  26.9 2.5 %collective-permute-done.7 = f16[272,128]{1,0:T(8,128)(2,1)S(1)} collective-permute-done((f16[272,128]{1,0:T(8,128)(2,1)S(1)}, f16[272,128]{1,0:T(8,128)(2,1)S(1)}, u32[]{:S(2)}, u32[]{:S(2)}) %collective-permute-start.7) | collective-permute-done | bytes 69664 | tf_op jit(solution)/shard_map/ppermute | solution.py:331
  29.5 0.1 shard_map.63
  29.7 1.4 %collective-permute-start.9 = (f16[272,128]{1,0:T(8,128)(2,1)S(1)}, f16[272,128]{1,0:T(8,128)(2,1)S(1)}, u32[]{:S(2)}, u32[]{:S(2)}) collective-permute-start(f16[272,128]{1,0:T(8,128)(2,1)S(1)} %convert_element_type.56), channel_id=1, source_target_pairs={{0,4},{1,5},{2,6},{3,7},{4,0},{5,1},{6,2},{7,3},{8,12},{9,13},{10,... | collective-permute-start | bytes 208904 | tf_op jit(solution)/shard_map/ppermute | solution.py:331
  31.1 1.2 %collective-permute-start.10 = (f16[272,128]{1,0:T(8,128)(2,1)S(1)}, f16[272,128]{1,0:T(8,128)(2,1)S(1)}, u32[]{:S(2)}, u32[]{:S(2)}) collective-permute-start(f16[272,128]{1,0:T(8,128)(2,1)S(1)} %convert_element_type.56), channel_id=1, source_target_pairs={{0,6},{1,7},{2,4},{3,5},{4,2},{5,3},{6,0},{7,1},{8,14},{9,15},{10,... | collective-permute-start | bytes 208904 | tf_op jit(solution)/shard_map/ppermute | solution.py:331
  32.4 0.5 %collective-permute-done.8 = f16[272,128]{1,0:T(8,128)(2,1)S(1)} collective-permute-done((f16[272,128]{1,0:T(8,128)(2,1)S(1)}, f16[272,128]{1,0:T(8,128)(2,1)S(1)}, u32[]{:S(2)}, u32[]{:S(2)}) %collective-permute-start.8) | collective-permute-done | bytes 69664 | tf_op jit(solution)/shard_map/ppermute | solution.py:331
  33.0 2.3 %collective-permute-done.10 = f16[272,128]{1,0:T(8,128)(2,1)S(1)} collective-permute-done((f16[272,128]{1,0:T(8,128)(2,1)S(1)}, f16[272,128]{1,0:T(8,128)(2,1)S(1)}, u32[]{:S(2)}, u32[]{:S(2)}) %collective-permute-start.10) | collective-permute-done | bytes 69664 | tf_op jit(solution)/shard_map/ppermute | solution.py:331
  35.2 4.2 %shard_map.64 = (bf16[256,512]{1,0:T(8,128)(2,1)S(1)}, bf16[3,512,512]{2,1,0:T(8,128)(2,1)S(1)}, f32[8,128]{1,0:T(8,128)S(1)}) custom-call(s32[3]{0:T(128)S(1)} %pad_add_fusion.pos_ref, f32[272,128]{1,0:T(8,128)S(1)} %get-tuple-element.28.own_ref, f32[272,128]{1,0:T(8,128)S(1)} %convert_element_type.57.refs_0_, f32[272,128]{1,0:T(8,128)S(1)} %convert_element_type.58.refs_1_, ...), custom_call_target="tpu_custom_call" | custom-call | flops 2684354560 | bytes 2920460 | tf_op jit(solution)/shard_map/pallas_call | solution.py:299
  39.5 3.7 %collective-permute-start.11 = (f32[8,128]{1,0:T(8,128)S(1)}, f32[8,128]{1,0:T(8,128)S(1)}, u32[]{:S(2)}, u32[]{:S(2)}) collective-permute-start(f32[8,128]{1,0:T(8,128)S(1)} %shard_map.65.refs_0_), channel_id=1, source_target_pairs={{0,1},{1,0},{2,3},{3,2},{4,5},{5,4},{6,7},{7,6},{8,9},{9,8},{10,11... | collective-permute-start | bytes 12296 | tf_op jit(solution)/shard_map/ppermute | solution.py:331
  43.3 0.7 %collective-permute-done.11.refs_1_ = f32[8,128]{1,0:T(8,128)S(1)} collective-permute-done((f32[8,128]{1,0:T(8,128)S(1)}, f32[8,128]{1,0:T(8,128)S(1)}, u32[]{:S(2)}, u32[]{:S(2)}) %collective-permute-start.11) | collective-permute-done | bytes 4128 | tf_op jit(solution)/shard_map/ppermute | solution.py:331
  44.0 1.1 %shard_map.66 = (bf16[256,512]{1,0:T(8,128)(2,1)S(1)}, f32[1,8]{1,0:T(1,128)}) custom-call(f32[256,512]{1,0:T(8,128)S(1)} %get-tuple-element.20.comb_ref, f32[8,128]{1,0:T(8,128)S(1)} %get-tuple-element.31.inv_ref, bf16[3,512,512]{2,1,0:T(8,128)(2,1)S(1)} %get-tuple-element.32.poly_ref, f32[8,128]{1,0:T(8,128)S(1)} %shard_map.65.refs_0_, ...), custom_call_target="tpu_custom_call" | custom-call | flops 402653184 | bytes 2371744 | tf_op jit(solution)/shard_map/pallas_call | solution.py:299
  45.2 1.1 %convert_multiply_fusion = f32[2,256,512]{2,1,0:T(8,128)} fusion(bf16[1,256,512]{2,1,0:T(8,128)(2,1)S(1)} %get-tuple-element.37, bf16[1,256,512]{2,1,0:T(8,128)(2,1)S(1)} %get-tuple-element.36), kind=kLoop, calls=%fused_computation.1 | loop fusion | flops 786432 | bytes 1572864 | tf_op jit(solution)/shard_map/mul | solution.py:478
  (39 shorter events, 0.8 us)
Async XLA Ops:
  0.6 6.1 %copy-start.3 = (s32[2]{0:T(128)S(1)}, s32[2]{0:T(128)}, u32[]{:S(2)}) copy-start(s32[2]{0:T(128)} %param.6) | copy-start | bytes 28
  0.6 6.2 %copy-start.1 = (f32[8]{0:T(128)S(1)}, f32[8]{0:T(128)}, u32[]{:S(2)}) copy-start(f32[8]{0:T(128)} %param.7) | copy-start | bytes 100
  0.7 7.6 %copy-start.2 = (s32[4]{0:T(128)S(1)}, s32[4]{0:T(128)}, u32[]{:S(2)}) copy-start(s32[4]{0:T(128)} %param.5) | copy-start | bytes 52
  1.7 8.6 %collective-permute-start = (bf16[256,512]{1,0:T(8,128)(2,1)S(1)}, bf16[256,512]{1,0:T(8,128)(2,1)S(1)}, u32[]{:S(2)}, u32[]{:S(2)}) collective-permute-start(bf16[256,512]{1,0:T(8,128)(2,1)S(1)} %dynamic-slice_bitcast_fusion), channel_id=1, source_target_pairs={{0,16},{1,17},{2,18},{3,19},{4,20},{5,21},{6,22},{7,23},{8,24},{9,... | collective-permute-start | bytes 786440 | tf_op jit(solution)/shard_map/ppermute | solution.py:331
  3.8 1.2 %copy-start = (bf16[1,4,256,512]{3,2,1,0:T(8,128)(2,1)S(1)}, bf16[1,4,256,512]{3,2,1,0:T(8,128)(2,1)}, u32[]{:S(2)}) copy-start(bf16[1,4,256,512]{3,2,1,0:T(8,128)(2,1)} %param.4) | copy-start | bytes 3145732
  5.7 5.6 %collective-permute-start.1 = (bf16[256,512]{1,0:T(8,128)(2,1)S(1)}, bf16[256,512]{1,0:T(8,128)(2,1)S(1)}, u32[]{:S(2)}, u32[]{:S(2)}) collective-permute-start(bf16[256,512]{1,0:T(8,128)(2,1)S(1)} %get-tuple-element.21), channel_id=1, source_target_pairs={{0,1},{1,0},{2,3},{3,2},{4,5},{5,4},{6,7},{7,6},{8,9},{9,8},{10,11... | collective-permute-start | bytes 786440 | tf_op jit(solution)/shard_map/ppermute | solution.py:331
  6.7 9.2 %collective-permute-start.2 = (bf16[256,512]{1,0:T(8,128)(2,1)S(1)}, bf16[256,512]{1,0:T(8,128)(2,1)S(1)}, u32[]{:S(2)}, u32[]{:S(2)}) collective-permute-start(bf16[256,512]{1,0:T(8,128)(2,1)S(1)} %get-tuple-element.22), channel_id=1, source_target_pairs={{0,17},{1,16},{2,19},{3,18},{4,21},{5,20},{6,23},{7,22},{8,25},{9,... | collective-permute-start | bytes 786440 | tf_op jit(solution)/shard_map/ppermute | solution.py:331
  17.2 4.2 %collective-permute-start.3 = (f16[272,128]{1,0:T(8,128)(2,1)S(1)}, f16[272,128]{1,0:T(8,128)(2,1)S(1)}, u32[]{:S(2)}, u32[]{:S(2)}) collective-permute-start(f16[272,128]{1,0:T(8,128)(2,1)S(1)} %get-tuple-element.40), channel_id=1, source_target_pairs={{0,2},{1,3},{2,0},{3,1},{4,6},{5,7},{6,4},{7,5},{8,10},{9,11},{10,... | collective-permute-start | bytes 208904 | tf_op jit(solution)/shard_map/ppermute | solution.py:331
  18.7 3.8 %collective-permute-start.4 = (f16[272,128]{1,0:T(8,128)(2,1)S(1)}, f16[272,128]{1,0:T(8,128)(2,1)S(1)}, u32[]{:S(2)}, u32[]{:S(2)}) collective-permute-start(f16[272,128]{1,0:T(8,128)(2,1)S(1)} %get-tuple-element.39), channel_id=1, source_target_pairs={{0,4},{1,5},{2,6},{3,7},{4,0},{5,1},{6,2},{7,3},{8,12},{9,13},{10,... | collective-permute-start | bytes 208904 | tf_op jit(solution)/shard_map/ppermute | solution.py:331
  20.0 4.4 %collective-permute-start.5 = (f16[272,128]{1,0:T(8,128)(2,1)S(1)}, f16[272,128]{1,0:T(8,128)(2,1)S(1)}, u32[]{:S(2)}, u32[]{:S(2)}) collective-permute-start(f16[272,128]{1,0:T(8,128)(2,1)S(1)} %get-tuple-element.38), channel_id=1, source_target_pairs={{0,6},{1,7},{2,4},{3,5},{4,2},{5,3},{6,0},{7,1},{8,14},{9,15},{10,... | collective-permute-start | bytes 208904 | tf_op jit(solution)/shard_map/ppermute | solution.py:331
  20.0 4.4 %collective-permute-start.6 = (f32[8,128]{1,0:T(8,128)S(1)}, f32[8,128]{1,0:T(8,128)S(1)}, u32[]{:S(2)}, u32[]{:S(2)}) collective-permute-start(f32[8,128]{1,0:T(8,128)S(1)} %slice_bitcast_fusion.4.refs_4_), channel_id=1, source_target_pairs={{0,16},{1,17},{2,18},{3,19},{4,20},{5,21},{6,22},{7,23},{8,24},{9,... | collective-permute-start | bytes 12296 | tf_op jit(solution)/shard_map/ppermute | solution.py:331
  24.6 4.9 %collective-permute-start.7 = (f16[272,128]{1,0:T(8,128)(2,1)S(1)}, f16[272,128]{1,0:T(8,128)(2,1)S(1)}, u32[]{:S(2)}, u32[]{:S(2)}) collective-permute-start(f16[272,128]{1,0:T(8,128)(2,1)S(1)} %convert_element_type.54), channel_id=1, source_target_pairs={{0,8},{1,9},{2,10},{3,11},{4,12},{5,13},{6,14},{7,15},{8,0},{9,1},... | collective-permute-start | bytes 208904 | tf_op jit(solution)/shard_map/ppermute | solution.py:331
  29.6 3.2 %collective-permute-start.8 = (f16[272,128]{1,0:T(8,128)(2,1)S(1)}, f16[272,128]{1,0:T(8,128)(2,1)S(1)}, u32[]{:S(2)}, u32[]{:S(2)}) collective-permute-start(f16[272,128]{1,0:T(8,128)(2,1)S(1)} %convert_element_type.56), channel_id=1, source_target_pairs={{0,2},{1,3},{2,0},{3,1},{4,6},{5,7},{6,4},{7,5},{8,10},{9,11},{10,... | collective-permute-start | bytes 208904 | tf_op jit(solution)/shard_map/ppermute | solution.py:331
  29.7 3.2 %collective-permute-start.9 = (f16[272,128]{1,0:T(8,128)(2,1)S(1)}, f16[272,128]{1,0:T(8,128)(2,1)S(1)}, u32[]{:S(2)}, u32[]{:S(2)}) collective-permute-start(f16[272,128]{1,0:T(8,128)(2,1)S(1)} %convert_element_type.56), channel_id=1, source_target_pairs={{0,4},{1,5},{2,6},{3,7},{4,0},{5,1},{6,2},{7,3},{8,12},{9,13},{10,... | collective-permute-start | bytes 208904 | tf_op jit(solution)/shard_map/ppermute | solution.py:331
  31.1 4.1 %collective-permute-start.10 = (f16[272,128]{1,0:T(8,128)(2,1)S(1)}, f16[272,128]{1,0:T(8,128)(2,1)S(1)}, u32[]{:S(2)}, u32[]{:S(2)}) collective-permute-start(f16[272,128]{1,0:T(8,128)(2,1)S(1)} %convert_element_type.56), channel_id=1, source_target_pairs={{0,6},{1,7},{2,4},{3,5},{4,2},{5,3},{6,0},{7,1},{8,14},{9,15},{10,... | collective-permute-start | bytes 208904 | tf_op jit(solution)/shard_map/ppermute | solution.py:331
  39.5 4.5 %collective-permute-start.11 = (f32[8,128]{1,0:T(8,128)S(1)}, f32[8,128]{1,0:T(8,128)S(1)}, u32[]{:S(2)}, u32[]{:S(2)}) collective-permute-start(f32[8,128]{1,0:T(8,128)S(1)} %shard_map.65.refs_0_), channel_id=1, source_target_pairs={{0,1},{1,0},{2,3},{3,2},{4,5},{5,4},{6,7},{7,6},{8,9},{9,8},{10,11... | collective-permute-start | bytes 12296 | tf_op jit(solution)/shard_map/ppermute | solution.py:331
  43.2 1.9 %collective-permute-start.12 = (bf16[256,512]{1,0:T(8,128)(2,1)S(1)}, bf16[256,512]{1,0:T(8,128)(2,1)S(1)}, u32[]{:S(2)}, u32[]{:S(2)}) collective-permute-start(bf16[256,512]{1,0:T(8,128)(2,1)S(1)} %get-tuple-element.34), channel_id=1, source_target_pairs={{0,1},{1,0},{2,3},{3,2},{4,5},{5,4},{6,7},{7,6},{8,9},{9,8},{10,11... | collective-permute-start | bytes 786440 | tf_op jit(solution)/shard_map/ppermute | solution.py:331

commit v7 on v6

--- a/solution.py
+++ b/solution.py
@@ -108,21 +108,29 @@
         combined = combined + weights[kd] * values[kd]
     comb_ref[...] = combined
     rounded = combined.astype(jnp.bfloat16)
-    gram = lax.dot_general(
-        rounded, rounded, (((0,), (0,)), ((), ())), preferred_element_type=F32
-    )
+    half_width = columns // 2
+
+    def inner(x, y):
+        return lax.dot_general(x, y, (((0,), (0,)), ((), ())), preferred_element_type=F32)
+
+    gram_top = inner(rounded[:, :half_width], rounded)
+    gram_low = inner(rounded[:, half_width:], rounded[:, half_width:])
     lane = lax.broadcasted_iota(jnp.int32, (1, BLOCK), 1)
-    scal = jnp.where(lane == 2 * domains, total(combined * combined), 0.0)
+    frob = total(combined * combined)
+    scal = jnp.where(lane == 2 * domains, frob, 0.0)
     for kd in range(domains):
         group = domain_pos ^ kd
         square = jnp.where(keep, total(values[kd] * values[kd]), 0.0)
         scal = jnp.where(lane == group, total(values[kd] * combined), scal)
         scal = jnp.where(lane == domains + group, square, scal)
     if stage:
+        frob = frob + lane_pick(scal_ref[0:1, :], 2 * domains)
         scal = scal + scal_ref[0:1, :]
     if not last:
         gram_ref, sums_ref = refs
-        gram_ref[...] = gram + sofar_ref[...] if stage else gram
+        top, low = pl.ds(0, half_width), pl.ds(half_width, half_width)
+        gram_ref[top, :] = gram_top + sofar_ref[top, :] if stage else gram_top
+        gram_ref[low, low] = gram_low + sofar_ref[low, low] if stage else gram_low
         sums_ref[...] = jnp.broadcast_to(scal, sums_ref.shape)
         return
 
@@ -130,13 +138,14 @@
     body_rows = pay_ref.shape[1] - TAIL
     parts = encode_row(scal)
     scal = decode_row(parts)
-    frob = lane_pick(scal, 2 * domains)
     scale = jnp.where(frob > TINY, HALF_SPAN / jnp.maximum(frob, TINY), 0.0)
     row_id = lax.broadcasted_iota(jnp.int32, (BLOCK, BLOCK), 0)
     col_id = lax.broadcasted_iota(jnp.int32, (BLOCK, BLOCK), 1)
 
     def part(i, j):
-        value = gram[i * BLOCK : (i + 1) * BLOCK, j * BLOCK : (j + 1) * BLOCK]
+        source, shift = (gram_top, 0) if i * BLOCK < half_width else (gram_low, half_width)
+        row, column = i * BLOCK - shift, j * BLOCK - shift
+        value = source[row : row + BLOCK, column : column + BLOCK]
         if stage:
             value = value + sofar_ref[pl.ds(i * BLOCK, BLOCK), pl.ds(j * BLOCK, BLOCK)]
         return value
@@ -184,9 +193,9 @@
         every = tree_sum(
             [row(own_ref, 2)] + [decode_row([row(ref, 5 + n) for n in range(4)]) for ref in got]
         )
+    frob = lane_pick(scal, scalar_lane)
     parts, every_parts = encode_row(scal), encode_row(every)
     scal, every = decode_row(parts), decode_row(every_parts)
-    frob = lane_pick(scal, scalar_lane)
     scale = jnp.where(frob > TINY, HALF_SPAN / jnp.maximum(frob, TINY), 0.0)
     out_ref[pl.ds(0, body_rows), :] = value
     out_ref[pl.ds(body_rows, TAIL), :] = tail_rows([diag, scal, every])
@@ -197,7 +206,7 @@
 def newton_kernel(scalar_lane, lanes, pos_ref, own_ref, *refs):
     got, refs = refs[: SQUARE - 1], refs[SQUARE - 1 :]
     combs, refs = refs[: lanes - 1], refs[lanes - 1 :]
-    away_ref, poly_ref, inv_ref, piece_ref, diag_ref, gram_ref, start_ref = refs
+    away_ref, poly_ref, inv_ref, piece_ref, diag_ref, gram_ref, start_ref, near_ref = refs
     quad = pos_ref[1]
     body_rows = own_ref.shape[0] - TAIL
     rows, columns = combs[0].shape
@@ -239,21 +248,47 @@
     inv_ref[...] = jnp.broadcast_to(inv, inv_ref.shape)
     for n, ref in enumerate(combs):
         start_ref[pl.ds(n * rows, rows), :] = (ref[...] * inv).astype(jnp.bfloat16)
-    gram = gram_ref[...]
+    half_width = columns // 2
+    top, low = pl.ds(0, half_width), pl.ds(half_width, half_width)
     iterate = start_ref[...]
+    gram_top, gram_low = gram_ref[top, :], gram_ref[low, low]
     for step in range(NS_ITERS):
-        gram_low = gram.astype(jnp.bfloat16)
-        square = dot(gram_low, gram_low)
-        poly = (COEF_B * gram + COEF_C * square).astype(jnp.bfloat16)
-        poly_ref[step] = poly
-        iterate = newton_rows(iterate, poly)
+        mirror(near_ref.at[step], gram_top.astype(jnp.bfloat16), gram_low.astype(jnp.bfloat16))
+        near = near_ref[step]
+        square_top = dot(near[:half_width], near)
+        square_low = dot(near[half_width:], near[:, half_width:])
+        mirror(
+            poly_ref.at[step],
+            (COEF_B * gram_top + COEF_C * square_top).astype(jnp.bfloat16),
+            (COEF_B * gram_low + COEF_C * square_low).astype(jnp.bfloat16),
+        )
+        if step:
+            iterate = newton_rows(iterate, poly)
+        poly = poly_ref[step]
         if step + 1 == NS_ITERS:
-            away_ref[...] = iterate
+            away_ref[...] = newton_rows(iterate, poly)
             return
-        half = COEF_A * gram + dot(gram_low, poly)
-        half_high = half.astype(jnp.bfloat16)
-        half_low = (half - half_high.astype(F32)).astype(jnp.bfloat16)
-        gram = COEF_A * half + dot(poly, half_high) + dot(poly, half_low)
+        moved = dot(near, poly)
+        left = gram_top[:, half_width:].T
+        half_top = COEF_A * gram_top + moved[:half_width]
+        half_low = COEF_A * jnp.concatenate([left, gram_low], axis=1) + moved[half_width:]
+        half = jnp.concatenate([half_top, half_low], axis=0)
+        high = half.astype(jnp.bfloat16)
+        rest = (half - high.astype(F32)).astype(jnp.bfloat16)
+        gram_top = COEF_A * half_top + dot(poly[:half_width], high) + dot(poly[:half_width], rest)
+        gram_low = (
+            COEF_A * half_low[:, half_width:]
+            + dot(poly[half_width:], high[:, half_width:])
+            + dot(poly[half_width:], rest[:, half_width:])
+        )
+
+
+def mirror(ref, top_value, low_value):
+    half_width = low_value.shape[0]
+    top, low = pl.ds(0, half_width), pl.ds(half_width, half_width)
+    ref[top, :] = top_value
+    ref[low, top] = top_value[:, half_width:].T
+    ref[low, low] = low_value
 
 
 def newton_rows(iterate, poly):
@@ -447,8 +482,9 @@
         + [
             pltpu.VMEM((columns, columns), F32),
             pltpu.VMEM(((lanes - 1) * rows, columns), jnp.bfloat16),
+            pltpu.VMEM((NS_ITERS, columns, columns), jnp.bfloat16),
         ],
-        flops=10 * 2 * columns**3,
+        flops=9 * 2 * columns**3,
     )
     away = away.reshape(lanes - 1, rows, columns)
     returned = [exchange(away[k - 1], k) for k in range(1, lanes)]

time: 46.8 us -> 46.4 us (level)
  Pallas kernels: 8.35 us -> 7.88 us
where the time goes in v7:
time: 46.4 us; the launch traced here: 45.9 us
  starting transfers between devices  16.2 us (35%)
  waiting for transfers between devices  13.7 us (30%)
  Pallas kernels  7.88 us (17%)
  other arithmetic  3.71 us (8%)
  local copies, waits for them, and re-layouts  3.49 us (8%)
  between operations  0.91 us (2%)
    ppermute x13, starting transfers between devices, exchange(): lax.ppermute(value, AXES, [(i, i ^ mask) for i in range(domains * shards)])  16.2 us
    ppermute x13, waiting for transfers between devices, exchange(): lax.ppermute(value, AXES, [(i, i ^ mask) for i in range(domains * shards)])  13.7 us
    pallas_call x8, Pallas kernels, call(): pl.pallas_call(kernel, out_shape=tuple(out_shape), in_specs=[pl.BlockSpec...  7.88 us
    unnamed x8, local copies, waits for them, and re-layouts  1.24 us
    mul x1, other arithmetic, body(): jnp.stack(ordered).astype(F32) * (MUON_SCALE * math.sqrt(full_rows))  1.11 us
    squeeze x1, local copies, waits for them, and re-layouts, body(): lax.dynamic_index_in_dim(gradients[0], member ^ order[0], 0, keepdims=False)  0.97 us
  transfers between devices with their start and end apart: 13, of which 8 were waited for; matrix products, arithmetic and copies ran while one was open for 8% of the time, Pallas kernels for 6%

profile of v7, /device:TPU:1, one launch (start us, length us, event | category | flops | bytes accessed | tf_op | source)
XLA Modules:
  0.0 45.9 jit_solution(7008534930801577895)
XLA Ops:
  0.7 1.0 %dynamic-slice_bitcast_fusion = bf16[256,512]{1,0:T(8,128)(2,1)S(1)} fusion(bf16[1,4,256,512]{3,2,1,0:T(8,128)(2,1)} %param.4, s32[]{:T(128)S(6)} %select_n.63), kind=kLoop, calls=%fused_computation.4 | loop fusion | bytes 524292 | tf_op jit(solution)/shard_map/jit(dynamic_index_in_dim)/squeeze | solution.py:383
  1.7 2.1 %collective-permute-start = (bf16[256,512]{1,0:T(8,128)(2,1)S(1)}, bf16[256,512]{1,0:T(8,128)(2,1)S(1)}, u32[]{:S(2)}, u32[]{:S(2)}) collective-permute-start(bf16[256,512]{1,0:T(8,128)(2,1)S(1)} %dynamic-slice_bitcast_fusion), channel_id=1, source_target_pairs={{0,16},{1,17},{2,18},{3,19},{4,20},{5,21},{6,22},{7,23},{8,24},{9,... | collective-permute-start | bytes 786440 | tf_op jit(solution)/shard_map/ppermute | solution.py:366
  3.8 1.2 %copy-done = bf16[1,4,256,512]{3,2,1,0:T(8,128)(2,1)S(1)} copy-done((bf16[1,4,256,512]{3,2,1,0:T(8,128)(2,1)S(1)}, bf16[1,4,256,512]{3,2,1,0:T(8,128)(2,1)}, u32[]{:S(2)}) %copy-start) | copy-done | bytes 1048600
  5.1 0.6 %shard_map.59 = (bf16[256,512]{1,0:T(8,128)(2,1)S(1)}, bf16[256,512]{1,0:T(8,128)(2,1)S(1)}, bf16[256,512]{1,0:T(8,128)(2,1)S(1)}) custom-call(s32[3]{0:T(128)S(1)} %pad_add_fusion.1.index_ref, bf16[4,256,512]{2,1,0:T(8,128)(2,1)S(1)} %bitcast.30), custom_call_target="tpu_custom_call" | custom-call | bytes 1835020 | tf_op jit(solution)/shard_map/pallas_call | solution.py:334
  5.7 1.0 %collective-permute-start.1 = (bf16[256,512]{1,0:T(8,128)(2,1)S(1)}, bf16[256,512]{1,0:T(8,128)(2,1)S(1)}, u32[]{:S(2)}, u32[]{:S(2)}) collective-permute-start(bf16[256,512]{1,0:T(8,128)(2,1)S(1)} %get-tuple-element.21), channel_id=1, source_target_pairs={{0,1},{1,0},{2,3},{3,2},{4,5},{5,4},{6,7},{7,6},{8,9},{9,8},{10,11... | collective-permute-start | bytes 786440 | tf_op jit(solution)/shard_map/ppermute | solution.py:366
  6.8 0.6 %reduce_sum.27 = f32[]{:T(128)} reduce(f32[8]{0:T(128)S(1)} %copy-done.1, f32[]{:T(128)} %constant.69.clone.1), dimensions={0}, to_apply=%region_0.1 | reduce | flops 7 | bytes 40 | tf_op jit(solution)/shard_map/reduce_sum | solution.py:30
  7.4 0.7 %divide_bitcast_fusion = (f32[1,8]{1,0:T(1,128)S(1)}, f32[8]{0:T(128)S(1)}) fusion(f32[8]{0:T(128)S(1)} %copy-done.1, f32[]{:T(128)} %reduce_sum.27, f32[8]{0:T(128)S(1)} %fusion.2), kind=kLoop, calls=%fused_computation.20 | loop fusion | flops 32 | bytes 132 | tf_op jit(solution)/shard_map/broadcast_in_dim | solution.py:495
  8.1 0.2 select_reduce_fusion
  8.3 0.6 %dynamic_slice.8 = s32[1]{0:T(128)} dynamic-slice(s32[4]{0:T(128)S(1)} %copy-done.2, s32[]{:T(128)S(6)} %select_n.60), dynamic_slice_sizes={1} | dynamic-slice | bytes 12 | tf_op jit(solution)/shard_map/jit(dynamic_index_in_dim)/dynamic_slice | solution.py:406
  8.9 0.7 %multiply_subtract_fusion.lim_ref = s32[2]{0:T(128)S(1)} fusion(s32[]{:T(128)} %select_n.55, s32[]{:T(128)S(6)} %mul.26, s32[]{:T(128)} %bitcast.1), kind=kLoop, calls=%fused_computation.21 | loop fusion | flops 8 | bytes 20 | tf_op jit(solution)/shard_map/sub | solution.py:406
  9.6 0.6 %gather_fusion = f32[2]{0:T(128)S(1)} fusion(f32[2]{0:T(128)S(1)} %select_reduce_fusion, s32[1024]{0:T(1024)S(1)} %pad_clamp_fusion), kind=kCustom, calls=%fused_computation | custom fusion | bytes 24 | tf_op jit(solution)/shard_map/jit(_take)/gather | solution.py:404
  10.3 1.0 %shard_map.60 = (f32[256,512]{1,0:T(8,128)S(1)}, f32[512,512]{1,0:T(8,128)S(1)}, f32[8,128]{1,0:T(8,128)S(1)}) custom-call(f32[2]{0:T(128)S(1)} %and_select_fusion.mix_ref, s32[2]{0:T(128)S(1)} %multiply_subtract_fusion.lim_ref, s32[3]{0:T(128)S(1)} %pad_add_fusion.pos_ref, bf16[256,512]{1,0:T(8,128)(2,1)S(1)} %get-tuple-element.19.refs_0_, ...), custom_call_target="tpu_custom_call" | custom-call | flops 134217728 | bytes 2101276 | tf_op jit(solution)/shard_map/pallas_call | solution.py:334
  11.2 4.7 %collective-permute-done.2.refs_1_ = bf16[256,512]{1,0:T(8,128)(2,1)S(1)} collective-permute-done((bf16[256,512]{1,0:T(8,128)(2,1)S(1)}, bf16[256,512]{1,0:T(8,128)(2,1)S(1)}, u32[]{:S(2)}, u32[]{:S(2)}) %collective-permute-start.2) | collective-permute-done | bytes 262176 | tf_op jit(solution)/shard_map/ppermute | solution.py:366
  15.9 1.0 %shard_map.61 = (f32[256,512]{1,0:T(8,128)S(1)}, f32[4,272,128]{2,1,0:T(8,128)S(1)}) custom-call(f32[2]{0:T(128)S(1)} %and_select_fusion.mix_ref, s32[2]{0:T(128)S(1)} %multiply_subtract_fusion.lim_ref, s32[3]{0:T(128)S(1)} %pad_add_fusion.pos_ref, bf16[256,512]{1,0:T(8,128)(2,1)S(1)} %collective-permute-done.1.refs_0_, ...), custom_call_target="tpu_custom_call" | custom-call | flops 134217728 | bytes 2658332 | tf_op jit(solution)/shard_map/pallas_call | solution.py:334
  17.1 1.6 %collective-permute-start.3 = (f16[272,128]{1,0:T(8,128)(2,1)S(1)}, f16[272,128]{1,0:T(8,128)(2,1)S(1)}, u32[]{:S(2)}, u32[]{:S(2)}) collective-permute-start(f16[272,128]{1,0:T(8,128)(2,1)S(1)} %get-tuple-element.40), channel_id=1, source_target_pairs={{0,2},{1,3},{2,0},{3,1},{4,6},{5,7},{6,4},{7,5},{8,10},{9,11},{10,... | collective-permute-start | bytes 208904 | tf_op jit(solution)/shard_map/ppermute | solution.py:366
  18.6 1.3 %collective-permute-start.4 = (f16[272,128]{1,0:T(8,128)(2,1)S(1)}, f16[272,128]{1,0:T(8,128)(2,1)S(1)}, u32[]{:S(2)}, u32[]{:S(2)}) collective-permute-start(f16[272,128]{1,0:T(8,128)(2,1)S(1)} %get-tuple-element.39), channel_id=1, source_target_pairs={{0,4},{1,5},{2,6},{3,7},{4,0},{5,1},{6,2},{7,3},{8,12},{9,13},{10,... | collective-permute-start | bytes 208904 | tf_op jit(solution)/shard_map/ppermute | solution.py:366
  19.9 1.3 %collective-permute-start.6 = (f32[8,128]{1,0:T(8,128)S(1)}, f32[8,128]{1,0:T(8,128)S(1)}, u32[]{:S(2)}, u32[]{:S(2)}) collective-permute-start(f32[8,128]{1,0:T(8,128)S(1)} %slice_bitcast_fusion.4.refs_4_), channel_id=1, source_target_pairs={{0,16},{1,17},{2,18},{3,19},{4,20},{5,21},{6,22},{7,23},{8,24},{9,... | collective-permute-start | bytes 12296 | tf_op jit(solution)/shard_map/ppermute | solution.py:366
  21.3 1.1 %collective-permute-done.4 = f16[272,128]{1,0:T(8,128)(2,1)S(1)} collective-permute-done((f16[272,128]{1,0:T(8,128)(2,1)S(1)}, f16[272,128]{1,0:T(8,128)(2,1)S(1)}, u32[]{:S(2)}, u32[]{:S(2)}) %collective-permute-start.4) | collective-permute-done | bytes 69664 | tf_op jit(solution)/shard_map/ppermute | solution.py:366
  22.4 1.9 %collective-permute-done.5 = f16[272,128]{1,0:T(8,128)(2,1)S(1)} collective-permute-done((f16[272,128]{1,0:T(8,128)(2,1)S(1)}, f16[272,128]{1,0:T(8,128)(2,1)S(1)}, u32[]{:S(2)}, u32[]{:S(2)}) %collective-permute-start.5) | collective-permute-done | bytes 69664 | tf_op jit(solution)/shard_map/ppermute | solution.py:366
  24.3 0.1 shard_map.62
  24.5 2.4 %collective-permute-start.7 = (f16[272,128]{1,0:T(8,128)(2,1)S(1)}, f16[272,128]{1,0:T(8,128)(2,1)S(1)}, u32[]{:S(2)}, u32[]{:S(2)}) collective-permute-start(f16[272,128]{1,0:T(8,128)(2,1)S(1)} %convert_element_type.54), channel_id=1, source_target_pairs={{0,8},{1,9},{2,10},{3,11},{4,12},{5,13},{6,14},{7,15},{8,0},{9,1},... | collective-permute-start | bytes 208904 | tf_op jit(solution)/shard_map/ppermute | solution.py:366
  26.9 2.5 %collective-permute-done.7 = f16[272,128]{1,0:T(8,128)(2,1)S(1)} collective-permute-done((f16[272,128]{1,0:T(8,128)(2,1)S(1)}, f16[272,128]{1,0:T(8,128)(2,1)S(1)}, u32[]{:S(2)}, u32[]{:S(2)}) %collective-permute-start.7) | collective-permute-done | bytes 69664 | tf_op jit(solution)/shard_map/ppermute | solution.py:366
  29.4 0.1 shard_map.63
  29.6 1.4 %collective-permute-start.9 = (f16[272,128]{1,0:T(8,128)(2,1)S(1)}, f16[272,128]{1,0:T(8,128)(2,1)S(1)}, u32[]{:S(2)}, u32[]{:S(2)}) collective-permute-start(f16[272,128]{1,0:T(8,128)(2,1)S(1)} %convert_element_type.56), channel_id=1, source_target_pairs={{0,4},{1,5},{2,6},{3,7},{4,0},{5,1},{6,2},{7,3},{8,12},{9,13},{10,... | collective-permute-start | bytes 208904 | tf_op jit(solution)/shard_map/ppermute | solution.py:366
  31.0 1.2 %collective-permute-start.10 = (f16[272,128]{1,0:T(8,128)(2,1)S(1)}, f16[272,128]{1,0:T(8,128)(2,1)S(1)}, u32[]{:S(2)}, u32[]{:S(2)}) collective-permute-start(f16[272,128]{1,0:T(8,128)(2,1)S(1)} %convert_element_type.56), channel_id=1, source_target_pairs={{0,6},{1,7},{2,4},{3,5},{4,2},{5,3},{6,0},{7,1},{8,14},{9,15},{10,... | collective-permute-start | bytes 208904 | tf_op jit(solution)/shard_map/ppermute | solution.py:366
  32.2 0.5 %collective-permute-done.8 = f16[272,128]{1,0:T(8,128)(2,1)S(1)} collective-permute-done((f16[272,128]{1,0:T(8,128)(2,1)S(1)}, f16[272,128]{1,0:T(8,128)(2,1)S(1)}, u32[]{:S(2)}, u32[]{:S(2)}) %collective-permute-start.8) | collective-permute-done | bytes 69664 | tf_op jit(solution)/shard_map/ppermute | solution.py:366
  32.8 2.3 %collective-permute-done.10 = f16[272,128]{1,0:T(8,128)(2,1)S(1)} collective-permute-done((f16[272,128]{1,0:T(8,128)(2,1)S(1)}, f16[272,128]{1,0:T(8,128)(2,1)S(1)}, u32[]{:S(2)}, u32[]{:S(2)}) %collective-permute-start.10) | collective-permute-done | bytes 69664 | tf_op jit(solution)/shard_map/ppermute | solution.py:366
  35.1 3.9 %shard_map.64 = (bf16[256,512]{1,0:T(8,128)(2,1)S(1)}, bf16[3,512,512]{2,1,0:T(8,128)(2,1)S(1)}, f32[8,128]{1,0:T(8,128)S(1)}) custom-call(s32[3]{0:T(128)S(1)} %pad_add_fusion.pos_ref, f32[272,128]{1,0:T(8,128)S(1)} %get-tuple-element.28.own_ref, f32[272,128]{1,0:T(8,128)S(1)} %convert_element_type.57.refs_0_, f32[272,128]{1,0:T(8,128)S(1)} %convert_element_type.58.refs_1_, ...), custom_call_target="tpu_custom_call" | custom-call | flops 2415919104 | bytes 2920460 | tf_op jit(solution)/shard_map/pallas_call | solution.py:334
  39.0 3.7 %collective-permute-start.11 = (f32[8,128]{1,0:T(8,128)S(1)}, f32[8,128]{1,0:T(8,128)S(1)}, u32[]{:S(2)}, u32[]{:S(2)}) collective-permute-start(f32[8,128]{1,0:T(8,128)S(1)} %shard_map.65.refs_0_), channel_id=1, source_target_pairs={{0,1},{1,0},{2,3},{3,2},{4,5},{5,4},{6,7},{7,6},{8,9},{9,8},{10,11... | collective-permute-start | bytes 12296 | tf_op jit(solution)/shard_map/ppermute | solution.py:366
  42.9 0.7 %collective-permute-done.11.refs_1_ = f32[8,128]{1,0:T(8,128)S(1)} collective-permute-done((f32[8,128]{1,0:T(8,128)S(1)}, f32[8,128]{1,0:T(8,128)S(1)}, u32[]{:S(2)}, u32[]{:S(2)}) %collective-permute-start.11) | collective-permute-done | bytes 4128 | tf_op jit(solution)/shard_map/ppermute | solution.py:366
  43.6 1.1 %shard_map.66 = (bf16[256,512]{1,0:T(8,128)(2,1)S(1)}, f32[1,8]{1,0:T(1,128)}) custom-call(f32[256,512]{1,0:T(8,128)S(1)} %get-tuple-element.20.comb_ref, f32[8,128]{1,0:T(8,128)S(1)} %get-tuple-element.31.inv_ref, bf16[3,512,512]{2,1,0:T(8,128)(2,1)S(1)} %get-tuple-element.32.poly_ref, f32[8,128]{1,0:T(8,128)S(1)} %shard_map.65.refs_0_, ...), custom_call_target="tpu_custom_call" | custom-call | flops 402653184 | bytes 2371744 | tf_op jit(solution)/shard_map/pallas_call | solution.py:334
  44.8 1.1 %convert_multiply_fusion = f32[2,256,512]{2,1,0:T(8,128)} fusion(bf16[1,256,512]{2,1,0:T(8,128)(2,1)S(1)} %get-tuple-element.37, bf16[1,256,512]{2,1,0:T(8,128)(2,1)S(1)} %get-tuple-element.36), kind=kLoop, calls=%fused_computation.1 | loop fusion | flops 786432 | bytes 1572864 | tf_op jit(solution)/shard_map/mul | solution.py:514
  (39 shorter events, 0.8 us)
Async XLA Ops:
  0.6 6.1 %copy-start.3 = (s32[2]{0:T(128)S(1)}, s32[2]{0:T(128)}, u32[]{:S(2)}) copy-start(s32[2]{0:T(128)} %param.6) | copy-start | bytes 28
  0.6 6.2 %copy-start.1 = (f32[8]{0:T(128)S(1)}, f32[8]{0:T(128)}, u32[]{:S(2)}) copy-start(f32[8]{0:T(128)} %param.7) | copy-start | bytes 100
  0.7 7.6 %copy-start.2 = (s32[4]{0:T(128)S(1)}, s32[4]{0:T(128)}, u32[]{:S(2)}) copy-start(s32[4]{0:T(128)} %param.5) | copy-start | bytes 52
  1.7 8.6 %collective-permute-start = (bf16[256,512]{1,0:T(8,128)(2,1)S(1)}, bf16[256,512]{1,0:T(8,128)(2,1)S(1)}, u32[]{:S(2)}, u32[]{:S(2)}) collective-permute-start(bf16[256,512]{1,0:T(8,128)(2,1)S(1)} %dynamic-slice_bitcast_fusion), channel_id=1, source_target_pairs={{0,16},{1,17},{2,18},{3,19},{4,20},{5,21},{6,22},{7,23},{8,24},{9,... | collective-permute-start | bytes 786440 | tf_op jit(solution)/shard_map/ppermute | solution.py:366
  3.8 1.2 %copy-start = (bf16[1,4,256,512]{3,2,1,0:T(8,128)(2,1)S(1)}, bf16[1,4,256,512]{3,2,1,0:T(8,128)(2,1)}, u32[]{:S(2)}) copy-start(bf16[1,4,256,512]{3,2,1,0:T(8,128)(2,1)} %param.4) | copy-start | bytes 3145732
  5.7 5.5 %collective-permute-start.1 = (bf16[256,512]{1,0:T(8,128)(2,1)S(1)}, bf16[256,512]{1,0:T(8,128)(2,1)S(1)}, u32[]{:S(2)}, u32[]{:S(2)}) collective-permute-start(bf16[256,512]{1,0:T(8,128)(2,1)S(1)} %get-tuple-element.21), channel_id=1, source_target_pairs={{0,1},{1,0},{2,3},{3,2},{4,5},{5,4},{6,7},{7,6},{8,9},{9,8},{10,11... | collective-permute-start | bytes 786440 | tf_op jit(solution)/shard_map/ppermute | solution.py:366
  6.7 9.2 %collective-permute-start.2 = (bf16[256,512]{1,0:T(8,128)(2,1)S(1)}, bf16[256,512]{1,0:T(8,128)(2,1)S(1)}, u32[]{:S(2)}, u32[]{:S(2)}) collective-permute-start(bf16[256,512]{1,0:T(8,128)(2,1)S(1)} %get-tuple-element.22), channel_id=1, source_target_pairs={{0,17},{1,16},{2,19},{3,18},{4,21},{5,20},{6,23},{7,22},{8,25},{9,... | collective-permute-start | bytes 786440 | tf_op jit(solution)/shard_map/ppermute | solution.py:366
  17.1 4.2 %collective-permute-start.3 = (f16[272,128]{1,0:T(8,128)(2,1)S(1)}, f16[272,128]{1,0:T(8,128)(2,1)S(1)}, u32[]{:S(2)}, u32[]{:S(2)}) collective-permute-start(f16[272,128]{1,0:T(8,128)(2,1)S(1)} %get-tuple-element.40), channel_id=1, source_target_pairs={{0,2},{1,3},{2,0},{3,1},{4,6},{5,7},{6,4},{7,5},{8,10},{9,11},{10,... | collective-permute-start | bytes 208904 | tf_op jit(solution)/shard_map/ppermute | solution.py:366
  18.6 3.8 %collective-permute-start.4 = (f16[272,128]{1,0:T(8,128)(2,1)S(1)}, f16[272,128]{1,0:T(8,128)(2,1)S(1)}, u32[]{:S(2)}, u32[]{:S(2)}) collective-permute-start(f16[272,128]{1,0:T(8,128)(2,1)S(1)} %get-tuple-element.39), channel_id=1, source_target_pairs={{0,4},{1,5},{2,6},{3,7},{4,0},{5,1},{6,2},{7,3},{8,12},{9,13},{10,... | collective-permute-start | bytes 208904 | tf_op jit(solution)/shard_map/ppermute | solution.py:366
  19.9 4.4 %collective-permute-start.5 = (f16[272,128]{1,0:T(8,128)(2,1)S(1)}, f16[272,128]{1,0:T(8,128)(2,1)S(1)}, u32[]{:S(2)}, u32[]{:S(2)}) collective-permute-start(f16[272,128]{1,0:T(8,128)(2,1)S(1)} %get-tuple-element.38), channel_id=1, source_target_pairs={{0,6},{1,7},{2,4},{3,5},{4,2},{5,3},{6,0},{7,1},{8,14},{9,15},{10,... | collective-permute-start | bytes 208904 | tf_op jit(solution)/shard_map/ppermute | solution.py:366
  19.9 4.4 %collective-permute-start.6 = (f32[8,128]{1,0:T(8,128)S(1)}, f32[8,128]{1,0:T(8,128)S(1)}, u32[]{:S(2)}, u32[]{:S(2)}) collective-permute-start(f32[8,128]{1,0:T(8,128)S(1)} %slice_bitcast_fusion.4.refs_4_), channel_id=1, source_target_pairs={{0,16},{1,17},{2,18},{3,19},{4,20},{5,21},{6,22},{7,23},{8,24},{9,... | collective-permute-start | bytes 12296 | tf_op jit(solution)/shard_map/ppermute | solution.py:366
  24.5 4.9 %collective-permute-start.7 = (f16[272,128]{1,0:T(8,128)(2,1)S(1)}, f16[272,128]{1,0:T(8,128)(2,1)S(1)}, u32[]{:S(2)}, u32[]{:S(2)}) collective-permute-start(f16[272,128]{1,0:T(8,128)(2,1)S(1)} %convert_element_type.54), channel_id=1, source_target_pairs={{0,8},{1,9},{2,10},{3,11},{4,12},{5,13},{6,14},{7,15},{8,0},{9,1},... | collective-permute-start | bytes 208904 | tf_op jit(solution)/shard_map/ppermute | solution.py:366
  29.5 3.2 %collective-permute-start.8 = (f16[272,128]{1,0:T(8,128)(2,1)S(1)}, f16[272,128]{1,0:T(8,128)(2,1)S(1)}, u32[]{:S(2)}, u32[]{:S(2)}) collective-permute-start(f16[272,128]{1,0:T(8,128)(2,1)S(1)} %convert_element_type.56), channel_id=1, source_target_pairs={{0,2},{1,3},{2,0},{3,1},{4,6},{5,7},{6,4},{7,5},{8,10},{9,11},{10,... | collective-permute-start | bytes 208904 | tf_op jit(solution)/shard_map/ppermute | solution.py:366
  29.6 3.2 %collective-permute-start.9 = (f16[272,128]{1,0:T(8,128)(2,1)S(1)}, f16[272,128]{1,0:T(8,128)(2,1)S(1)}, u32[]{:S(2)}, u32[]{:S(2)}) collective-permute-start(f16[272,128]{1,0:T(8,128)(2,1)S(1)} %convert_element_type.56), channel_id=1, source_target_pairs={{0,4},{1,5},{2,6},{3,7},{4,0},{5,1},{6,2},{7,3},{8,12},{9,13},{10,... | collective-permute-start | bytes 208904 | tf_op jit(solution)/shard_map/ppermute | solution.py:366
  31.0 4.1 %collective-permute-start.10 = (f16[272,128]{1,0:T(8,128)(2,1)S(1)}, f16[272,128]{1,0:T(8,128)(2,1)S(1)}, u32[]{:S(2)}, u32[]{:S(2)}) collective-permute-start(f16[272,128]{1,0:T(8,128)(2,1)S(1)} %convert_element_type.56), channel_id=1, source_target_pairs={{0,6},{1,7},{2,4},{3,5},{4,2},{5,3},{6,0},{7,1},{8,14},{9,15},{10,... | collective-permute-start | bytes 208904 | tf_op jit(solution)/shard_map/ppermute | solution.py:366
  39.0 4.5 %collective-permute-start.11 = (f32[8,128]{1,0:T(8,128)S(1)}, f32[8,128]{1,0:T(8,128)S(1)}, u32[]{:S(2)}, u32[]{:S(2)}) collective-permute-start(f32[8,128]{1,0:T(8,128)S(1)} %shard_map.65.refs_0_), channel_id=1, source_target_pairs={{0,1},{1,0},{2,3},{3,2},{4,5},{5,4},{6,7},{7,6},{8,9},{9,8},{10,11... | collective-permute-start | bytes 12296 | tf_op jit(solution)/shard_map/ppermute | solution.py:366
  42.7 1.9 %collective-permute-start.12 = (bf16[256,512]{1,0:T(8,128)(2,1)S(1)}, bf16[256,512]{1,0:T(8,128)(2,1)S(1)}, u32[]{:S(2)}, u32[]{:S(2)}) collective-permute-start(bf16[256,512]{1,0:T(8,128)(2,1)S(1)} %get-tuple-element.34), channel_id=1, source_target_pairs={{0,1},{1,0},{2,3},{3,2},{4,5},{5,4},{6,7},{7,6},{8,9},{9,8},{10,11... | collective-permute-start | bytes 786440 | tf_op jit(solution)/shard_map/ppermute | solution.py:366

commit v8 on v7

--- a/solution.py
+++ b/solution.py
@@ -206,7 +206,7 @@
 def newton_kernel(scalar_lane, lanes, pos_ref, own_ref, *refs):
     got, refs = refs[: SQUARE - 1], refs[SQUARE - 1 :]
     combs, refs = refs[: lanes - 1], refs[lanes - 1 :]
-    away_ref, poly_ref, inv_ref, piece_ref, diag_ref, gram_ref, start_ref, near_ref = refs
+    away_ref, poly_ref, inv_ref, piece_ref, diag_ref, gram_ref, start_ref = refs
     quad = pos_ref[1]
     body_rows = own_ref.shape[0] - TAIL
     rows, columns = combs[0].shape
@@ -251,44 +251,31 @@
     half_width = columns // 2
     top, low = pl.ds(0, half_width), pl.ds(half_width, half_width)
     iterate = start_ref[...]
-    gram_top, gram_low = gram_ref[top, :], gram_ref[low, low]
+    gram = gram_ref[...]
     for step in range(NS_ITERS):
-        mirror(near_ref.at[step], gram_top.astype(jnp.bfloat16), gram_low.astype(jnp.bfloat16))
-        near = near_ref[step]
-        square_top = dot(near[:half_width], near)
-        square_low = dot(near[half_width:], near[:, half_width:])
-        mirror(
-            poly_ref.at[step],
-            (COEF_B * gram_top + COEF_C * square_top).astype(jnp.bfloat16),
-            (COEF_B * gram_low + COEF_C * square_low).astype(jnp.bfloat16),
-        )
+        near = gram.astype(jnp.bfloat16)
         if step:
             iterate = newton_rows(iterate, poly)
-        poly = poly_ref[step]
+        poly = (COEF_B * gram + COEF_C * dot(near, near)).astype(jnp.bfloat16)
+        poly_ref[step] = poly
         if step + 1 == NS_ITERS:
             away_ref[...] = newton_rows(iterate, poly)
             return
-        moved = dot(near, poly)
-        left = gram_top[:, half_width:].T
-        half_top = COEF_A * gram_top + moved[:half_width]
-        half_low = COEF_A * jnp.concatenate([left, gram_low], axis=1) + moved[half_width:]
-        half = jnp.concatenate([half_top, half_low], axis=0)
+        half = COEF_A * gram + dot(near, poly)
         high = half.astype(jnp.bfloat16)
         rest = (half - high.astype(F32)).astype(jnp.bfloat16)
-        gram_top = COEF_A * half_top + dot(poly[:half_width], high) + dot(poly[:half_width], rest)
-        gram_low = (
-            COEF_A * half_low[:, half_width:]
+        gram_ref[top, :] = (
+            COEF_A * half[:half_width]
+            + dot(poly[:half_width], high)
+            + dot(poly[:half_width], rest)
+        )
+        gram_ref[low, low] = (
+            COEF_A * half[half_width:, half_width:]
             + dot(poly[half_width:], high[:, half_width:])
             + dot(poly[half_width:], rest[:, half_width:])
         )
-
-
-def mirror(ref, top_value, low_value):
-    half_width = low_value.shape[0]
-    top, low = pl.ds(0, half_width), pl.ds(half_width, half_width)
-    ref[top, :] = top_value
-    ref[low, top] = top_value[:, half_width:].T
-    ref[low, low] = low_value
+        gram_ref[low, top] = gram_ref[top, low].T
+        gram = gram_ref[...]
 
 
 def newton_rows(iterate, poly):
@@ -482,7 +469,6 @@
         + [
             pltpu.VMEM((columns, columns), F32),
             pltpu.VMEM(((lanes - 1) * rows, columns), jnp.bfloat16),
-            pltpu.VMEM((NS_ITERS, columns, columns), jnp.bfloat16),
         ],
         flops=9 * 2 * columns**3,
     )

time: 46.4 us -> 46.4 us (level)
  no operation moved by 1% of the time
where the time goes in v8:
time: 46.4 us; the launch traced here: 45.8 us
  starting transfers between devices  16.2 us (35%)
  waiting for transfers between devices  13.7 us (30%)
  Pallas kernels  7.86 us (17%)
  other arithmetic  3.71 us (8%)
  local copies, waits for them, and re-layouts  3.49 us (8%)
  between operations  0.91 us (2%)
    ppermute x13, starting transfers between devices, exchange(): lax.ppermute(value, AXES, [(i, i ^ mask) for i in range(domains * shards)])  16.2 us
    ppermute x13, waiting for transfers between devices, exchange(): lax.ppermute(value, AXES, [(i, i ^ mask) for i in range(domains * shards)])  13.7 us
    pallas_call x8, Pallas kernels, call(): pl.pallas_call(kernel, out_shape=tuple(out_shape), in_specs=[pl.BlockSpec...  7.86 us
    unnamed x8, local copies, waits for them, and re-layouts  1.24 us
    mul x1, other arithmetic, body(): jnp.stack(ordered).astype(F32) * (MUON_SCALE * math.sqrt(full_rows))  1.11 us
    squeeze x1, local copies, waits for them, and re-layouts, body(): lax.dynamic_index_in_dim(gradients[0], member ^ order[0], 0, keepdims=False)  0.97 us
  transfers between devices with their start and end apart: 13, of which 8 were waited for; matrix products, arithmetic and copies ran while one was open for 8% of the time, Pallas kernels for 6%

profile of v8, /device:TPU:1, one launch (start us, length us, event | category | flops | bytes accessed | tf_op | source)
XLA Modules:
  0.0 45.8 jit_solution(9196863441434341450)
XLA Ops:
  0.7 1.0 %dynamic-slice_bitcast_fusion = bf16[256,512]{1,0:T(8,128)(2,1)S(1)} fusion(bf16[1,4,256,512]{3,2,1,0:T(8,128)(2,1)} %param.4, s32[]{:T(128)S(6)} %select_n.63), kind=kLoop, calls=%fused_computation.4 | loop fusion | bytes 524292 | tf_op jit(solution)/shard_map/jit(dynamic_index_in_dim)/squeeze | solution.py:370
  1.7 2.1 %collective-permute-start = (bf16[256,512]{1,0:T(8,128)(2,1)S(1)}, bf16[256,512]{1,0:T(8,128)(2,1)S(1)}, u32[]{:S(2)}, u32[]{:S(2)}) collective-permute-start(bf16[256,512]{1,0:T(8,128)(2,1)S(1)} %dynamic-slice_bitcast_fusion), channel_id=1, source_target_pairs={{0,16},{1,17},{2,18},{3,19},{4,20},{5,21},{6,22},{7,23},{8,24},{9,... | collective-permute-start | bytes 786440 | tf_op jit(solution)/shard_map/ppermute | solution.py:353
  3.8 1.2 %copy-done = bf16[1,4,256,512]{3,2,1,0:T(8,128)(2,1)S(1)} copy-done((bf16[1,4,256,512]{3,2,1,0:T(8,128)(2,1)S(1)}, bf16[1,4,256,512]{3,2,1,0:T(8,128)(2,1)}, u32[]{:S(2)}) %copy-start) | copy-done | bytes 1048600
  5.1 0.6 %shard_map.59 = (bf16[256,512]{1,0:T(8,128)(2,1)S(1)}, bf16[256,512]{1,0:T(8,128)(2,1)S(1)}, bf16[256,512]{1,0:T(8,128)(2,1)S(1)}) custom-call(s32[3]{0:T(128)S(1)} %pad_add_fusion.1.index_ref, bf16[4,256,512]{2,1,0:T(8,128)(2,1)S(1)} %bitcast.30), custom_call_target="tpu_custom_call" | custom-call | bytes 1835020 | tf_op jit(solution)/shard_map/pallas_call | solution.py:321
  5.7 1.0 %collective-permute-start.1 = (bf16[256,512]{1,0:T(8,128)(2,1)S(1)}, bf16[256,512]{1,0:T(8,128)(2,1)S(1)}, u32[]{:S(2)}, u32[]{:S(2)}) collective-permute-start(bf16[256,512]{1,0:T(8,128)(2,1)S(1)} %get-tuple-element.21), channel_id=1, source_target_pairs={{0,1},{1,0},{2,3},{3,2},{4,5},{5,4},{6,7},{7,6},{8,9},{9,8},{10,11... | collective-permute-start | bytes 786440 | tf_op jit(solution)/shard_map/ppermute | solution.py:353
  6.8 0.6 %reduce_sum.27 = f32[]{:T(128)} reduce(f32[8]{0:T(128)S(1)} %copy-done.1, f32[]{:T(128)} %constant.69.clone.1), dimensions={0}, to_apply=%region_0.1 | reduce | flops 7 | bytes 40 | tf_op jit(solution)/shard_map/reduce_sum | solution.py:30
  7.4 0.7 %divide_bitcast_fusion = (f32[1,8]{1,0:T(1,128)S(1)}, f32[8]{0:T(128)S(1)}) fusion(f32[8]{0:T(128)S(1)} %copy-done.1, f32[]{:T(128)} %reduce_sum.27, f32[8]{0:T(128)S(1)} %fusion.2), kind=kLoop, calls=%fused_computation.20 | loop fusion | flops 32 | bytes 132 | tf_op jit(solution)/shard_map/broadcast_in_dim | solution.py:481
  8.1 0.2 select_reduce_fusion
  8.3 0.6 %dynamic_slice.8 = s32[1]{0:T(128)} dynamic-slice(s32[4]{0:T(128)S(1)} %copy-done.2, s32[]{:T(128)S(6)} %select_n.60), dynamic_slice_sizes={1} | dynamic-slice | bytes 12 | tf_op jit(solution)/shard_map/jit(dynamic_index_in_dim)/dynamic_slice | solution.py:393
  8.9 0.7 %multiply_subtract_fusion.lim_ref = s32[2]{0:T(128)S(1)} fusion(s32[]{:T(128)} %select_n.55, s32[]{:T(128)S(6)} %mul.26, s32[]{:T(128)} %bitcast.1), kind=kLoop, calls=%fused_computation.21 | loop fusion | flops 8 | bytes 20 | tf_op jit(solution)/shard_map/sub | solution.py:393
  9.6 0.6 %gather_fusion = f32[2]{0:T(128)S(1)} fusion(f32[2]{0:T(128)S(1)} %select_reduce_fusion, s32[1024]{0:T(1024)S(1)} %pad_clamp_fusion), kind=kCustom, calls=%fused_computation | custom fusion | bytes 24 | tf_op jit(solution)/shard_map/jit(_take)/gather | solution.py:391
  10.3 1.0 %shard_map.60 = (f32[256,512]{1,0:T(8,128)S(1)}, f32[512,512]{1,0:T(8,128)S(1)}, f32[8,128]{1,0:T(8,128)S(1)}) custom-call(f32[2]{0:T(128)S(1)} %and_select_fusion.mix_ref, s32[2]{0:T(128)S(1)} %multiply_subtract_fusion.lim_ref, s32[3]{0:T(128)S(1)} %pad_add_fusion.pos_ref, bf16[256,512]{1,0:T(8,128)(2,1)S(1)} %get-tuple-element.19.refs_0_, ...), custom_call_target="tpu_custom_call" | custom-call | flops 134217728 | bytes 2101276 | tf_op jit(solution)/shard_map/pallas_call | solution.py:321
  11.2 4.7 %collective-permute-done.2.refs_1_ = bf16[256,512]{1,0:T(8,128)(2,1)S(1)} collective-permute-done((bf16[256,512]{1,0:T(8,128)(2,1)S(1)}, bf16[256,512]{1,0:T(8,128)(2,1)S(1)}, u32[]{:S(2)}, u32[]{:S(2)}) %collective-permute-start.2) | collective-permute-done | bytes 262176 | tf_op jit(solution)/shard_map/ppermute | solution.py:353
  15.9 1.0 %shard_map.61 = (f32[256,512]{1,0:T(8,128)S(1)}, f32[4,272,128]{2,1,0:T(8,128)S(1)}) custom-call(f32[2]{0:T(128)S(1)} %and_select_fusion.mix_ref, s32[2]{0:T(128)S(1)} %multiply_subtract_fusion.lim_ref, s32[3]{0:T(128)S(1)} %pad_add_fusion.pos_ref, bf16[256,512]{1,0:T(8,128)(2,1)S(1)} %collective-permute-done.1.refs_0_, ...), custom_call_target="tpu_custom_call" | custom-call | flops 134217728 | bytes 2658332 | tf_op jit(solution)/shard_map/pallas_call | solution.py:321
  17.1 1.6 %collective-permute-start.3 = (f16[272,128]{1,0:T(8,128)(2,1)S(1)}, f16[272,128]{1,0:T(8,128)(2,1)S(1)}, u32[]{:S(2)}, u32[]{:S(2)}) collective-permute-start(f16[272,128]{1,0:T(8,128)(2,1)S(1)} %get-tuple-element.40), channel_id=1, source_target_pairs={{0,2},{1,3},{2,0},{3,1},{4,6},{5,7},{6,4},{7,5},{8,10},{9,11},{10,... | collective-permute-start | bytes 208904 | tf_op jit(solution)/shard_map/ppermute | solution.py:353
  18.6 1.3 %collective-permute-start.4 = (f16[272,128]{1,0:T(8,128)(2,1)S(1)}, f16[272,128]{1,0:T(8,128)(2,1)S(1)}, u32[]{:S(2)}, u32[]{:S(2)}) collective-permute-start(f16[272,128]{1,0:T(8,128)(2,1)S(1)} %get-tuple-element.39), channel_id=1, source_target_pairs={{0,4},{1,5},{2,6},{3,7},{4,0},{5,1},{6,2},{7,3},{8,12},{9,13},{10,... | collective-permute-start | bytes 208904 | tf_op jit(solution)/shard_map/ppermute | solution.py:353
  19.9 1.3 %collective-permute-start.6 = (f32[8,128]{1,0:T(8,128)S(1)}, f32[8,128]{1,0:T(8,128)S(1)}, u32[]{:S(2)}, u32[]{:S(2)}) collective-permute-start(f32[8,128]{1,0:T(8,128)S(1)} %slice_bitcast_fusion.4.refs_4_), channel_id=1, source_target_pairs={{0,16},{1,17},{2,18},{3,19},{4,20},{5,21},{6,22},{7,23},{8,24},{9,... | collective-permute-start | bytes 12296 | tf_op jit(solution)/shard_map/ppermute | solution.py:353
  21.3 1.1 %collective-permute-done.4 = f16[272,128]{1,0:T(8,128)(2,1)S(1)} collective-permute-done((f16[272,128]{1,0:T(8,128)(2,1)S(1)}, f16[272,128]{1,0:T(8,128)(2,1)S(1)}, u32[]{:S(2)}, u32[]{:S(2)}) %collective-permute-start.4) | collective-permute-done | bytes 69664 | tf_op jit(solution)/shard_map/ppermute | solution.py:353
  22.4 1.9 %collective-permute-done.5 = f16[272,128]{1,0:T(8,128)(2,1)S(1)} collective-permute-done((f16[272,128]{1,0:T(8,128)(2,1)S(1)}, f16[272,128]{1,0:T(8,128)(2,1)S(1)}, u32[]{:S(2)}, u32[]{:S(2)}) %collective-permute-start.5) | collective-permute-done | bytes 69664 | tf_op jit(solution)/shard_map/ppermute | solution.py:353
  24.3 0.1 shard_map.62
  24.5 2.4 %collective-permute-start.7 = (f16[272,128]{1,0:T(8,128)(2,1)S(1)}, f16[272,128]{1,0:T(8,128)(2,1)S(1)}, u32[]{:S(2)}, u32[]{:S(2)}) collective-permute-start(f16[272,128]{1,0:T(8,128)(2,1)S(1)} %convert_element_type.54), channel_id=1, source_target_pairs={{0,8},{1,9},{2,10},{3,11},{4,12},{5,13},{6,14},{7,15},{8,0},{9,1},... | collective-permute-start | bytes 208904 | tf_op jit(solution)/shard_map/ppermute | solution.py:353
  26.9 2.5 %collective-permute-done.7 = f16[272,128]{1,0:T(8,128)(2,1)S(1)} collective-permute-done((f16[272,128]{1,0:T(8,128)(2,1)S(1)}, f16[272,128]{1,0:T(8,128)(2,1)S(1)}, u32[]{:S(2)}, u32[]{:S(2)}) %collective-permute-start.7) | collective-permute-done | bytes 69664 | tf_op jit(solution)/shard_map/ppermute | solution.py:353
  29.4 0.1 shard_map.63
  29.6 1.4 %collective-permute-start.9 = (f16[272,128]{1,0:T(8,128)(2,1)S(1)}, f16[272,128]{1,0:T(8,128)(2,1)S(1)}, u32[]{:S(2)}, u32[]{:S(2)}) collective-permute-start(f16[272,128]{1,0:T(8,128)(2,1)S(1)} %convert_element_type.56), channel_id=1, source_target_pairs={{0,4},{1,5},{2,6},{3,7},{4,0},{5,1},{6,2},{7,3},{8,12},{9,13},{10,... | collective-permute-start | bytes 208904 | tf_op jit(solution)/shard_map/ppermute | solution.py:353
  31.0 1.2 %collective-permute-start.10 = (f16[272,128]{1,0:T(8,128)(2,1)S(1)}, f16[272,128]{1,0:T(8,128)(2,1)S(1)}, u32[]{:S(2)}, u32[]{:S(2)}) collective-permute-start(f16[272,128]{1,0:T(8,128)(2,1)S(1)} %convert_element_type.56), channel_id=1, source_target_pairs={{0,6},{1,7},{2,4},{3,5},{4,2},{5,3},{6,0},{7,1},{8,14},{9,15},{10,... | collective-permute-start | bytes 208904 | tf_op jit(solution)/shard_map/ppermute | solution.py:353
  32.2 0.5 %collective-permute-done.8 = f16[272,128]{1,0:T(8,128)(2,1)S(1)} collective-permute-done((f16[272,128]{1,0:T(8,128)(2,1)S(1)}, f16[272,128]{1,0:T(8,128)(2,1)S(1)}, u32[]{:S(2)}, u32[]{:S(2)}) %collective-permute-start.8) | collective-permute-done | bytes 69664 | tf_op jit(solution)/shard_map/ppermute | solution.py:353
  32.8 2.3 %collective-permute-done.10 = f16[272,128]{1,0:T(8,128)(2,1)S(1)} collective-permute-done((f16[272,128]{1,0:T(8,128)(2,1)S(1)}, f16[272,128]{1,0:T(8,128)(2,1)S(1)}, u32[]{:S(2)}, u32[]{:S(2)}) %collective-permute-start.10) | collective-permute-done | bytes 69664 | tf_op jit(solution)/shard_map/ppermute | solution.py:353
  35.1 3.9 %shard_map.64 = (bf16[256,512]{1,0:T(8,128)(2,1)S(1)}, bf16[3,512,512]{2,1,0:T(8,128)(2,1)S(1)}, f32[8,128]{1,0:T(8,128)S(1)}) custom-call(s32[3]{0:T(128)S(1)} %pad_add_fusion.pos_ref, f32[272,128]{1,0:T(8,128)S(1)} %get-tuple-element.28.own_ref, f32[272,128]{1,0:T(8,128)S(1)} %convert_element_type.57.refs_0_, f32[272,128]{1,0:T(8,128)S(1)} %convert_element_type.58.refs_1_, ...), custom_call_target="tpu_custom_call" | custom-call | flops 2415919104 | bytes 2920460 | tf_op jit(solution)/shard_map/pallas_call | solution.py:321
  39.0 3.7 %collective-permute-start.11 = (f32[8,128]{1,0:T(8,128)S(1)}, f32[8,128]{1,0:T(8,128)S(1)}, u32[]{:S(2)}, u32[]{:S(2)}) collective-permute-start(f32[8,128]{1,0:T(8,128)S(1)} %shard_map.65.refs_0_), channel_id=1, source_target_pairs={{0,1},{1,0},{2,3},{3,2},{4,5},{5,4},{6,7},{7,6},{8,9},{9,8},{10,11... | collective-permute-start | bytes 12296 | tf_op jit(solution)/shard_map/ppermute | solution.py:353
  42.9 0.7 %collective-permute-done.11.refs_1_ = f32[8,128]{1,0:T(8,128)S(1)} collective-permute-done((f32[8,128]{1,0:T(8,128)S(1)}, f32[8,128]{1,0:T(8,128)S(1)}, u32[]{:S(2)}, u32[]{:S(2)}) %collective-permute-start.11) | collective-permute-done | bytes 4128 | tf_op jit(solution)/shard_map/ppermute | solution.py:353
  43.6 1.1 %shard_map.66 = (bf16[256,512]{1,0:T(8,128)(2,1)S(1)}, f32[1,8]{1,0:T(1,128)}) custom-call(f32[256,512]{1,0:T(8,128)S(1)} %get-tuple-element.20.comb_ref, f32[8,128]{1,0:T(8,128)S(1)} %get-tuple-element.31.inv_ref, bf16[3,512,512]{2,1,0:T(8,128)(2,1)S(1)} %get-tuple-element.32.poly_ref, f32[8,128]{1,0:T(8,128)S(1)} %shard_map.65.refs_0_, ...), custom_call_target="tpu_custom_call" | custom-call | flops 402653184 | bytes 2371744 | tf_op jit(solution)/shard_map/pallas_call | solution.py:321
  44.7 1.1 %convert_multiply_fusion = f32[2,256,512]{2,1,0:T(8,128)} fusion(bf16[1,256,512]{2,1,0:T(8,128)(2,1)S(1)} %get-tuple-element.37, bf16[1,256,512]{2,1,0:T(8,128)(2,1)S(1)} %get-tuple-element.36), kind=kLoop, calls=%fused_computation.1 | loop fusion | flops 786432 | bytes 1572864 | tf_op jit(solution)/shard_map/mul | solution.py:500
  (39 shorter events, 0.8 us)
Async XLA Ops:
  0.6 6.1 %copy-start.3 = (s32[2]{0:T(128)S(1)}, s32[2]{0:T(128)}, u32[]{:S(2)}) copy-start(s32[2]{0:T(128)} %param.6) | copy-start | bytes 28
  0.6 6.2 %copy-start.1 = (f32[8]{0:T(128)S(1)}, f32[8]{0:T(128)}, u32[]{:S(2)}) copy-start(f32[8]{0:T(128)} %param.7) | copy-start | bytes 100
  0.7 7.6 %copy-start.2 = (s32[4]{0:T(128)S(1)}, s32[4]{0:T(128)}, u32[]{:S(2)}) copy-start(s32[4]{0:T(128)} %param.5) | copy-start | bytes 52
  1.7 8.6 %collective-permute-start = (bf16[256,512]{1,0:T(8,128)(2,1)S(1)}, bf16[256,512]{1,0:T(8,128)(2,1)S(1)}, u32[]{:S(2)}, u32[]{:S(2)}) collective-permute-start(bf16[256,512]{1,0:T(8,128)(2,1)S(1)} %dynamic-slice_bitcast_fusion), channel_id=1, source_target_pairs={{0,16},{1,17},{2,18},{3,19},{4,20},{5,21},{6,22},{7,23},{8,24},{9,... | collective-permute-start | bytes 786440 | tf_op jit(solution)/shard_map/ppermute | solution.py:353
  3.8 1.2 %copy-start = (bf16[1,4,256,512]{3,2,1,0:T(8,128)(2,1)S(1)}, bf16[1,4,256,512]{3,2,1,0:T(8,128)(2,1)}, u32[]{:S(2)}) copy-start(bf16[1,4,256,512]{3,2,1,0:T(8,128)(2,1)} %param.4) | copy-start | bytes 3145732
  5.7 5.5 %collective-permute-start.1 = (bf16[256,512]{1,0:T(8,128)(2,1)S(1)}, bf16[256,512]{1,0:T(8,128)(2,1)S(1)}, u32[]{:S(2)}, u32[]{:S(2)}) collective-permute-start(bf16[256,512]{1,0:T(8,128)(2,1)S(1)} %get-tuple-element.21), channel_id=1, source_target_pairs={{0,1},{1,0},{2,3},{3,2},{4,5},{5,4},{6,7},{7,6},{8,9},{9,8},{10,11... | collective-permute-start | bytes 786440 | tf_op jit(solution)/shard_map/ppermute | solution.py:353
  6.7 9.2 %collective-permute-start.2 = (bf16[256,512]{1,0:T(8,128)(2,1)S(1)}, bf16[256,512]{1,0:T(8,128)(2,1)S(1)}, u32[]{:S(2)}, u32[]{:S(2)}) collective-permute-start(bf16[256,512]{1,0:T(8,128)(2,1)S(1)} %get-tuple-element.22), channel_id=1, source_target_pairs={{0,17},{1,16},{2,19},{3,18},{4,21},{5,20},{6,23},{7,22},{8,25},{9,... | collective-permute-start | bytes 786440 | tf_op jit(solution)/shard_map/ppermute | solution.py:353
  17.1 4.2 %collective-permute-start.3 = (f16[272,128]{1,0:T(8,128)(2,1)S(1)}, f16[272,128]{1,0:T(8,128)(2,1)S(1)}, u32[]{:S(2)}, u32[]{:S(2)}) collective-permute-start(f16[272,128]{1,0:T(8,128)(2,1)S(1)} %get-tuple-element.40), channel_id=1, source_target_pairs={{0,2},{1,3},{2,0},{3,1},{4,6},{5,7},{6,4},{7,5},{8,10},{9,11},{10,... | collective-permute-start | bytes 208904 | tf_op jit(solution)/shard_map/ppermute | solution.py:353
  18.6 3.8 %collective-permute-start.4 = (f16[272,128]{1,0:T(8,128)(2,1)S(1)}, f16[272,128]{1,0:T(8,128)(2,1)S(1)}, u32[]{:S(2)}, u32[]{:S(2)}) collective-permute-start(f16[272,128]{1,0:T(8,128)(2,1)S(1)} %get-tuple-element.39), channel_id=1, source_target_pairs={{0,4},{1,5},{2,6},{3,7},{4,0},{5,1},{6,2},{7,3},{8,12},{9,13},{10,... | collective-permute-start | bytes 208904 | tf_op jit(solution)/shard_map/ppermute | solution.py:353
  19.9 4.4 %collective-permute-start.5 = (f16[272,128]{1,0:T(8,128)(2,1)S(1)}, f16[272,128]{1,0:T(8,128)(2,1)S(1)}, u32[]{:S(2)}, u32[]{:S(2)}) collective-permute-start(f16[272,128]{1,0:T(8,128)(2,1)S(1)} %get-tuple-element.38), channel_id=1, source_target_pairs={{0,6},{1,7},{2,4},{3,5},{4,2},{5,3},{6,0},{7,1},{8,14},{9,15},{10,... | collective-permute-start | bytes 208904 | tf_op jit(solution)/shard_map/ppermute | solution.py:353
  19.9 4.4 %collective-permute-start.6 = (f32[8,128]{1,0:T(8,128)S(1)}, f32[8,128]{1,0:T(8,128)S(1)}, u32[]{:S(2)}, u32[]{:S(2)}) collective-permute-start(f32[8,128]{1,0:T(8,128)S(1)} %slice_bitcast_fusion.4.refs_4_), channel_id=1, source_target_pairs={{0,16},{1,17},{2,18},{3,19},{4,20},{5,21},{6,22},{7,23},{8,24},{9,... | collective-permute-start | bytes 12296 | tf_op jit(solution)/shard_map/ppermute | solution.py:353
  24.5 4.9 %collective-permute-start.7 = (f16[272,128]{1,0:T(8,128)(2,1)S(1)}, f16[272,128]{1,0:T(8,128)(2,1)S(1)}, u32[]{:S(2)}, u32[]{:S(2)}) collective-permute-start(f16[272,128]{1,0:T(8,128)(2,1)S(1)} %convert_element_type.54), channel_id=1, source_target_pairs={{0,8},{1,9},{2,10},{3,11},{4,12},{5,13},{6,14},{7,15},{8,0},{9,1},... | collective-permute-start | bytes 208904 | tf_op jit(solution)/shard_map/ppermute | solution.py:353
  29.5 3.2 %collective-permute-start.8 = (f16[272,128]{1,0:T(8,128)(2,1)S(1)}, f16[272,128]{1,0:T(8,128)(2,1)S(1)}, u32[]{:S(2)}, u32[]{:S(2)}) collective-permute-start(f16[272,128]{1,0:T(8,128)(2,1)S(1)} %convert_element_type.56), channel_id=1, source_target_pairs={{0,2},{1,3},{2,0},{3,1},{4,6},{5,7},{6,4},{7,5},{8,10},{9,11},{10,... | collective-permute-start | bytes 208904 | tf_op jit(solution)/shard_map/ppermute | solution.py:353
  29.6 3.2 %collective-permute-start.9 = (f16[272,128]{1,0:T(8,128)(2,1)S(1)}, f16[272,128]{1,0:T(8,128)(2,1)S(1)}, u32[]{:S(2)}, u32[]{:S(2)}) collective-permute-start(f16[272,128]{1,0:T(8,128)(2,1)S(1)} %convert_element_type.56), channel_id=1, source_target_pairs={{0,4},{1,5},{2,6},{3,7},{4,0},{5,1},{6,2},{7,3},{8,12},{9,13},{10,... | collective-permute-start | bytes 208904 | tf_op jit(solution)/shard_map/ppermute | solution.py:353
  31.0 4.1 %collective-permute-start.10 = (f16[272,128]{1,0:T(8,128)(2,1)S(1)}, f16[272,128]{1,0:T(8,128)(2,1)S(1)}, u32[]{:S(2)}, u32[]{:S(2)}) collective-permute-start(f16[272,128]{1,0:T(8,128)(2,1)S(1)} %convert_element_type.56), channel_id=1, source_target_pairs={{0,6},{1,7},{2,4},{3,5},{4,2},{5,3},{6,0},{7,1},{8,14},{9,15},{10,... | collective-permute-start | bytes 208904 | tf_op jit(solution)/shard_map/ppermute | solution.py:353
  39.0 4.5 %collective-permute-start.11 = (f32[8,128]{1,0:T(8,128)S(1)}, f32[8,128]{1,0:T(8,128)S(1)}, u32[]{:S(2)}, u32[]{:S(2)}) collective-permute-start(f32[8,128]{1,0:T(8,128)S(1)} %shard_map.65.refs_0_), channel_id=1, source_target_pairs={{0,1},{1,0},{2,3},{3,2},{4,5},{5,4},{6,7},{7,6},{8,9},{9,8},{10,11... | collective-permute-start | bytes 12296 | tf_op jit(solution)/shard_map/ppermute | solution.py:353
  42.7 1.9 %collective-permute-start.12 = (bf16[256,512]{1,0:T(8,128)(2,1)S(1)}, bf16[256,512]{1,0:T(8,128)(2,1)S(1)}, u32[]{:S(2)}, u32[]{:S(2)}) collective-permute-start(bf16[256,512]{1,0:T(8,128)(2,1)S(1)} %get-tuple-element.34), channel_id=1, source_target_pairs={{0,1},{1,0},{2,3},{3,2},{4,5},{5,4},{6,7},{7,6},{8,9},{9,8},{10,11... | collective-permute-start | bytes 786440 | tf_op jit(solution)/shard_map/ppermute | solution.py:353

commit v9 on v8

--- a/solution.py
+++ b/solution.py
@@ -264,15 +264,11 @@
         half = COEF_A * gram + dot(near, poly)
         high = half.astype(jnp.bfloat16)
         rest = (half - high.astype(F32)).astype(jnp.bfloat16)
-        gram_ref[top, :] = (
-            COEF_A * half[:half_width]
-            + dot(poly[:half_width], high)
-            + dot(poly[:half_width], rest)
-        )
-        gram_ref[low, low] = (
-            COEF_A * half[half_width:, half_width:]
-            + dot(poly[half_width:], high[:, half_width:])
-            + dot(poly[half_width:], rest[:, half_width:])
+        twice = jnp.concatenate([poly, poly], axis=1)
+        both = jnp.concatenate([high, rest], axis=0)
+        gram_ref[top, :] = COEF_A * half[:half_width] + dot(twice[:half_width], both)
+        gram_ref[low, low] = COEF_A * half[half_width:, half_width:] + dot(
+            twice[half_width:], both[:, half_width:]
         )
         gram_ref[low, top] = gram_ref[top, low].T
         gram = gram_ref[...]

time: 46.4 us -> 46.4 us (level)
  no operation moved by 1% of the time
where the time goes in v9:
time: 46.4 us; the launch traced here: 45.8 us
  starting transfers between devices  16.2 us (35%)
  waiting for transfers between devices  13.7 us (30%)
  Pallas kernels  7.86 us (17%)
  other arithmetic  3.71 us (8%)
  local copies, waits for them, and re-layouts  3.49 us (8%)
  between operations  0.91 us (2%)
    ppermute x13, starting transfers between devices, exchange(): lax.ppermute(value, AXES, [(i, i ^ mask) for i in range(domains * shards)])  16.2 us
    ppermute x13, waiting for transfers between devices, exchange(): lax.ppermute(value, AXES, [(i, i ^ mask) for i in range(domains * shards)])  13.7 us
    pallas_call x8, Pallas kernels, call(): pl.pallas_call(kernel, out_shape=tuple(out_shape), in_specs=[pl.BlockSpec...  7.86 us
    unnamed x8, local copies, waits for them, and re-layouts  1.24 us
    mul x1, other arithmetic, body(): jnp.stack(ordered).astype(F32) * (MUON_SCALE * math.sqrt(full_rows))  1.11 us
    squeeze x1, local copies, waits for them, and re-layouts, body(): lax.dynamic_index_in_dim(gradients[0], member ^ order[0], 0, keepdims=False)  0.97 us
  transfers between devices with their start and end apart: 13, of which 8 were waited for; matrix products, arithmetic and copies ran while one was open for 8% of the time, Pallas kernels for 6%

profile of v9, /device:TPU:1, one launch (start us, length us, event | category | flops | bytes accessed | tf_op | source)
XLA Modules:
  0.0 45.8 jit_solution(9196863441434341450)
XLA Ops:
  0.7 1.0 %dynamic-slice_bitcast_fusion = bf16[256,512]{1,0:T(8,128)(2,1)S(1)} fusion(bf16[1,4,256,512]{3,2,1,0:T(8,128)(2,1)} %param.4, s32[]{:T(128)S(6)} %select_n.63), kind=kLoop, calls=%fused_computation.4 | loop fusion | bytes 524292 | tf_op jit(solution)/shard_map/jit(dynamic_index_in_dim)/squeeze | solution.py:366
  1.7 2.1 %collective-permute-start = (bf16[256,512]{1,0:T(8,128)(2,1)S(1)}, bf16[256,512]{1,0:T(8,128)(2,1)S(1)}, u32[]{:S(2)}, u32[]{:S(2)}) collective-permute-start(bf16[256,512]{1,0:T(8,128)(2,1)S(1)} %dynamic-slice_bitcast_fusion), channel_id=1, source_target_pairs={{0,16},{1,17},{2,18},{3,19},{4,20},{5,21},{6,22},{7,23},{8,24},{9,... | collective-permute-start | bytes 786440 | tf_op jit(solution)/shard_map/ppermute | solution.py:349
  3.8 1.2 %copy-done = bf16[1,4,256,512]{3,2,1,0:T(8,128)(2,1)S(1)} copy-done((bf16[1,4,256,512]{3,2,1,0:T(8,128)(2,1)S(1)}, bf16[1,4,256,512]{3,2,1,0:T(8,128)(2,1)}, u32[]{:S(2)}) %copy-start) | copy-done | bytes 1048600
  5.1 0.6 %shard_map.59 = (bf16[256,512]{1,0:T(8,128)(2,1)S(1)}, bf16[256,512]{1,0:T(8,128)(2,1)S(1)}, bf16[256,512]{1,0:T(8,128)(2,1)S(1)}) custom-call(s32[3]{0:T(128)S(1)} %pad_add_fusion.1.index_ref, bf16[4,256,512]{2,1,0:T(8,128)(2,1)S(1)} %bitcast.30), custom_call_target="tpu_custom_call" | custom-call | bytes 1835020 | tf_op jit(solution)/shard_map/pallas_call | solution.py:317
  5.7 1.0 %collective-permute-start.1 = (bf16[256,512]{1,0:T(8,128)(2,1)S(1)}, bf16[256,512]{1,0:T(8,128)(2,1)S(1)}, u32[]{:S(2)}, u32[]{:S(2)}) collective-permute-start(bf16[256,512]{1,0:T(8,128)(2,1)S(1)} %get-tuple-element.21), channel_id=1, source_target_pairs={{0,1},{1,0},{2,3},{3,2},{4,5},{5,4},{6,7},{7,6},{8,9},{9,8},{10,11... | collective-permute-start | bytes 786440 | tf_op jit(solution)/shard_map/ppermute | solution.py:349
  6.8 0.6 %reduce_sum.27 = f32[]{:T(128)} reduce(f32[8]{0:T(128)S(1)} %copy-done.1, f32[]{:T(128)} %constant.69.clone.1), dimensions={0}, to_apply=%region_0.1 | reduce | flops 7 | bytes 40 | tf_op jit(solution)/shard_map/reduce_sum | solution.py:30
  7.4 0.7 %divide_bitcast_fusion = (f32[1,8]{1,0:T(1,128)S(1)}, f32[8]{0:T(128)S(1)}) fusion(f32[8]{0:T(128)S(1)} %copy-done.1, f32[]{:T(128)} %reduce_sum.27, f32[8]{0:T(128)S(1)} %fusion.2), kind=kLoop, calls=%fused_computation.20 | loop fusion | flops 32 | bytes 132 | tf_op jit(solution)/shard_map/broadcast_in_dim | solution.py:477
  8.1 0.2 select_reduce_fusion
  8.3 0.6 %dynamic_slice.8 = s32[1]{0:T(128)} dynamic-slice(s32[4]{0:T(128)S(1)} %copy-done.2, s32[]{:T(128)S(6)} %select_n.60), dynamic_slice_sizes={1} | dynamic-slice | bytes 12 | tf_op jit(solution)/shard_map/jit(dynamic_index_in_dim)/dynamic_slice | solution.py:389
  8.9 0.7 %multiply_subtract_fusion.lim_ref = s32[2]{0:T(128)S(1)} fusion(s32[]{:T(128)} %select_n.55, s32[]{:T(128)S(6)} %mul.26, s32[]{:T(128)} %bitcast.1), kind=kLoop, calls=%fused_computation.21 | loop fusion | flops 8 | bytes 20 | tf_op jit(solution)/shard_map/sub | solution.py:389
  9.6 0.6 %gather_fusion = f32[2]{0:T(128)S(1)} fusion(f32[2]{0:T(128)S(1)} %select_reduce_fusion, s32[1024]{0:T(1024)S(1)} %pad_clamp_fusion), kind=kCustom, calls=%fused_computation | custom fusion | bytes 24 | tf_op jit(solution)/shard_map/jit(_take)/gather | solution.py:387
  10.3 1.0 %shard_map.60 = (f32[256,512]{1,0:T(8,128)S(1)}, f32[512,512]{1,0:T(8,128)S(1)}, f32[8,128]{1,0:T(8,128)S(1)}) custom-call(f32[2]{0:T(128)S(1)} %and_select_fusion.mix_ref, s32[2]{0:T(128)S(1)} %multiply_subtract_fusion.lim_ref, s32[3]{0:T(128)S(1)} %pad_add_fusion.pos_ref, bf16[256,512]{1,0:T(8,128)(2,1)S(1)} %get-tuple-element.19.refs_0_, ...), custom_call_target="tpu_custom_call" | custom-call | flops 134217728 | bytes 2101276 | tf_op jit(solution)/shard_map/pallas_call | solution.py:317
  11.2 4.7 %collective-permute-done.2.refs_1_ = bf16[256,512]{1,0:T(8,128)(2,1)S(1)} collective-permute-done((bf16[256,512]{1,0:T(8,128)(2,1)S(1)}, bf16[256,512]{1,0:T(8,128)(2,1)S(1)}, u32[]{:S(2)}, u32[]{:S(2)}) %collective-permute-start.2) | collective-permute-done | bytes 262176 | tf_op jit(solution)/shard_map/ppermute | solution.py:349
  15.9 1.0 %shard_map.61 = (f32[256,512]{1,0:T(8,128)S(1)}, f32[4,272,128]{2,1,0:T(8,128)S(1)}) custom-call(f32[2]{0:T(128)S(1)} %and_select_fusion.mix_ref, s32[2]{0:T(128)S(1)} %multiply_subtract_fusion.lim_ref, s32[3]{0:T(128)S(1)} %pad_add_fusion.pos_ref, bf16[256,512]{1,0:T(8,128)(2,1)S(1)} %collective-permute-done.1.refs_0_, ...), custom_call_target="tpu_custom_call" | custom-call | flops 134217728 | bytes 2658332 | tf_op jit(solution)/shard_map/pallas_call | solution.py:317
  17.1 1.6 %collective-permute-start.3 = (f16[272,128]{1,0:T(8,128)(2,1)S(1)}, f16[272,128]{1,0:T(8,128)(2,1)S(1)}, u32[]{:S(2)}, u32[]{:S(2)}) collective-permute-start(f16[272,128]{1,0:T(8,128)(2,1)S(1)} %get-tuple-element.40), channel_id=1, source_target_pairs={{0,2},{1,3},{2,0},{3,1},{4,6},{5,7},{6,4},{7,5},{8,10},{9,11},{10,... | collective-permute-start | bytes 208904 | tf_op jit(solution)/shard_map/ppermute | solution.py:349
  18.6 1.3 %collective-permute-start.4 = (f16[272,128]{1,0:T(8,128)(2,1)S(1)}, f16[272,128]{1,0:T(8,128)(2,1)S(1)}, u32[]{:S(2)}, u32[]{:S(2)}) collective-permute-start(f16[272,128]{1,0:T(8,128)(2,1)S(1)} %get-tuple-element.39), channel_id=1, source_target_pairs={{0,4},{1,5},{2,6},{3,7},{4,0},{5,1},{6,2},{7,3},{8,12},{9,13},{10,... | collective-permute-start | bytes 208904 | tf_op jit(solution)/shard_map/ppermute | solution.py:349
  19.9 1.3 %collective-permute-start.6 = (f32[8,128]{1,0:T(8,128)S(1)}, f32[8,128]{1,0:T(8,128)S(1)}, u32[]{:S(2)}, u32[]{:S(2)}) collective-permute-start(f32[8,128]{1,0:T(8,128)S(1)} %slice_bitcast_fusion.4.refs_4_), channel_id=1, source_target_pairs={{0,16},{1,17},{2,18},{3,19},{4,20},{5,21},{6,22},{7,23},{8,24},{9,... | collective-permute-start | bytes 12296 | tf_op jit(solution)/shard_map/ppermute | solution.py:349
  21.3 1.1 %collective-permute-done.4 = f16[272,128]{1,0:T(8,128)(2,1)S(1)} collective-permute-done((f16[272,128]{1,0:T(8,128)(2,1)S(1)}, f16[272,128]{1,0:T(8,128)(2,1)S(1)}, u32[]{:S(2)}, u32[]{:S(2)}) %collective-permute-start.4) | collective-permute-done | bytes 69664 | tf_op jit(solution)/shard_map/ppermute | solution.py:349
  22.4 1.9 %collective-permute-done.5 = f16[272,128]{1,0:T(8,128)(2,1)S(1)} collective-permute-done((f16[272,128]{1,0:T(8,128)(2,1)S(1)}, f16[272,128]{1,0:T(8,128)(2,1)S(1)}, u32[]{:S(2)}, u32[]{:S(2)}) %collective-permute-start.5) | collective-permute-done | bytes 69664 | tf_op jit(solution)/shard_map/ppermute | solution.py:349
  24.3 0.1 shard_map.62
  24.5 2.4 %collective-permute-start.7 = (f16[272,128]{1,0:T(8,128)(2,1)S(1)}, f16[272,128]{1,0:T(8,128)(2,1)S(1)}, u32[]{:S(2)}, u32[]{:S(2)}) collective-permute-start(f16[272,128]{1,0:T(8,128)(2,1)S(1)} %convert_element_type.54), channel_id=1, source_target_pairs={{0,8},{1,9},{2,10},{3,11},{4,12},{5,13},{6,14},{7,15},{8,0},{9,1},... | collective-permute-start | bytes 208904 | tf_op jit(solution)/shard_map/ppermute | solution.py:349
  26.9 2.5 %collective-permute-done.7 = f16[272,128]{1,0:T(8,128)(2,1)S(1)} collective-permute-done((f16[272,128]{1,0:T(8,128)(2,1)S(1)}, f16[272,128]{1,0:T(8,128)(2,1)S(1)}, u32[]{:S(2)}, u32[]{:S(2)}) %collective-permute-start.7) | collective-permute-done | bytes 69664 | tf_op jit(solution)/shard_map/ppermute | solution.py:349
  29.4 0.1 shard_map.63
  29.6 1.4 %collective-permute-start.9 = (f16[272,128]{1,0:T(8,128)(2,1)S(1)}, f16[272,128]{1,0:T(8,128)(2,1)S(1)}, u32[]{:S(2)}, u32[]{:S(2)}) collective-permute-start(f16[272,128]{1,0:T(8,128)(2,1)S(1)} %convert_element_type.56), channel_id=1, source_target_pairs={{0,4},{1,5},{2,6},{3,7},{4,0},{5,1},{6,2},{7,3},{8,12},{9,13},{10,... | collective-permute-start | bytes 208904 | tf_op jit(solution)/shard_map/ppermute | solution.py:349
  31.0 1.2 %collective-permute-start.10 = (f16[272,128]{1,0:T(8,128)(2,1)S(1)}, f16[272,128]{1,0:T(8,128)(2,1)S(1)}, u32[]{:S(2)}, u32[]{:S(2)}) collective-permute-start(f16[272,128]{1,0:T(8,128)(2,1)S(1)} %convert_element_type.56), channel_id=1, source_target_pairs={{0,6},{1,7},{2,4},{3,5},{4,2},{5,3},{6,0},{7,1},{8,14},{9,15},{10,... | collective-permute-start | bytes 208904 | tf_op jit(solution)/shard_map/ppermute | solution.py:349
  32.2 0.5 %collective-permute-done.8 = f16[272,128]{1,0:T(8,128)(2,1)S(1)} collective-permute-done((f16[272,128]{1,0:T(8,128)(2,1)S(1)}, f16[272,128]{1,0:T(8,128)(2,1)S(1)}, u32[]{:S(2)}, u32[]{:S(2)}) %collective-permute-start.8) | collective-permute-done | bytes 69664 | tf_op jit(solution)/shard_map/ppermute | solution.py:349
  32.8 2.3 %collective-permute-done.10 = f16[272,128]{1,0:T(8,128)(2,1)S(1)} collective-permute-done((f16[272,128]{1,0:T(8,128)(2,1)S(1)}, f16[272,128]{1,0:T(8,128)(2,1)S(1)}, u32[]{:S(2)}, u32[]{:S(2)}) %collective-permute-start.10) | collective-permute-done | bytes 69664 | tf_op jit(solution)/shard_map/ppermute | solution.py:349
  35.1 3.9 %shard_map.64 = (bf16[256,512]{1,0:T(8,128)(2,1)S(1)}, bf16[3,512,512]{2,1,0:T(8,128)(2,1)S(1)}, f32[8,128]{1,0:T(8,128)S(1)}) custom-call(s32[3]{0:T(128)S(1)} %pad_add_fusion.pos_ref, f32[272,128]{1,0:T(8,128)S(1)} %get-tuple-element.28.own_ref, f32[272,128]{1,0:T(8,128)S(1)} %convert_element_type.57.refs_0_, f32[272,128]{1,0:T(8,128)S(1)} %convert_element_type.58.refs_1_, ...), custom_call_target="tpu_custom_call" | custom-call | flops 2415919104 | bytes 2920460 | tf_op jit(solution)/shard_map/pallas_call | solution.py:317
  39.0 3.7 %collective-permute-start.11 = (f32[8,128]{1,0:T(8,128)S(1)}, f32[8,128]{1,0:T(8,128)S(1)}, u32[]{:S(2)}, u32[]{:S(2)}) collective-permute-start(f32[8,128]{1,0:T(8,128)S(1)} %shard_map.65.refs_0_), channel_id=1, source_target_pairs={{0,1},{1,0},{2,3},{3,2},{4,5},{5,4},{6,7},{7,6},{8,9},{9,8},{10,11... | collective-permute-start | bytes 12296 | tf_op jit(solution)/shard_map/ppermute | solution.py:349
  42.9 0.7 %collective-permute-done.11.refs_1_ = f32[8,128]{1,0:T(8,128)S(1)} collective-permute-done((f32[8,128]{1,0:T(8,128)S(1)}, f32[8,128]{1,0:T(8,128)S(1)}, u32[]{:S(2)}, u32[]{:S(2)}) %collective-permute-start.11) | collective-permute-done | bytes 4128 | tf_op jit(solution)/shard_map/ppermute | solution.py:349
  43.6 1.1 %shard_map.66 = (bf16[256,512]{1,0:T(8,128)(2,1)S(1)}, f32[1,8]{1,0:T(1,128)}) custom-call(f32[256,512]{1,0:T(8,128)S(1)} %get-tuple-element.20.comb_ref, f32[8,128]{1,0:T(8,128)S(1)} %get-tuple-element.31.inv_ref, bf16[3,512,512]{2,1,0:T(8,128)(2,1)S(1)} %get-tuple-element.32.poly_ref, f32[8,128]{1,0:T(8,128)S(1)} %shard_map.65.refs_0_, ...), custom_call_target="tpu_custom_call" | custom-call | flops 402653184 | bytes 2371744 | tf_op jit(solution)/shard_map/pallas_call | solution.py:317
  44.7 1.1 %convert_multiply_fusion = f32[2,256,512]{2,1,0:T(8,128)} fusion(bf16[1,256,512]{2,1,0:T(8,128)(2,1)S(1)} %get-tuple-element.37, bf16[1,256,512]{2,1,0:T(8,128)(2,1)S(1)} %get-tuple-element.36), kind=kLoop, calls=%fused_computation.1 | loop fusion | flops 786432 | bytes 1572864 | tf_op jit(solution)/shard_map/mul | solution.py:496
  (39 shorter events, 0.8 us)
Async XLA Ops:
  0.6 6.1 %copy-start.3 = (s32[2]{0:T(128)S(1)}, s32[2]{0:T(128)}, u32[]{:S(2)}) copy-start(s32[2]{0:T(128)} %param.6) | copy-start | bytes 28
  0.6 6.2 %copy-start.1 = (f32[8]{0:T(128)S(1)}, f32[8]{0:T(128)}, u32[]{:S(2)}) copy-start(f32[8]{0:T(128)} %param.7) | copy-start | bytes 100
  0.7 7.6 %copy-start.2 = (s32[4]{0:T(128)S(1)}, s32[4]{0:T(128)}, u32[]{:S(2)}) copy-start(s32[4]{0:T(128)} %param.5) | copy-start | bytes 52
  1.7 8.6 %collective-permute-start = (bf16[256,512]{1,0:T(8,128)(2,1)S(1)}, bf16[256,512]{1,0:T(8,128)(2,1)S(1)}, u32[]{:S(2)}, u32[]{:S(2)}) collective-permute-start(bf16[256,512]{1,0:T(8,128)(2,1)S(1)} %dynamic-slice_bitcast_fusion), channel_id=1, source_target_pairs={{0,16},{1,17},{2,18},{3,19},{4,20},{5,21},{6,22},{7,23},{8,24},{9,... | collective-permute-start | bytes 786440 | tf_op jit(solution)/shard_map/ppermute | solution.py:349
  3.8 1.2 %copy-start = (bf16[1,4,256,512]{3,2,1,0:T(8,128)(2,1)S(1)}, bf16[1,4,256,512]{3,2,1,0:T(8,128)(2,1)}, u32[]{:S(2)}) copy-start(bf16[1,4,256,512]{3,2,1,0:T(8,128)(2,1)} %param.4) | copy-start | bytes 3145732
  5.7 5.5 %collective-permute-start.1 = (bf16[256,512]{1,0:T(8,128)(2,1)S(1)}, bf16[256,512]{1,0:T(8,128)(2,1)S(1)}, u32[]{:S(2)}, u32[]{:S(2)}) collective-permute-start(bf16[256,512]{1,0:T(8,128)(2,1)S(1)} %get-tuple-element.21), channel_id=1, source_target_pairs={{0,1},{1,0},{2,3},{3,2},{4,5},{5,4},{6,7},{7,6},{8,9},{9,8},{10,11... | collective-permute-start | bytes 786440 | tf_op jit(solution)/shard_map/ppermute | solution.py:349
  6.7 9.2 %collective-permute-start.2 = (bf16[256,512]{1,0:T(8,128)(2,1)S(1)}, bf16[256,512]{1,0:T(8,128)(2,1)S(1)}, u32[]{:S(2)}, u32[]{:S(2)}) collective-permute-start(bf16[256,512]{1,0:T(8,128)(2,1)S(1)} %get-tuple-element.22), channel_id=1, source_target_pairs={{0,17},{1,16},{2,19},{3,18},{4,21},{5,20},{6,23},{7,22},{8,25},{9,... | collective-permute-start | bytes 786440 | tf_op jit(solution)/shard_map/ppermute | solution.py:349
  17.1 4.2 %collective-permute-start.3 = (f16[272,128]{1,0:T(8,128)(2,1)S(1)}, f16[272,128]{1,0:T(8,128)(2,1)S(1)}, u32[]{:S(2)}, u32[]{:S(2)}) collective-permute-start(f16[272,128]{1,0:T(8,128)(2,1)S(1)} %get-tuple-element.40), channel_id=1, source_target_pairs={{0,2},{1,3},{2,0},{3,1},{4,6},{5,7},{6,4},{7,5},{8,10},{9,11},{10,... | collective-permute-start | bytes 208904 | tf_op jit(solution)/shard_map/ppermute | solution.py:349
  18.6 3.8 %collective-permute-start.4 = (f16[272,128]{1,0:T(8,128)(2,1)S(1)}, f16[272,128]{1,0:T(8,128)(2,1)S(1)}, u32[]{:S(2)}, u32[]{:S(2)}) collective-permute-start(f16[272,128]{1,0:T(8,128)(2,1)S(1)} %get-tuple-element.39), channel_id=1, source_target_pairs={{0,4},{1,5},{2,6},{3,7},{4,0},{5,1},{6,2},{7,3},{8,12},{9,13},{10,... | collective-permute-start | bytes 208904 | tf_op jit(solution)/shard_map/ppermute | solution.py:349
  19.9 4.4 %collective-permute-start.5 = (f16[272,128]{1,0:T(8,128)(2,1)S(1)}, f16[272,128]{1,0:T(8,128)(2,1)S(1)}, u32[]{:S(2)}, u32[]{:S(2)}) collective-permute-start(f16[272,128]{1,0:T(8,128)(2,1)S(1)} %get-tuple-element.38), channel_id=1, source_target_pairs={{0,6},{1,7},{2,4},{3,5},{4,2},{5,3},{6,0},{7,1},{8,14},{9,15},{10,... | collective-permute-start | bytes 208904 | tf_op jit(solution)/shard_map/ppermute | solution.py:349
  19.9 4.4 %collective-permute-start.6 = (f32[8,128]{1,0:T(8,128)S(1)}, f32[8,128]{1,0:T(8,128)S(1)}, u32[]{:S(2)}, u32[]{:S(2)}) collective-permute-start(f32[8,128]{1,0:T(8,128)S(1)} %slice_bitcast_fusion.4.refs_4_), channel_id=1, source_target_pairs={{0,16},{1,17},{2,18},{3,19},{4,20},{5,21},{6,22},{7,23},{8,24},{9,... | collective-permute-start | bytes 12296 | tf_op jit(solution)/shard_map/ppermute | solution.py:349
  24.5 4.9 %collective-permute-start.7 = (f16[272,128]{1,0:T(8,128)(2,1)S(1)}, f16[272,128]{1,0:T(8,128)(2,1)S(1)}, u32[]{:S(2)}, u32[]{:S(2)}) collective-permute-start(f16[272,128]{1,0:T(8,128)(2,1)S(1)} %convert_element_type.54), channel_id=1, source_target_pairs={{0,8},{1,9},{2,10},{3,11},{4,12},{5,13},{6,14},{7,15},{8,0},{9,1},... | collective-permute-start | bytes 208904 | tf_op jit(solution)/shard_map/ppermute | solution.py:349
  29.5 3.2 %collective-permute-start.8 = (f16[272,128]{1,0:T(8,128)(2,1)S(1)}, f16[272,128]{1,0:T(8,128)(2,1)S(1)}, u32[]{:S(2)}, u32[]{:S(2)}) collective-permute-start(f16[272,128]{1,0:T(8,128)(2,1)S(1)} %convert_element_type.56), channel_id=1, source_target_pairs={{0,2},{1,3},{2,0},{3,1},{4,6},{5,7},{6,4},{7,5},{8,10},{9,11},{10,... | collective-permute-start | bytes 208904 | tf_op jit(solution)/shard_map/ppermute | solution.py:349
  29.6 3.2 %collective-permute-start.9 = (f16[272,128]{1,0:T(8,128)(2,1)S(1)}, f16[272,128]{1,0:T(8,128)(2,1)S(1)}, u32[]{:S(2)}, u32[]{:S(2)}) collective-permute-start(f16[272,128]{1,0:T(8,128)(2,1)S(1)} %convert_element_type.56), channel_id=1, source_target_pairs={{0,4},{1,5},{2,6},{3,7},{4,0},{5,1},{6,2},{7,3},{8,12},{9,13},{10,... | collective-permute-start | bytes 208904 | tf_op jit(solution)/shard_map/ppermute | solution.py:349
  31.0 4.1 %collective-permute-start.10 = (f16[272,128]{1,0:T(8,128)(2,1)S(1)}, f16[272,128]{1,0:T(8,128)(2,1)S(1)}, u32[]{:S(2)}, u32[]{:S(2)}) collective-permute-start(f16[272,128]{1,0:T(8,128)(2,1)S(1)} %convert_element_type.56), channel_id=1, source_target_pairs={{0,6},{1,7},{2,4},{3,5},{4,2},{5,3},{6,0},{7,1},{8,14},{9,15},{10,... | collective-permute-start | bytes 208904 | tf_op jit(solution)/shard_map/ppermute | solution.py:349
  39.0 4.5 %collective-permute-start.11 = (f32[8,128]{1,0:T(8,128)S(1)}, f32[8,128]{1,0:T(8,128)S(1)}, u32[]{:S(2)}, u32[]{:S(2)}) collective-permute-start(f32[8,128]{1,0:T(8,128)S(1)} %shard_map.65.refs_0_), channel_id=1, source_target_pairs={{0,1},{1,0},{2,3},{3,2},{4,5},{5,4},{6,7},{7,6},{8,9},{9,8},{10,11... | collective-permute-start | bytes 12296 | tf_op jit(solution)/shard_map/ppermute | solution.py:349
  42.7 1.9 %collective-permute-start.12 = (bf16[256,512]{1,0:T(8,128)(2,1)S(1)}, bf16[256,512]{1,0:T(8,128)(2,1)S(1)}, u32[]{:S(2)}, u32[]{:S(2)}) collective-permute-start(bf16[256,512]{1,0:T(8,128)(2,1)S(1)} %get-tuple-element.34), channel_id=1, source_target_pairs={{0,1},{1,0},{2,3},{3,2},{4,5},{5,4},{6,7},{7,6},{8,9},{9,8},{10,11... | collective-permute-start | bytes 786440 | tf_op jit(solution)/shard_map/ppermute | solution.py:349

commit v10 on v9

--- a/solution.py
+++ b/solution.py
@@ -89,8 +89,9 @@
         copy.wait()
 
 
-def gram_kernel(domains, stage, last, mix_ref, lim_ref, pos_ref, *refs):
+def gram_kernel(domains, others, stage, last, mix_ref, lim_ref, pos_ref, *refs):
     blocks, refs = refs[:domains], refs[domains:]
+    ahead, refs = (refs[:others], refs[others:]) if stage == 0 else ((), refs)
     if stage:
         sofar_ref, scal_ref, refs = refs[0], refs[1], refs[2:]
     comb_ref, refs = refs[0], refs[1:]
@@ -120,8 +121,13 @@
     scal = jnp.where(lane == 2 * domains, frob, 0.0)
     for kd in range(domains):
         group = domain_pos ^ kd
+        scal = jnp.where(lane == group, total(values[kd] * combined), scal)
+        if kd == 0 and stage:
+            continue
         square = jnp.where(keep, total(values[kd] * values[kd]), 0.0)
-        scal = jnp.where(lane == group, total(values[kd] * combined), scal)
+        for n, ref in enumerate(ahead if kd == 0 else (), 1):
+            value = ref[...].astype(F32)
+            square = square + jnp.where(lim_ref[n] > 0, total(value * value), 0.0)
         scal = jnp.where(lane == domains + group, square, scal)
     if stage:
         frob = frob + lane_pick(scal_ref[0:1, :], 2 * domains)
@@ -399,16 +405,17 @@
     combs, carried = [], []
     for kl in range(lanes):
         last = kl == lanes - 1
+        ahead = blocks[1:lanes] if kl == 0 else []
         results = [jax.ShapeDtypeStruct((rows, columns), F32)]
         if last:
             results += [jax.ShapeDtypeStruct((SQUARE, packed, BLOCK), F32)]
         else:
             results += [square, jax.ShapeDtypeStruct((8, BLOCK), F32)]
         comb, *carried = call(
-            functools.partial(gram_kernel, domains, kl, last),
+            functools.partial(gram_kernel, domains, lanes - 1, kl, last),
             results,
-            [mix, limits, position, *blocks[kl::lanes], *carried],
-            [smem] * 3 + [vmem] * (domains + len(carried)),
+            [mix, limits, position, *blocks[kl::lanes], *ahead, *carried],
+            [smem] * 3 + [vmem] * (domains + len(ahead) + len(carried)),
             flops=2 * rows * columns * columns,
         )
         combs.append(comb)

time: 46.4 us -> 46.4 us (level)
  no operation moved by 1% of the time
where the time goes in v10:
time: 46.4 us; the launch traced here: 45.8 us
  starting transfers between devices  16.2 us (35%)
  waiting for transfers between devices  13.7 us (30%)
  Pallas kernels  7.85 us (17%)
  other arithmetic  3.71 us (8%)
  local copies, waits for them, and re-layouts  3.49 us (8%)
  between operations  0.91 us (2%)
    ppermute x13, starting transfers between devices, exchange(): lax.ppermute(value, AXES, [(i, i ^ mask) for i in range(domains * shards)])  16.2 us
    ppermute x13, waiting for transfers between devices, exchange(): lax.ppermute(value, AXES, [(i, i ^ mask) for i in range(domains * shards)])  13.7 us
    pallas_call x8, Pallas kernels, call(): pl.pallas_call(kernel, out_shape=tuple(out_shape), in_specs=[pl.BlockSpec...  7.85 us
    unnamed x8, local copies, waits for them, and re-layouts  1.24 us
    mul x1, other arithmetic, body(): jnp.stack(ordered).astype(F32) * (MUON_SCALE * math.sqrt(full_rows))  1.11 us
    squeeze x1, local copies, waits for them, and re-layouts, body(): lax.dynamic_index_in_dim(gradients[0], member ^ order[0], 0, keepdims=False)  0.97 us
  transfers between devices with their start and end apart: 13, of which 8 were waited for; matrix products, arithmetic and copies ran while one was open for 8% of the time, Pallas kernels for 6%

profile of v10, /device:TPU:1, one launch (start us, length us, event | category | flops | bytes accessed | tf_op | source)
XLA Modules:
  0.0 45.8 jit_solution(6633780744932752342)
XLA Ops:
  0.7 1.0 %dynamic-slice_bitcast_fusion = bf16[256,512]{1,0:T(8,128)(2,1)S(1)} fusion(bf16[1,4,256,512]{3,2,1,0:T(8,128)(2,1)} %param.4, s32[]{:T(128)S(6)} %select_n.63), kind=kLoop, calls=%fused_computation.4 | loop fusion | bytes 524292 | tf_op jit(solution)/shard_map/jit(dynamic_index_in_dim)/squeeze | solution.py:372
  1.7 2.1 %collective-permute-start = (bf16[256,512]{1,0:T(8,128)(2,1)S(1)}, bf16[256,512]{1,0:T(8,128)(2,1)S(1)}, u32[]{:S(2)}, u32[]{:S(2)}) collective-permute-start(bf16[256,512]{1,0:T(8,128)(2,1)S(1)} %dynamic-slice_bitcast_fusion), channel_id=1, source_target_pairs={{0,16},{1,17},{2,18},{3,19},{4,20},{5,21},{6,22},{7,23},{8,24},{9,... | collective-permute-start | bytes 786440 | tf_op jit(solution)/shard_map/ppermute | solution.py:355
  3.8 1.2 %copy-done = bf16[1,4,256,512]{3,2,1,0:T(8,128)(2,1)S(1)} copy-done((bf16[1,4,256,512]{3,2,1,0:T(8,128)(2,1)S(1)}, bf16[1,4,256,512]{3,2,1,0:T(8,128)(2,1)}, u32[]{:S(2)}) %copy-start) | copy-done | bytes 1048600
  5.1 0.6 %shard_map.59 = (bf16[256,512]{1,0:T(8,128)(2,1)S(1)}, bf16[256,512]{1,0:T(8,128)(2,1)S(1)}, bf16[256,512]{1,0:T(8,128)(2,1)S(1)}) custom-call(s32[3]{0:T(128)S(1)} %pad_add_fusion.1.index_ref, bf16[4,256,512]{2,1,0:T(8,128)(2,1)S(1)} %bitcast.30), custom_call_target="tpu_custom_call" | custom-call | bytes 1835020 | tf_op jit(solution)/shard_map/pallas_call | solution.py:323
  5.7 1.0 %collective-permute-start.1 = (bf16[256,512]{1,0:T(8,128)(2,1)S(1)}, bf16[256,512]{1,0:T(8,128)(2,1)S(1)}, u32[]{:S(2)}, u32[]{:S(2)}) collective-permute-start(bf16[256,512]{1,0:T(8,128)(2,1)S(1)} %get-tuple-element.20), channel_id=1, source_target_pairs={{0,1},{1,0},{2,3},{3,2},{4,5},{5,4},{6,7},{7,6},{8,9},{9,8},{10,11... | collective-permute-start | bytes 786440 | tf_op jit(solution)/shard_map/ppermute | solution.py:355
  6.8 0.6 %reduce_sum.27 = f32[]{:T(128)} reduce(f32[8]{0:T(128)S(1)} %copy-done.1, f32[]{:T(128)} %constant.69.clone.1), dimensions={0}, to_apply=%region_0.1 | reduce | flops 7 | bytes 40 | tf_op jit(solution)/shard_map/reduce_sum | solution.py:30
  7.4 0.7 %divide_bitcast_fusion = (f32[1,8]{1,0:T(1,128)S(1)}, f32[8]{0:T(128)S(1)}) fusion(f32[8]{0:T(128)S(1)} %copy-done.1, f32[]{:T(128)} %reduce_sum.27, f32[8]{0:T(128)S(1)} %fusion.2), kind=kLoop, calls=%fused_computation.20 | loop fusion | flops 32 | bytes 132 | tf_op jit(solution)/shard_map/broadcast_in_dim | solution.py:484
  8.1 0.2 select_reduce_fusion
  8.3 0.6 %dynamic_slice.8 = s32[1]{0:T(128)} dynamic-slice(s32[4]{0:T(128)S(1)} %copy-done.2, s32[]{:T(128)S(6)} %select_n.60), dynamic_slice_sizes={1} | dynamic-slice | bytes 12 | tf_op jit(solution)/shard_map/jit(dynamic_index_in_dim)/dynamic_slice | solution.py:395
  8.9 0.7 %multiply_subtract_fusion.lim_ref = s32[2]{0:T(128)S(1)} fusion(s32[]{:T(128)} %select_n.55, s32[]{:T(128)S(6)} %mul.26, s32[]{:T(128)} %bitcast.1), kind=kLoop, calls=%fused_computation.21 | loop fusion | flops 8 | bytes 20 | tf_op jit(solution)/shard_map/sub | solution.py:395
  9.6 0.6 %gather_fusion = f32[2]{0:T(128)S(1)} fusion(f32[2]{0:T(128)S(1)} %select_reduce_fusion, s32[1024]{0:T(1024)S(1)} %pad_clamp_fusion), kind=kCustom, calls=%fused_computation | custom fusion | bytes 24 | tf_op jit(solution)/shard_map/jit(_take)/gather | solution.py:393
  10.3 1.0 %shard_map.60 = (f32[256,512]{1,0:T(8,128)S(1)}, f32[512,512]{1,0:T(8,128)S(1)}, f32[8,128]{1,0:T(8,128)S(1)}) custom-call(f32[2]{0:T(128)S(1)} %and_select_fusion.mix_ref, s32[2]{0:T(128)S(1)} %multiply_subtract_fusion.lim_ref, s32[3]{0:T(128)S(1)} %pad_add_fusion.pos_ref, bf16[256,512]{1,0:T(8,128)(2,1)S(1)} %get-tuple-element.19.refs_0_, ...), custom_call_target="tpu_custom_call" | custom-call | flops 134217728 | bytes 2363420 | tf_op jit(solution)/shard_map/pallas_call | solution.py:323
  11.2 4.7 %collective-permute-done.2.refs_1_ = bf16[256,512]{1,0:T(8,128)(2,1)S(1)} collective-permute-done((bf16[256,512]{1,0:T(8,128)(2,1)S(1)}, bf16[256,512]{1,0:T(8,128)(2,1)S(1)}, u32[]{:S(2)}, u32[]{:S(2)}) %collective-permute-start.2) | collective-permute-done | bytes 262176 | tf_op jit(solution)/shard_map/ppermute | solution.py:355
  15.9 1.0 %shard_map.61 = (f32[256,512]{1,0:T(8,128)S(1)}, f32[4,272,128]{2,1,0:T(8,128)S(1)}) custom-call(f32[2]{0:T(128)S(1)} %and_select_fusion.mix_ref, s32[2]{0:T(128)S(1)} %multiply_subtract_fusion.lim_ref, s32[3]{0:T(128)S(1)} %pad_add_fusion.pos_ref, bf16[256,512]{1,0:T(8,128)(2,1)S(1)} %collective-permute-done.1.refs_2_.refs_0_, ...), custom_call_target="tpu_custom_call" | custom-call | flops 134217728 | bytes 2658332 | tf_op jit(solution)/shard_map/pallas_call | solution.py:323
  17.1 1.6 %collective-permute-start.3 = (f16[272,128]{1,0:T(8,128)(2,1)S(1)}, f16[272,128]{1,0:T(8,128)(2,1)S(1)}, u32[]{:S(2)}, u32[]{:S(2)}) collective-permute-start(f16[272,128]{1,0:T(8,128)(2,1)S(1)} %get-tuple-element.40), channel_id=1, source_target_pairs={{0,2},{1,3},{2,0},{3,1},{4,6},{5,7},{6,4},{7,5},{8,10},{9,11},{10,... | collective-permute-start | bytes 208904 | tf_op jit(solution)/shard_map/ppermute | solution.py:355
  18.6 1.3 %collective-permute-start.4 = (f16[272,128]{1,0:T(8,128)(2,1)S(1)}, f16[272,128]{1,0:T(8,128)(2,1)S(1)}, u32[]{:S(2)}, u32[]{:S(2)}) collective-permute-start(f16[272,128]{1,0:T(8,128)(2,1)S(1)} %get-tuple-element.39), channel_id=1, source_target_pairs={{0,4},{1,5},{2,6},{3,7},{4,0},{5,1},{6,2},{7,3},{8,12},{9,13},{10,... | collective-permute-start | bytes 208904 | tf_op jit(solution)/shard_map/ppermute | solution.py:355
  19.9 1.3 %collective-permute-start.6 = (f32[8,128]{1,0:T(8,128)S(1)}, f32[8,128]{1,0:T(8,128)S(1)}, u32[]{:S(2)}, u32[]{:S(2)}) collective-permute-start(f32[8,128]{1,0:T(8,128)S(1)} %slice_bitcast_fusion.4.refs_4_), channel_id=1, source_target_pairs={{0,16},{1,17},{2,18},{3,19},{4,20},{5,21},{6,22},{7,23},{8,24},{9,... | collective-permute-start | bytes 12296 | tf_op jit(solution)/shard_map/ppermute | solution.py:355
  21.3 1.1 %collective-permute-done.4 = f16[272,128]{1,0:T(8,128)(2,1)S(1)} collective-permute-done((f16[272,128]{1,0:T(8,128)(2,1)S(1)}, f16[272,128]{1,0:T(8,128)(2,1)S(1)}, u32[]{:S(2)}, u32[]{:S(2)}) %collective-permute-start.4) | collective-permute-done | bytes 69664 | tf_op jit(solution)/shard_map/ppermute | solution.py:355
  22.4 1.9 %collective-permute-done.5 = f16[272,128]{1,0:T(8,128)(2,1)S(1)} collective-permute-done((f16[272,128]{1,0:T(8,128)(2,1)S(1)}, f16[272,128]{1,0:T(8,128)(2,1)S(1)}, u32[]{:S(2)}, u32[]{:S(2)}) %collective-permute-start.5) | collective-permute-done | bytes 69664 | tf_op jit(solution)/shard_map/ppermute | solution.py:355
  24.3 0.1 shard_map.62
  24.5 2.4 %collective-permute-start.7 = (f16[272,128]{1,0:T(8,128)(2,1)S(1)}, f16[272,128]{1,0:T(8,128)(2,1)S(1)}, u32[]{:S(2)}, u32[]{:S(2)}) collective-permute-start(f16[272,128]{1,0:T(8,128)(2,1)S(1)} %convert_element_type.54), channel_id=1, source_target_pairs={{0,8},{1,9},{2,10},{3,11},{4,12},{5,13},{6,14},{7,15},{8,0},{9,1},... | collective-permute-start | bytes 208904 | tf_op jit(solution)/shard_map/ppermute | solution.py:355
  26.9 2.5 %collective-permute-done.7 = f16[272,128]{1,0:T(8,128)(2,1)S(1)} collective-permute-done((f16[272,128]{1,0:T(8,128)(2,1)S(1)}, f16[272,128]{1,0:T(8,128)(2,1)S(1)}, u32[]{:S(2)}, u32[]{:S(2)}) %collective-permute-start.7) | collective-permute-done | bytes 69664 | tf_op jit(solution)/shard_map/ppermute | solution.py:355
  29.4 0.1 shard_map.63
  29.6 1.4 %collective-permute-start.9 = (f16[272,128]{1,0:T(8,128)(2,1)S(1)}, f16[272,128]{1,0:T(8,128)(2,1)S(1)}, u32[]{:S(2)}, u32[]{:S(2)}) collective-permute-start(f16[272,128]{1,0:T(8,128)(2,1)S(1)} %convert_element_type.56), channel_id=1, source_target_pairs={{0,4},{1,5},{2,6},{3,7},{4,0},{5,1},{6,2},{7,3},{8,12},{9,13},{10,... | collective-permute-start | bytes 208904 | tf_op jit(solution)/shard_map/ppermute | solution.py:355
  31.0 1.2 %collective-permute-start.10 = (f16[272,128]{1,0:T(8,128)(2,1)S(1)}, f16[272,128]{1,0:T(8,128)(2,1)S(1)}, u32[]{:S(2)}, u32[]{:S(2)}) collective-permute-start(f16[272,128]{1,0:T(8,128)(2,1)S(1)} %convert_element_type.56), channel_id=1, source_target_pairs={{0,6},{1,7},{2,4},{3,5},{4,2},{5,3},{6,0},{7,1},{8,14},{9,15},{10,... | collective-permute-start | bytes 208904 | tf_op jit(solution)/shard_map/ppermute | solution.py:355
  32.2 0.5 %collective-permute-done.8 = f16[272,128]{1,0:T(8,128)(2,1)S(1)} collective-permute-done((f16[272,128]{1,0:T(8,128)(2,1)S(1)}, f16[272,128]{1,0:T(8,128)(2,1)S(1)}, u32[]{:S(2)}, u32[]{:S(2)}) %collective-permute-start.8) | collective-permute-done | bytes 69664 | tf_op jit(solution)/shard_map/ppermute | solution.py:355
  32.8 2.3 %collective-permute-done.10 = f16[272,128]{1,0:T(8,128)(2,1)S(1)} collective-permute-done((f16[272,128]{1,0:T(8,128)(2,1)S(1)}, f16[272,128]{1,0:T(8,128)(2,1)S(1)}, u32[]{:S(2)}, u32[]{:S(2)}) %collective-permute-start.10) | collective-permute-done | bytes 69664 | tf_op jit(solution)/shard_map/ppermute | solution.py:355
  35.1 3.9 %shard_map.64 = (bf16[256,512]{1,0:T(8,128)(2,1)S(1)}, bf16[3,512,512]{2,1,0:T(8,128)(2,1)S(1)}, f32[8,128]{1,0:T(8,128)S(1)}) custom-call(s32[3]{0:T(128)S(1)} %pad_add_fusion.pos_ref, f32[272,128]{1,0:T(8,128)S(1)} %get-tuple-element.28.own_ref, f32[272,128]{1,0:T(8,128)S(1)} %convert_element_type.57.refs_0_, f32[272,128]{1,0:T(8,128)S(1)} %convert_element_type.58.refs_1_, ...), custom_call_target="tpu_custom_call" | custom-call | flops 2415919104 | bytes 2920460 | tf_op jit(solution)/shard_map/pallas_call | solution.py:323
  39.0 3.7 %collective-permute-start.11 = (f32[8,128]{1,0:T(8,128)S(1)}, f32[8,128]{1,0:T(8,128)S(1)}, u32[]{:S(2)}, u32[]{:S(2)}) collective-permute-start(f32[8,128]{1,0:T(8,128)S(1)} %shard_map.65.refs_0_), channel_id=1, source_target_pairs={{0,1},{1,0},{2,3},{3,2},{4,5},{5,4},{6,7},{7,6},{8,9},{9,8},{10,11... | collective-permute-start | bytes 12296 | tf_op jit(solution)/shard_map/ppermute | solution.py:355
  42.9 0.7 %collective-permute-done.11.refs_1_ = f32[8,128]{1,0:T(8,128)S(1)} collective-permute-done((f32[8,128]{1,0:T(8,128)S(1)}, f32[8,128]{1,0:T(8,128)S(1)}, u32[]{:S(2)}, u32[]{:S(2)}) %collective-permute-start.11) | collective-permute-done | bytes 4128 | tf_op jit(solution)/shard_map/ppermute | solution.py:355
  43.5 1.1 %shard_map.66 = (bf16[256,512]{1,0:T(8,128)(2,1)S(1)}, f32[1,8]{1,0:T(1,128)}) custom-call(f32[256,512]{1,0:T(8,128)S(1)} %get-tuple-element.21.comb_ref, f32[8,128]{1,0:T(8,128)S(1)} %get-tuple-element.31.inv_ref, bf16[3,512,512]{2,1,0:T(8,128)(2,1)S(1)} %get-tuple-element.32.poly_ref, f32[8,128]{1,0:T(8,128)S(1)} %shard_map.65.refs_0_, ...), custom_call_target="tpu_custom_call" | custom-call | flops 402653184 | bytes 2371744 | tf_op jit(solution)/shard_map/pallas_call | solution.py:323
  44.7 1.1 %convert_multiply_fusion = f32[2,256,512]{2,1,0:T(8,128)} fusion(bf16[1,256,512]{2,1,0:T(8,128)(2,1)S(1)} %get-tuple-element.37, bf16[1,256,512]{2,1,0:T(8,128)(2,1)S(1)} %get-tuple-element.36), kind=kLoop, calls=%fused_computation.1 | loop fusion | flops 786432 | bytes 1572864 | tf_op jit(solution)/shard_map/mul | solution.py:503
  (39 shorter events, 0.8 us)
Async XLA Ops:
  0.6 6.1 %copy-start.3 = (s32[2]{0:T(128)S(1)}, s32[2]{0:T(128)}, u32[]{:S(2)}) copy-start(s32[2]{0:T(128)} %param.6) | copy-start | bytes 28
  0.6 6.2 %copy-start.1 = (f32[8]{0:T(128)S(1)}, f32[8]{0:T(128)}, u32[]{:S(2)}) copy-start(f32[8]{0:T(128)} %param.7) | copy-start | bytes 100
  0.7 7.6 %copy-start.2 = (s32[4]{0:T(128)S(1)}, s32[4]{0:T(128)}, u32[]{:S(2)}) copy-start(s32[4]{0:T(128)} %param.5) | copy-start | bytes 52
  1.7 8.6 %collective-permute-start = (bf16[256,512]{1,0:T(8,128)(2,1)S(1)}, bf16[256,512]{1,0:T(8,128)(2,1)S(1)}, u32[]{:S(2)}, u32[]{:S(2)}) collective-permute-start(bf16[256,512]{1,0:T(8,128)(2,1)S(1)} %dynamic-slice_bitcast_fusion), channel_id=1, source_target_pairs={{0,16},{1,17},{2,18},{3,19},{4,20},{5,21},{6,22},{7,23},{8,24},{9,... | collective-permute-start | bytes 786440 | tf_op jit(solution)/shard_map/ppermute | solution.py:355
  3.8 1.2 %copy-start = (bf16[1,4,256,512]{3,2,1,0:T(8,128)(2,1)S(1)}, bf16[1,4,256,512]{3,2,1,0:T(8,128)(2,1)}, u32[]{:S(2)}) copy-start(bf16[1,4,256,512]{3,2,1,0:T(8,128)(2,1)} %param.4) | copy-start | bytes 3145732
  5.7 4.6 %collective-permute-start.1 = (bf16[256,512]{1,0:T(8,128)(2,1)S(1)}, bf16[256,512]{1,0:T(8,128)(2,1)S(1)}, u32[]{:S(2)}, u32[]{:S(2)}) collective-permute-start(bf16[256,512]{1,0:T(8,128)(2,1)S(1)} %get-tuple-element.20), channel_id=1, source_target_pairs={{0,1},{1,0},{2,3},{3,2},{4,5},{5,4},{6,7},{7,6},{8,9},{9,8},{10,11... | collective-permute-start | bytes 786440 | tf_op jit(solution)/shard_map/ppermute | solution.py:355
  6.7 9.2 %collective-permute-start.2 = (bf16[256,512]{1,0:T(8,128)(2,1)S(1)}, bf16[256,512]{1,0:T(8,128)(2,1)S(1)}, u32[]{:S(2)}, u32[]{:S(2)}) collective-permute-start(bf16[256,512]{1,0:T(8,128)(2,1)S(1)} %get-tuple-element.22), channel_id=1, source_target_pairs={{0,17},{1,16},{2,19},{3,18},{4,21},{5,20},{6,23},{7,22},{8,25},{9,... | collective-permute-start | bytes 786440 | tf_op jit(solution)/shard_map/ppermute | solution.py:355
  17.1 4.2 %collective-permute-start.3 = (f16[272,128]{1,0:T(8,128)(2,1)S(1)}, f16[272,128]{1,0:T(8,128)(2,1)S(1)}, u32[]{:S(2)}, u32[]{:S(2)}) collective-permute-start(f16[272,128]{1,0:T(8,128)(2,1)S(1)} %get-tuple-element.40), channel_id=1, source_target_pairs={{0,2},{1,3},{2,0},{3,1},{4,6},{5,7},{6,4},{7,5},{8,10},{9,11},{10,... | collective-permute-start | bytes 208904 | tf_op jit(solution)/shard_map/ppermute | solution.py:355
  18.6 3.8 %collective-permute-start.4 = (f16[272,128]{1,0:T(8,128)(2,1)S(1)}, f16[272,128]{1,0:T(8,128)(2,1)S(1)}, u32[]{:S(2)}, u32[]{:S(2)}) collective-permute-start(f16[272,128]{1,0:T(8,128)(2,1)S(1)} %get-tuple-element.39), channel_id=1, source_target_pairs={{0,4},{1,5},{2,6},{3,7},{4,0},{5,1},{6,2},{7,3},{8,12},{9,13},{10,... | collective-permute-start | bytes 208904 | tf_op jit(solution)/shard_map/ppermute | solution.py:355
  19.9 4.4 %collective-permute-start.5 = (f16[272,128]{1,0:T(8,128)(2,1)S(1)}, f16[272,128]{1,0:T(8,128)(2,1)S(1)}, u32[]{:S(2)}, u32[]{:S(2)}) collective-permute-start(f16[272,128]{1,0:T(8,128)(2,1)S(1)} %get-tuple-element.38), channel_id=1, source_target_pairs={{0,6},{1,7},{2,4},{3,5},{4,2},{5,3},{6,0},{7,1},{8,14},{9,15},{10,... | collective-permute-start | bytes 208904 | tf_op jit(solution)/shard_map/ppermute | solution.py:355
  19.9 4.4 %collective-permute-start.6 = (f32[8,128]{1,0:T(8,128)S(1)}, f32[8,128]{1,0:T(8,128)S(1)}, u32[]{:S(2)}, u32[]{:S(2)}) collective-permute-start(f32[8,128]{1,0:T(8,128)S(1)} %slice_bitcast_fusion.4.refs_4_), channel_id=1, source_target_pairs={{0,16},{1,17},{2,18},{3,19},{4,20},{5,21},{6,22},{7,23},{8,24},{9,... | collective-permute-start | bytes 12296 | tf_op jit(solution)/shard_map/ppermute | solution.py:355
  24.5 4.9 %collective-permute-start.7 = (f16[272,128]{1,0:T(8,128)(2,1)S(1)}, f16[272,128]{1,0:T(8,128)(2,1)S(1)}, u32[]{:S(2)}, u32[]{:S(2)}) collective-permute-start(f16[272,128]{1,0:T(8,128)(2,1)S(1)} %convert_element_type.54), channel_id=1, source_target_pairs={{0,8},{1,9},{2,10},{3,11},{4,12},{5,13},{6,14},{7,15},{8,0},{9,1},... | collective-permute-start | bytes 208904 | tf_op jit(solution)/shard_map/ppermute | solution.py:355
  29.5 3.2 %collective-permute-start.8 = (f16[272,128]{1,0:T(8,128)(2,1)S(1)}, f16[272,128]{1,0:T(8,128)(2,1)S(1)}, u32[]{:S(2)}, u32[]{:S(2)}) collective-permute-start(f16[272,128]{1,0:T(8,128)(2,1)S(1)} %convert_element_type.56), channel_id=1, source_target_pairs={{0,2},{1,3},{2,0},{3,1},{4,6},{5,7},{6,4},{7,5},{8,10},{9,11},{10,... | collective-permute-start | bytes 208904 | tf_op jit(solution)/shard_map/ppermute | solution.py:355
  29.6 3.2 %collective-permute-start.9 = (f16[272,128]{1,0:T(8,128)(2,1)S(1)}, f16[272,128]{1,0:T(8,128)(2,1)S(1)}, u32[]{:S(2)}, u32[]{:S(2)}) collective-permute-start(f16[272,128]{1,0:T(8,128)(2,1)S(1)} %convert_element_type.56), channel_id=1, source_target_pairs={{0,4},{1,5},{2,6},{3,7},{4,0},{5,1},{6,2},{7,3},{8,12},{9,13},{10,... | collective-permute-start | bytes 208904 | tf_op jit(solution)/shard_map/ppermute | solution.py:355
  31.0 4.1 %collective-permute-start.10 = (f16[272,128]{1,0:T(8,128)(2,1)S(1)}, f16[272,128]{1,0:T(8,128)(2,1)S(1)}, u32[]{:S(2)}, u32[]{:S(2)}) collective-permute-start(f16[272,128]{1,0:T(8,128)(2,1)S(1)} %convert_element_type.56), channel_id=1, source_target_pairs={{0,6},{1,7},{2,4},{3,5},{4,2},{5,3},{6,0},{7,1},{8,14},{9,15},{10,... | collective-permute-start | bytes 208904 | tf_op jit(solution)/shard_map/ppermute | solution.py:355
  39.0 4.5 %collective-permute-start.11 = (f32[8,128]{1,0:T(8,128)S(1)}, f32[8,128]{1,0:T(8,128)S(1)}, u32[]{:S(2)}, u32[]{:S(2)}) collective-permute-start(f32[8,128]{1,0:T(8,128)S(1)} %shard_map.65.refs_0_), channel_id=1, source_target_pairs={{0,1},{1,0},{2,3},{3,2},{4,5},{5,4},{6,7},{7,6},{8,9},{9,8},{10,11... | collective-permute-start | bytes 12296 | tf_op jit(solution)/shard_map/ppermute | solution.py:355
  42.7 1.9 %collective-permute-start.12 = (bf16[256,512]{1,0:T(8,128)(2,1)S(1)}, bf16[256,512]{1,0:T(8,128)(2,1)S(1)}, u32[]{:S(2)}, u32[]{:S(2)}) collective-permute-start(bf16[256,512]{1,0:T(8,128)(2,1)S(1)} %get-tuple-element.34), channel_id=1, source_target_pairs={{0,1},{1,0},{2,3},{3,2},{4,5},{5,4},{6,7},{7,6},{8,9},{9,8},{10,11... | collective-permute-start | bytes 786440 | tf_op jit(solution)/shard_map/ppermute | solution.py:355
